TPU v7x, 256 devices: a whole 4x4x8 slice. The times are simulated.
256 devices in a mesh: seq: 32 (over y, x, core), tensor: 8 (over z).
Axes of the slice: x: 4, y: 4, z: 8, core: 2. Of those that a mesh axis runs over, the one named last changes fastest.
Arguments:
- hidden: bfloat16 [8192, 3072], P('seq'), may hold values from -6 to 6
- attention_norm_gain: bfloat16 [3072], replicated, may hold values from 0.099609375 to 1.8984375
- query_key_value_weight: bfloat16 [3, 3072, 3072], P(None, None, 'tensor'), may hold values from -0.109375 to 0.109375
- output_weight: bfloat16 [3072, 3072], P('tensor'), may hold values from -0.3125 to 0.3125
- adapter_down_weight: bfloat16 [3072, 16], P('tensor'), may hold values from -0.3125 to 0.3125
- adapter_up_weight: bfloat16 [16, 3072], replicated, may hold values from -1.5 to 1.5
- final_norm_gain: bfloat16 [3072], replicated, may hold values from 0.099609375 to 1.8984375
- head: bfloat16 [16384, 3072], P('tensor', 'seq')
- prompt_key_slots: bfloat16 [64, 128, 3072], P('seq', None, 'tensor')
- prompt_value_slots: bfloat16 [64, 128, 3072], P('seq', None, 'tensor'), may hold values from -6 to 6
- counts: int32 [8], replicated, may hold values from 1 to 8, as said below
- page_slot_index: int32 [64], replicated, may hold values from 0 to 63, each once
- owner: int32 [128], replicated, may hold values from 0 to 7, as said below
- targets: int32 [8192], P('seq'), may hold values from 0 to 16383
Outputs:
- logprob_policy: float32 [8192], P('seq')
- logprob_reference: float32 [8192], P('seq')
Inputs may be any that keep to these rules, and one draw needn't show every extreme that they name: `counts`: every prompt fills 1 to 8 pages, and some prompt fills exactly 8. `page_slot_index`: slot s is held by index s // 2 of seq; every slot is named once. `owner`: every prompt owns exactly 16 rollouts, placed anywhere.
All inputs are finite; a program needn't handle non-finite values.
Results may differ from a plain program's by a relative error of at most 0.014.
The roundings to bfloat16 on the way count: a program that leaves them out, or rounds other values in their place, can miss the bound.
Values may be sent and summed in bfloat16 or wider, within the bound.
No kernel may reach another device: no remote copies, remote signals or barrier semaphores. Data moves between devices by JAX's collectives and lax.ppermute only.
A program may use at most 192 MiB of HBM per device.

v0:
```python
import math

import jax
import jax.numpy as jnp
from jax import lax
from jax.experimental import pallas as pl
from jax.experimental.pallas import tpu as pltpu
from jax.sharding import PartitionSpec as P

HEAD_WIDTH = 96
LEN = 64
PAGE = 128
MAXP = 8


EPSILON = 1e-05
NEGATIVE = -1e30
PAD = 128
BLOCK = LEN // 2
VMEM_LIMIT = 28 * 1024 * 1024
F32 = jnp.float32
BF16 = jnp.bfloat16


def rms_norm(values, gain):
    mean_sq = jnp.mean(values * values, axis=-1, keepdims=True)
    return (values * lax.rsqrt(mean_sq + EPSILON) * gain.astype(F32)).astype(BF16)


def project_kernel(hidden_ref, gain_ref, weight_ref, cos_ref, sin_ref, out_ref, normed):
    part = pl.program_id(0)

    @pl.when(part == 0)
    def _():
        normed[...] = rms_norm(hidden_ref[...].astype(F32), gain_ref[...])

    product = jnp.dot(normed[...], weight_ref[0], preferred_element_type=F32)

    @pl.when(part < 2)
    def _():
        width = product.shape[1]
        half = HEAD_WIDTH // 2
        lane = lax.broadcasted_iota(jnp.int32, product.shape, 1) % HEAD_WIDTH
        partner = jnp.where(
            lane < half, -pltpu.roll(product, width - half, 1), pltpu.roll(product, half, 1)
        )
        out_ref[0] = (product * cos_ref[...] + partner * sin_ref[...]).astype(BF16)

    @pl.when(part == 2)
    def _():
        out_ref[0] = product.astype(BF16)


def project(hidden, gain, weight, cosine, sinus):
    rows, width = hidden.shape
    parts, _, cols = weight.shape
    whole = lambda i: (0, 0)
    return pl.pallas_call(
        project_kernel,
        grid=(parts,),
        in_specs=[
            pl.BlockSpec((rows, width), whole),
            pl.BlockSpec((1, width), whole),
            pl.BlockSpec((1, width, cols), lambda i: (i, 0, 0)),
            pl.BlockSpec((rows, cols), whole),
            pl.BlockSpec((rows, cols), whole),
        ],
        out_specs=pl.BlockSpec((1, rows, cols), lambda i: (i, 0, 0)),
        out_shape=jax.ShapeDtypeStruct((parts, rows, cols), BF16),
        scratch_shapes=[pltpu.VMEM((rows, width), BF16)],
        compiler_params=pltpu.CompilerParams(vmem_limit_bytes=VMEM_LIMIT),
        name="project",
    )(hidden, gain, weight, cosine, sinus)


def dot_nt(left, right):
    return lax.dot_general(left, right, (((1,), (1,)), ((), ())), preferred_element_type=F32)


def attend_kernel(*refs):
    first_ref, counts_ref, index_ref, owner_ref = refs[:4]
    qkv_ref = refs[4]
    out_ref, keys, values, sems = refs[-4:]
    pieces = refs[5:-4]
    rollouts = keys.shape[0]
    width = qkv_ref.shape[2]
    heads = width // HEAD_WIDTH
    scale = 1.0 / math.sqrt(HEAD_WIDTH)
    first = first_ref[0]
    my_y, my_x, my_core = first_ref[1], first_ref[2], first_ref[3]

    def start_copies(r, j):
        slot = index_ref[owner_ref[first + r] * MAXP + j]
        device = slot // 2
        down_y = (device // 8 - my_y + 4) % 4
        down_x = (device // 2 % 4 - my_x + 4) % 4
        other = (device % 2 != my_core).astype(jnp.int32)
        rows = pl.ds(pl.multiple_of(j * PAGE, PAGE), PAGE)
        for which, (buffer, far, near) in enumerate(
            ((keys, down_y, down_x), (values, down_x, down_y))
        ):
            at = near * 4 + 2 * (device % 2 != which).astype(jnp.int32) + slot % 2
            high = ((far == 2) & (at >= 8)).astype(jnp.int32)
            piece = far + high + (far == 3).astype(jnp.int32)
            piece = piece + 5 * (my_core != which).astype(jnp.int32)
            at = at - 8 * high
            for p, ref in enumerate(pieces):

                @pl.when(piece == p)
                def _():
                    row = jnp.minimum(at, ref.shape[0] - 1)
                    pltpu.make_async_copy(
                        ref.at[row], buffer.at[r, rows], sems.at[r, which, j]
                    ).start()

        return 0

    def live_pages(r):
        return counts_ref[owner_ref[first + r]]

    def covering(live):
        return jnp.where(live <= 2, 2, jnp.where(live <= 4, 4, MAXP))

    def start_rollout(r, _):
        return lax.fori_loop(0, covering(live_pages(r)), lambda j, _: start_copies(r, j), 0)

    lax.fori_loop(0, rollouts, start_rollout, 0)
    lane_head = lax.broadcasted_iota(jnp.int32, (LEN, width), 1) // HEAD_WIDTH
    own_row = lax.broadcasted_iota(jnp.int32, (heads * LEN, LEN), 0) % LEN
    own_col = lax.broadcasted_iota(jnp.int32, (heads * LEN, LEN), 1)

    def mix_rollout(r, _):
        live = live_pages(r)
        rows = pl.ds(pl.multiple_of(r * LEN, LEN), LEN)

        def mix(pages):
            query = qkv_ref[0, rows, :].astype(F32)
            stacked = jnp.concatenate(
                [jnp.where(lane_head == h, query, 0.0) for h in range(heads)], axis=0
            ).astype(BF16)
            own = dot_nt(stacked, qkv_ref[1, rows, :]) * scale
            own = jnp.where(own_col <= own_row, own, NEGATIVE)
            for j in range(pages):
                for which, buffer in enumerate((keys, values)):
                    pltpu.make_async_copy(
                        pieces[0].at[0],
                        buffer.at[r, pl.ds(j * PAGE, PAGE)],
                        sems.at[r, which, j],
                    ).wait()
            span = pl.ds(0, pages * PAGE)
            cached = dot_nt(stacked, keys[r, span]) * scale
            page_of = lax.broadcasted_iota(jnp.int32, cached.shape, 1) // PAGE
            cached = jnp.where(page_of < live, cached, NEGATIVE)
            largest = jnp.maximum(
                jnp.max(own, axis=1, keepdims=True), jnp.max(cached, axis=1, keepdims=True)
            )
            own = jnp.exp(own - largest)
            cached = jnp.exp(cached - largest)
            total = jnp.sum(own, axis=1, keepdims=True) + jnp.sum(cached, axis=1, keepdims=True)
            mixed = jnp.dot(
                cached.astype(BF16), values[r, span], preferred_element_type=F32
            ) + jnp.dot(own.astype(BF16), qkv_ref[2, rows, :], preferred_element_type=F32)
            mixed = mixed / total
            picked = jnp.zeros((LEN, width), F32)
            for h in range(heads):
                picked = jnp.where(lane_head == h, mixed[h * LEN : (h + 1) * LEN], picked)
            for parity in range(2):
                out_ref[parity, pl.ds(pl.multiple_of(r * BLOCK, BLOCK), BLOCK), :] = picked[
                    parity * BLOCK : (parity + 1) * BLOCK
                ].astype(BF16)

        for pages in (2, 4, MAXP):
            pl.when(covering(live) == pages)(lambda pages=pages: mix(pages))
        return 0

    lax.fori_loop(0, rollouts, mix_rollout, 0)


def attend(first, counts, index, owner, qkv, pieces):
    _, rows, width = qkv.shape
    rollouts = rows // LEN
    vmem = pl.BlockSpec(memory_space=pltpu.VMEM)
    pieces = [pltpu.with_memory_space_constraint(piece, pltpu.HBM) for piece in pieces]
    return pl.pallas_call(
        attend_kernel,
        grid_spec=pltpu.PrefetchScalarGridSpec(
            num_scalar_prefetch=4,
            grid=(),
            in_specs=[vmem] + [pl.BlockSpec(memory_space=pltpu.HBM)] * len(pieces),
            out_specs=vmem,
            scratch_shapes=[
                pltpu.VMEM((rollouts, MAXP * PAGE, width), BF16),
                pltpu.VMEM((rollouts, MAXP * PAGE, width), BF16),
                pltpu.SemaphoreType.DMA((rollouts, 2, MAXP)),
            ],
        ),
        out_shape=jax.ShapeDtypeStruct((2, rows // 2, width), BF16),
        compiler_params=pltpu.CompilerParams(vmem_limit_bytes=VMEM_LIMIT),
        name="attend",
    )(first, counts, index, owner, qkv, *pieces)


def branch_kernel(*refs):
    mine_ref, theirs_ref = refs[:2]
    out_ref = refs[-1]
    chunks = refs[2:-1]
    count = len(chunks) // 2
    start = 0
    for own, partner in zip(chunks[:count], chunks[count:]):
        columns = slice(start, start + own.shape[1])
        out_ref[:, columns] = (
            jnp.dot(mine_ref[...], own[...], preferred_element_type=F32)
            + jnp.dot(theirs_ref[...], partner[...], preferred_element_type=F32)
        ).astype(BF16)
        start += own.shape[1]


def branch_part(mine, theirs, own, partner):
    width = sum(chunk.shape[1] for chunk in own)
    operands = [mine, theirs] + [
        pltpu.with_memory_space_constraint(chunk, pltpu.HBM)
        for chunk in list(own) + list(partner)
    ]
    whole = lambda i: (0, 0)
    out = jax.ShapeDtypeStruct((mine.shape[0], width), BF16)
    return pl.pallas_call(
        branch_kernel,
        grid=(1,),
        in_specs=[pl.BlockSpec(operand.shape, whole) for operand in operands],
        out_specs=pl.BlockSpec(out.shape, whole),
        out_shape=out,
        compiler_params=pltpu.CompilerParams(vmem_limit_bytes=VMEM_LIMIT),
        name="branch",
    )(*operands)


def two_parts(value):
    high = value.astype(BF16)
    return high, (value - high.astype(F32)).astype(BF16)


def score_kernel(*refs):
    place_ref, up_ref, gain_ref, head_ref = refs[:4]
    out_ref, normed, deltas, scales, wanted, largest, total, picked = refs[-8:]
    inputs = refs[4:-8]
    step = pl.program_id(0)
    rank, model = up_ref.shape
    rows = deltas.shape[0]

    @pl.when(step == 0)
    def _():
        start = 0
        gain = gain_ref[...].astype(F32)
        up = up_ref[...]
        for hidden_ref, target_ref, block in zip(inputs[::3], inputs[1::3], inputs[2::3]):
            at = slice(start, start + block.shape[0])
            start += block.shape[0]
            delta = block[:, model : model + rank]
            reference = hidden_ref[...].astype(F32) + block[:, :model].astype(F32)
            policy = reference + jnp.dot(delta, up, preferred_element_type=F32)
            reference_scale = lax.rsqrt(
                jnp.mean(reference * reference, axis=1, keepdims=True) + EPSILON
            )
            policy_scale = lax.rsqrt(jnp.mean(policy * policy, axis=1, keepdims=True) + EPSILON)
            normed[at, :] = (reference * reference_scale * gain).astype(BF16)
            deltas[at, :] = jnp.concatenate([delta, delta], axis=1)
            scales[0, at, :] = policy_scale / reference_scale
            scales[1, at, :] = policy_scale
            wanted[at, :] = target_ref[...]
        high, low = two_parts(up.astype(F32) * gain)
        normed[rows : rows + rank, :] = high
        normed[rows + rank :, :] = low
        largest[...] = jnp.full_like(largest, NEGATIVE)
        total[...] = jnp.zeros_like(total)
        picked[...] = jnp.zeros_like(picked)

    product = jnp.dot(normed[...], head_ref[...], preferred_element_type=F32)
    reference_logits = product[:rows]
    high, low = two_parts(product[rows : rows + rank] + product[rows + rank :])
    adapted = jnp.dot(
        deltas[...], jnp.concatenate([high, low], axis=0), preferred_element_type=F32
    )
    policy_logits = scales[0] * reference_logits + scales[1] * adapted
    columns = lax.broadcasted_iota(jnp.int32, reference_logits.shape, 1)
    tile = head_ref.shape[1]
    hit = columns == wanted[...] - (place_ref[0] * pl.num_programs(0) + step) * tile
    for which, logits in enumerate((policy_logits, reference_logits)):
        picked[which] += jnp.sum(jnp.where(hit, logits, 0.0), axis=1, keepdims=True)
        before = largest[which]
        after = jnp.maximum(before, jnp.max(logits, axis=1, keepdims=True))
        total[which] = total[which] * jnp.exp(before - after) + jnp.sum(
            jnp.exp(logits - after), axis=1, keepdims=True
        )
        largest[which] = after

    @pl.when(step == pl.num_programs(0) - 1)
    def _():
        lane = lax.broadcasted_iota(jnp.int32, (2, rows, 128), 2)
        packed = jnp.where(
            lane == 0, largest[...], jnp.where(lane == 1, total[...], picked[...])
        )
        out_ref[...] = jnp.transpose(packed.reshape(2 * rows, 128))[:8, :]


def score(place, hidden, up, gain, targets, head, blocks):
    model = hidden.shape[1]
    vocab = head.shape[1]
    rank = up.shape[0]
    rows = sum(block.shape[0] for block in blocks)
    tile = 256
    whole = lambda i, p: (0, 0)
    per_block, operands = [], []
    for k, block in enumerate(blocks):
        size = block.shape[0]
        here = lambda i, p, k=k: (p[1 + k], 0)
        per_block += [
            pl.BlockSpec((size, model), here),
            pl.BlockSpec((size, 1), here),
            pl.BlockSpec(block.shape, whole),
        ]
        operands += [hidden, targets, block]
    column = pltpu.VMEM((2, rows, 1), F32)
    return pl.pallas_call(
        score_kernel,
        grid_spec=pltpu.PrefetchScalarGridSpec(
            num_scalar_prefetch=1,
            grid=(vocab // tile,),
            in_specs=[
                pl.BlockSpec(up.shape, whole),
                pl.BlockSpec(gain.shape, whole),
                pl.BlockSpec((model, tile), lambda i, p: (0, i)),
            ]
            + per_block,
            out_specs=pl.BlockSpec((8, 2 * rows), whole),
            scratch_shapes=[
                pltpu.VMEM((rows + 2 * rank, model), BF16),
                pltpu.VMEM((rows, 2 * rank), BF16),
                column,
                pltpu.VMEM((rows, 1), jnp.int32),
                column,
                column,
                column,
            ],
        ),
        out_shape=jax.ShapeDtypeStruct((8, 2 * rows), F32),
        compiler_params=pltpu.CompilerParams(vmem_limit_bytes=VMEM_LIMIT),
        cost_estimate=pl.CostEstimate(
            flops=4 * rows * model * vocab,
            transcendentals=2 * rows * vocab,
            bytes_accessed=2 * model * vocab,
        ),
        name="score",
    )(place, up, gain, head, *operands)


def shifted(value, ranks, step):
    return lax.ppermute(value, "tensor", [(i, (i + step) % ranks) for i in range(ranks)])


def partnered(value, ranks):
    return lax.ppermute(value, "tensor", [(i, i ^ 1) for i in range(ranks)])


def reduce_rows(branch, ranks):
    me = lax.axis_index("tensor")
    size = branch.shape[0] // (ranks // 2)

    def block(step):
        at = (me + step) % ranks // 2 * size
        return lax.dynamic_slice_in_dim(branch, at, size, 0)

    arrived = [shifted(block(step), ranks, step) for step in (ranks // 2, 2, ranks - 2)]
    total = block(0).astype(F32)
    for value in lax.optimization_barrier(arrived):
        total = total + value.astype(F32)
    return total.astype(BF16)


def crossed(value):
    return lax.ppermute(value, "seq", [(i, i ^ 1) for i in range(32)])


def turned(value, stage, step):
    def target(i):
        y, x, core = i // 8, i // 2 % 4, i % 2
        if core == stage:
            x = (x + step) % 4
        else:
            y = (y + step) % 4
        return y * 8 + x * 2 + core

    return lax.ppermute(value, "seq", [(i, target(i)) for i in range(32)])


def gather_pages(keys, values, chunks, ranks):
    first_core = lax.axis_index("seq") % 2 == 0
    kept = jnp.where(first_core, keys, values)
    sent = jnp.where(first_core, values, keys)
    pair = jnp.concatenate([kept, crossed(sent)])
    partner = [partnered(chunks[0], ranks)]
    line = [pair] + [turned(pair, 0, step) for step in (3, 2, 1)]
    line, partner[0] = lax.optimization_barrier((line, partner[0]))
    line = lax.optimization_barrier(jnp.concatenate(line))
    front, behind = turned(line, 1, 3), turned(line, 1, 1)
    near = crossed(line)
    sources = lax.optimization_barrier((chunks[1], line))
    partner.append(partnered(sources[0], ranks))
    front, behind, second = lax.optimization_barrier((front, behind, partner[1]))
    partner[1] = second
    middle = front.shape[0] // 2
    low, high = turned(behind[:middle], 1, 1), turned(front[middle:], 1, 3)
    sources = lax.optimization_barrier((chunks[2], front))
    partner.append(partnered(sources[0], ranks))
    far_front, far_behind = crossed(front), crossed(behind)
    low, high, third = lax.optimization_barrier((low, high, partner[2]))
    partner[2] = third
    sources = lax.optimization_barrier((chunks[3], low))
    partner.append(partnered(sources[0], ranks))
    pieces = [line, front, low, high, behind]
    pieces += [near, far_front, crossed(low), crossed(high), far_behind]
    return pieces, partner, front


def local(
    hidden,
    attention_norm_gain,
    query_key_value_weight,
    output_weight,
    adapter_down_weight,
    adapter_up_weight,
    final_norm_gain,
    head,
    prompt_key_slots,
    prompt_value_slots,
    counts,
    page_slot_index,
    owner,
    targets,
):
    tok_rows, model = hidden.shape
    rollouts_here = tok_rows // LEN
    width_here = output_weight.shape[0]
    heads_here = width_here // HEAD_WIDTH
    ranks = lax.axis_size("tensor")
    first = lax.axis_index("seq") * rollouts_here
    me = lax.axis_index("seq")
    rank = lax.axis_index("tensor")
    down = jnp.pad(adapter_down_weight, ((0, 0), (0, PAD - adapter_down_weight.shape[1])))
    cuts = (0, model // 6, model // 6 * 3, model // 6 * 4, model)
    chunks = [output_weight[:, a:b] for a, b in zip(cuts, cuts[1:])]
    chunks[-1] = jnp.concatenate([chunks[-1], down], axis=1)
    pieces, partner_chunks, stage = gather_pages(
        prompt_key_slots, prompt_value_slots, chunks, ranks
    )
    head_rows, _ = lax.optimization_barrier((head.T, stage))
    head_columns = lax.all_gather(head_rows, "seq", axis=0, tiled=True)

    groups_iota = jnp.arange(counts.shape[0], dtype=jnp.int32)
    my_groups = lax.dynamic_slice_in_dim(owner, first, rollouts_here, 0)
    my_pages = jnp.sum(
        jnp.where(my_groups[:, None] == groups_iota[None, :], counts[None, :], 0), axis=1
    )
    positions = jnp.repeat(my_pages, LEN) * PAGE + jnp.arange(tok_rows, dtype=jnp.int32) % LEN
    half = HEAD_WIDTH // 2
    place_in_head = jnp.arange(width_here, dtype=jnp.int32) % half
    frequency = 10000.0 ** (-place_in_head.astype(F32) * 2.0 / HEAD_WIDTH)
    angles = positions.astype(F32)[:, None] * frequency[None, :]
    qkv = project(
        hidden,
        attention_norm_gain[None, :],
        query_key_value_weight,
        jnp.cos(angles),
        jnp.sin(angles),
    )
    attended = attend(
        jnp.stack([first, me // 8, me // 2 % 4, me % 2]).astype(jnp.int32),
        counts,
        page_slot_index,
        owner,
        qkv,
        pieces,
    )
    branch = branch_part(
        lax.dynamic_index_in_dim(attended, rank % 2, 0, False),
        partnered(lax.dynamic_index_in_dim(attended, 1 - rank % 2, 0, False), ranks),
        chunks,
        partner_chunks,
    )
    mine = reduce_rows(branch, ranks)
    size = tok_rows // ranks
    half = size // 2
    head_columns = pltpu.with_memory_space_constraint(head_columns, pltpu.HBM)

    def score_blocks(places, blocks):
        return score(
            jnp.stack([rank] + places).astype(jnp.int32),
            hidden,
            adapter_up_weight,
            final_norm_gain[None, :],
            targets[:, None],
            head_columns,
            blocks,
        )

    def by_offset(offsets, part):
        part = part.reshape(8, 2, len(offsets), size)
        return {offset: part[:, :, n] for n, offset in enumerate(offsets)}

    def place(offset):
        return (rank + offset) % ranks

    near = [shifted(mine, ranks, step) for step in (-1, 1, -2, 2)]
    near = lax.optimization_barrier(near)
    _, _, after_two, before_two = near
    far = [
        shifted(after_two, ranks, -1),
        shifted(before_two, ranks, 1),
        shifted(after_two[:half], ranks, -2),
        shifted(before_two[half:], ranks, 2),
    ]
    near_offsets = (0, 1, ranks - 1, 2, ranks - 2)
    near_part = score_blocks([place(n) for n in near_offsets], [mine] + near)
    far, near_part = lax.optimization_barrier((far, near_part))
    far_offsets = (3, ranks - 3, ranks // 2)
    opposite = 2 * place(ranks // 2)
    far_part = score_blocks([place(3), place(ranks - 3), opposite, opposite + 1], far)
    stats = by_offset(near_offsets, near_part) | by_offset(far_offsets, far_part)
    line = jnp.stack([stats[k] for k in range(ranks)] * 2, axis=2)
    ordered = lax.dynamic_slice_in_dim(line, ranks - rank, ranks, 2).reshape(8, 2 * tok_rows)
    every = lax.all_to_all(
        jnp.broadcast_to(ordered[None], (ranks, 8, 2 * tok_rows)), "tensor", 0, 0, tiled=True
    )
    maxima, totals, picked = every[:, 0], every[:, 1], every[:, 2]
    largest = jnp.max(maxima, axis=0)
    total = jnp.sum(totals * jnp.exp(maxima - largest[None]), axis=0)
    log_probs = jnp.sum(picked, axis=0) - largest - jnp.log(total)
    return (log_probs[:tok_rows], log_probs[tok_rows:])


def solution(mesh):
    return jax.shard_map(
        local,
        mesh=mesh,
        in_specs=(
            P("seq", None),
            P(),
            P(None, None, "tensor"),
            P("tensor", None),
            P("tensor", None),
            P(),
            P(),
            P("tensor", "seq"),
            P("seq", None, "tensor"),
            P("seq", None, "tensor"),
            P(),
            P(),
            P(),
            P("seq"),
        ),
        out_specs=(P("seq"), P("seq")),
        check_vma=False,
    )
```

profile of v0, /device:TPU:24, one launch (start us, length us, event | category | flops | bytes accessed | tf_op | source)
XLA Modules:
  0.0 201.9 jit_solution(13666979351740233511)
XLA Ops:
  11.7 2.8 %collective-permute-start.1 = (bf16[4,128,384]{2,1,0:T(8,128)(2,1)S(1)}, bf16[4,128,384]{2,1,0:T(8,128)(2,1)S(1)}, u32[]{:S(2)}, u32[]{:S(2)}) collective-permute-start(bf16[4,128,384]{2,1,0:T(8,128)(2,1)S(1)} %pad_maximum_fusion.1), channel_id=1, source_target_pairs={{0,48},{8,200},{16,0},{24,216},{32,16},{40,232},{48,32},{56,248},{... | collective-permute-start | bytes 1179656 | tf_op jit(solution)/shard_map/ppermute | solution.py:392
  16.2 5.2 %collective-permute-done.4.refs_6_ = bf16[384,512]{1,0:T(8,128)(2,1)S(1)} collective-permute-done((bf16[384,512]{1,0:T(8,128)(2,1)S(1)}, bf16[384,512]{1,0:T(8,128)(2,1)S(1)}, u32[]{:S(2)}, u32[]{:S(2)}) %collective-permute-start.4) | collective-permute-done | bytes 393248 | tf_op jit(solution)/shard_map/ppermute | solution.py:361
  21.4 2.7 %collective-permute-done.1 = bf16[4,128,384]{2,1,0:T(8,128)(2,1)S(1)} collective-permute-done((bf16[4,128,384]{2,1,0:T(8,128)(2,1)S(1)}, bf16[4,128,384]{2,1,0:T(8,128)(2,1)S(1)}, u32[]{:S(2)}, u32[]{:S(2)}) %collective-permute-start.1) | collective-permute-done | bytes 393248 | tf_op jit(solution)/shard_map/ppermute | solution.py:392
  24.0 3.9 %collective-permute-done.3 = bf16[4,128,384]{2,1,0:T(8,128)(2,1)S(1)} collective-permute-done((bf16[4,128,384]{2,1,0:T(8,128)(2,1)S(1)}, bf16[4,128,384]{2,1,0:T(8,128)(2,1)S(1)}, u32[]{:S(2)}, u32[]{:S(2)}) %collective-permute-start.3) | collective-permute-done | bytes 393248 | tf_op jit(solution)/shard_map/ppermute | solution.py:392
  29.1 2.5 %collective-permute-start.6 = (bf16[16,128,384]{2,1,0:T(8,128)(2,1)S(1)}, bf16[16,128,384]{2,1,0:T(8,128)(2,1)}, u32[]{:S(2)}, u32[]{:S(2)}) collective-permute-start(bf16[16,128,384]{2,1,0:T(8,128)(2,1)S(1)} %pad_maximum_fusion.refs_5_), channel_id=1, source_target_pairs={{0,64},{8,24},{16,80},{24,40},{32,96},{40,56},{48,112},{56,8},{64,... | collective-permute-start | bytes 4718600 | tf_op jit(solution)/shard_map/ppermute | solution.py:392
  32.7 15.5 %collective-permute-done.7.refs_7_ = bf16[384,1024]{1,0:T(8,128)(2,1)S(1)} collective-permute-done((bf16[384,1024]{1,0:T(8,128)(2,1)S(1)}, bf16[384,1024]{1,0:T(8,128)(2,1)S(1)}, u32[]{:S(2)}, u32[]{:S(2)}) %collective-permute-start.7) | collective-permute-done | bytes 786464 | tf_op jit(solution)/shard_map/ppermute | solution.py:361
  51.4 2.1 %slice.65 = bf16[8,128,384]{2,1,0:T(8,128)(2,1)} slice(bf16[16,128,384]{2,1,0:T(8,128)(2,1)} %collective-permute-done.6.refs_9_), slice={[0:8], [0:128], [0:384]} | slice | bytes 1572864 | tf_op jit(solution)/shard_map/slice | solution.py:411
  53.5 3.3 %collective-permute-start.8 = (bf16[8,128,384]{2,1,0:T(8,128)(2,1)}, bf16[8,128,384]{2,1,0:T(8,128)(2,1)}, u32[]{:S(2)}, u32[]{:S(2)}) collective-permute-start(bf16[8,128,384]{2,1,0:T(8,128)(2,1)} %slice.65), channel_id=1, source_target_pairs={{0,64},{8,24},{16,80},{24,40},{32,96},{40,56},{48,112},{56,8},{64,... | collective-permute-start | bytes 2359304 | tf_op jit(solution)/shard_map/ppermute | solution.py:392
  56.8 4.8 %collective-permute-done.10.refs_8_ = bf16[384,512]{1,0:T(8,128)(2,1)S(1)} collective-permute-done((bf16[384,512]{1,0:T(8,128)(2,1)S(1)}, bf16[384,512]{1,0:T(8,128)(2,1)S(1)}, u32[]{:S(2)}, u32[]{:S(2)}) %collective-permute-start.10) | collective-permute-done | bytes 393248 | tf_op jit(solution)/shard_map/ppermute | solution.py:361
  63.5 2.2 %fusion.1.refs_5_ = bf16[384,1152]{1,0:T(8,128)(2,1)} fusion(bf16[384,16]{1,0:T(8,128)(2,1)S(1)} %copy.39, bf16[384,1024]{1,0:T(8,128)(2,1)} %get-tuple-element.58), kind=kLoop, calls=%fused_computation.3 | loop fusion | flops 2654208 | bytes 1683456 | tf_op jit(solution)/shard_map/concatenate | solution.py:451
  65.6 3.2 %collective-permute-done.8.refs_7_ = bf16[8,128,384]{2,1,0:T(8,128)(2,1)} collective-permute-done((bf16[8,128,384]{2,1,0:T(8,128)(2,1)}, bf16[8,128,384]{2,1,0:T(8,128)(2,1)}, u32[]{:S(2)}, u32[]{:S(2)}) %collective-permute-start.8) | collective-permute-done | bytes 786464 | tf_op jit(solution)/shard_map/ppermute | solution.py:392
  68.9 6.2 %collective-permute-done.9.refs_8_ = bf16[8,128,384]{2,1,0:T(8,128)(2,1)} collective-permute-done((bf16[8,128,384]{2,1,0:T(8,128)(2,1)}, bf16[8,128,384]{2,1,0:T(8,128)(2,1)}, u32[]{:S(2)}, u32[]{:S(2)}) %collective-permute-start.9) | collective-permute-done | bytes 786464 | tf_op jit(solution)/shard_map/ppermute | solution.py:392
  75.8 2.1 %collective-permute-start.17 = (bf16[384,1152]{1,0:T(8,128)(2,1)}, bf16[384,1152]{1,0:T(8,128)(2,1)S(1)}, u32[]{:S(2)}, u32[]{:S(2)}) collective-permute-start(bf16[384,1152]{1,0:T(8,128)(2,1)} %fusion.1.refs_5_), channel_id=1, source_target_pairs={{0,1},{1,0},{2,3},{3,2},{4,5},{5,4},{6,7},{7,6},{8,9},{9,8},{10,11... | collective-permute-start | bytes 2654216 | tf_op jit(solution)/shard_map/ppermute | solution.py:361
  79.3 3.0 %copy-done.1 = bf16[3,3072,384]{2,1,0:T(8,128)(2,1)S(1)} copy-done((bf16[3,3072,384]{2,1,0:T(8,128)(2,1)S(1)}, bf16[3,3072,384]{2,1,0:T(8,128)(2,1)}, u32[]{:S(2)}) %copy-start.1) | copy-done | bytes 7077912
  82.3 4.6 %project.1.refs_4_ = bf16[3,256,384]{2,1,0:T(8,128)(2,1)S(1)} custom-call(bf16[256,3072]{1,0:T(8,128)(2,1)S(1)} %copy-done, bf16[1,3072]{1,0:T(2,128)(2,1)S(1)} %broadcast_in_dim.39.gain_ref, bf16[3,3072,384]{2,1,0:T(8,128)(2,1)S(1)} %copy-done.1, f32[256,384]{1,0:T(8,128)S(1)} %get-tuple-element.78.cos_ref, f32[256,384]{1,0:T(8,128)S(1)} %get-tuple-element.77.sin_ref), custom_call_target="tpu_custom_call" | custom-call | tf_op jit(solution)/shard_map/project/pallas_call | solution.py:58
  87.1 5.6 %attend.1 = bf16[2,128,384]{2,1,0:T(8,128)(2,1)S(1)} custom-call(s32[4]{0:T(128)S(1)} %pad_add_fusion.refs_0_, s32[8]{0:T(128)S(1)} %copy-done.3, s32[64]{0:T(128)S(1)} %copy-done.4, s32[128]{0:T(128)S(1)} %copy-done.5, bf16[3,256,384]{2,1,0:T(8,128)(2,1)S(1)} %project.1.refs_4_, bf16[16,128,384]{2,1,0:T(8,128)(2,1)} %copy-done.6, ...), custom_call_target="tpu_custom_call" | custom-call | tf_op jit(solution)/shard_map/attend/pallas_call | solution.py:184
  92.9 5.7 %collective-permute-done.17.refs_9_ = bf16[384,1152]{1,0:T(8,128)(2,1)S(1)} collective-permute-done((bf16[384,1152]{1,0:T(8,128)(2,1)}, bf16[384,1152]{1,0:T(8,128)(2,1)S(1)}, u32[]{:S(2)}, u32[]{:S(2)}) %collective-permute-start.17) | collective-permute-done | bytes 884768 | tf_op jit(solution)/shard_map/ppermute | solution.py:361
  100.0 3.6 %branch.1 = bf16[128,3200]{1,0:T(8,128)(2,1)S(1)} custom-call(bf16[128,384]{1,0:T(8,128)(2,1)S(1)} %get-tuple-element.68.refs_0_, bf16[128,384]{1,0:T(8,128)(2,1)S(1)} %collective-permute-done.16.refs_1_, bf16[384,512]{1,0:T(8,128)(2,1)} %copy-done.11, bf16[384,1024]{1,0:T(8,128)(2,1)} %copy-done.8, bf16[384,512]{1,0:T(8,128)(2,1)} %copy-done.10, ...), custom_call_target="tpu_custom_call" | custom-call | tf_op jit(solution)/shard_map/branch/pallas_call | solution.py:226
  104.3 8.1 %collective-permute-start.18 = (bf16[32,3200]{1,0:T(8,128)(2,1)}, bf16[32,3200]{1,0:T(8,128)(2,1)S(1)}, u32[]{:S(2)}, u32[]{:S(2)}) collective-permute-start(bf16[32,3200]{1,0:T(8,128)(2,1)} %get-tuple-element.64), channel_id=1, source_target_pairs={{0,4},{1,5},{2,6},{3,7},{4,0},{5,1},{6,2},{7,3},{8,12},{9,13},{10,... | collective-permute-start | bytes 614408 | tf_op jit(solution)/shard_map/ppermute | solution.py:357
  114.3 2.4 %collective-permute-start.20 = (bf16[32,3200]{1,0:T(8,128)(2,1)S(1)}, bf16[32,3200]{1,0:T(8,128)(2,1)S(1)}, u32[]{:S(2)}, u32[]{:S(2)}) collective-permute-start(bf16[32,3200]{1,0:T(8,128)(2,1)S(1)} %get-tuple-element.62), channel_id=1, source_target_pairs={{0,6},{1,7},{2,0},{3,1},{4,2},{5,3},{6,4},{7,5},{8,14},{9,15},{10,... | collective-permute-start | bytes 614408 | tf_op jit(solution)/shard_map/ppermute | solution.py:357
  116.6 6.5 %collective-permute-done.18 = bf16[32,3200]{1,0:T(8,128)(2,1)S(1)} collective-permute-done((bf16[32,3200]{1,0:T(8,128)(2,1)}, bf16[32,3200]{1,0:T(8,128)(2,1)S(1)}, u32[]{:S(2)}, u32[]{:S(2)}) %collective-permute-start.18) | collective-permute-done | bytes 204832 | tf_op jit(solution)/shard_map/ppermute | solution.py:357
  123.2 3.4 %collective-permute-done.19 = bf16[32,3200]{1,0:T(8,128)(2,1)S(1)} collective-permute-done((bf16[32,3200]{1,0:T(8,128)(2,1)S(1)}, bf16[32,3200]{1,0:T(8,128)(2,1)S(1)}, u32[]{:S(2)}, u32[]{:S(2)}) %collective-permute-start.19) | collective-permute-done | bytes 204832 | tf_op jit(solution)/shard_map/ppermute | solution.py:357
  126.5 4.7 %collective-permute-done.20 = bf16[32,3200]{1,0:T(8,128)(2,1)S(1)} collective-permute-done((bf16[32,3200]{1,0:T(8,128)(2,1)S(1)}, bf16[32,3200]{1,0:T(8,128)(2,1)S(1)}, u32[]{:S(2)}, u32[]{:S(2)}) %collective-permute-start.20) | collective-permute-done | bytes 204832 | tf_op jit(solution)/shard_map/ppermute | solution.py:357
  131.3 2.9 %collective-permute-start.21 = (bf16[32,3200]{1,0:T(8,128)(2,1)S(1)}, bf16[32,3200]{1,0:T(8,128)(2,1)S(1)}, u32[]{:S(2)}, u32[]{:S(2)}) collective-permute-start(bf16[32,3200]{1,0:T(8,128)(2,1)S(1)} %add_convert_fusion.refs_6_), channel_id=1, source_target_pairs={{0,7},{1,0},{2,1},{3,2},{4,3},{5,4},{6,5},{7,6},{8,15},{9,8},{10,9... | collective-permute-start | bytes 614408 | tf_op jit(solution)/shard_map/ppermute | solution.py:357
  134.2 2.8 %collective-permute-start.23 = (bf16[32,3200]{1,0:T(8,128)(2,1)S(1)}, bf16[32,3200]{1,0:T(8,128)(2,1)S(1)}, u32[]{:S(2)}, u32[]{:S(2)}) collective-permute-start(bf16[32,3200]{1,0:T(8,128)(2,1)S(1)} %add_convert_fusion.refs_6_), channel_id=1, source_target_pairs={{0,6},{1,7},{2,0},{3,1},{4,2},{5,3},{6,4},{7,5},{8,14},{9,15},{10,... | collective-permute-start | bytes 614408 | tf_op jit(solution)/shard_map/ppermute | solution.py:357
  137.5 3.1 %collective-permute-done.21.refs_9_ = bf16[32,3200]{1,0:T(8,128)(2,1)S(1)} collective-permute-done((bf16[32,3200]{1,0:T(8,128)(2,1)S(1)}, bf16[32,3200]{1,0:T(8,128)(2,1)S(1)}, u32[]{:S(2)}, u32[]{:S(2)}) %collective-permute-start.21) | collective-permute-done | bytes 204832 | tf_op jit(solution)/shard_map/ppermute | solution.py:357
  140.6 3.9 %collective-permute-done.22.refs_12_ = bf16[32,3200]{1,0:T(8,128)(2,1)S(1)} collective-permute-done((bf16[32,3200]{1,0:T(8,128)(2,1)S(1)}, bf16[32,3200]{1,0:T(8,128)(2,1)S(1)}, u32[]{:S(2)}, u32[]{:S(2)}) %collective-permute-start.22) | collective-permute-done | bytes 204832 | tf_op jit(solution)/shard_map/ppermute | solution.py:357
  144.6 2.1 %collective-permute-done.23.refs_15_ = bf16[32,3200]{1,0:T(8,128)(2,1)S(1)} collective-permute-done((bf16[32,3200]{1,0:T(8,128)(2,1)S(1)}, bf16[32,3200]{1,0:T(8,128)(2,1)S(1)}, u32[]{:S(2)}, u32[]{:S(2)}) %collective-permute-start.23) | collective-permute-done | bytes 204832 | tf_op jit(solution)/shard_map/ppermute | solution.py:357
  146.7 3.8 %collective-permute-done.24.refs_18_ = bf16[32,3200]{1,0:T(8,128)(2,1)S(1)} collective-permute-done((bf16[32,3200]{1,0:T(8,128)(2,1)S(1)}, bf16[32,3200]{1,0:T(8,128)(2,1)S(1)}, u32[]{:S(2)}, u32[]{:S(2)}) %collective-permute-start.24) | collective-permute-done | bytes 204832 | tf_op jit(solution)/shard_map/ppermute | solution.py:357
  156.7 12.3 %score.2 = f32[8,320]{1,0:T(8,128)S(1)} custom-call(s32[6]{0:T(128)S(1)} %stack.67.refs_0_, bf16[16,3072]{1,0:T(8,128)(2,1)S(1)} %copy-done.2, bf16[1,3072]{1,0:T(2,128)(2,1)S(1)} %broadcast_in_dim.43.refs_2_, bf16[3072,2048]{1,0:T(8,128)(2,1)} %all-gather.2.cloned.1.call-done.refs_3_, bf16[256,3072]{1,0:T(8,128)(2,1)S(1)} %copy-done, ...), custom_call_target="tpu_custom_call" | custom-call | flops 4026531840 | bytes 12582912 | tf_op jit(solution)/shard_map/score/pallas_call | solution.py:323
  169.2 11.6 %score.3 = f32[8,192]{1,0:T(8,128)S(1)} custom-call(s32[5]{0:T(128)S(1)} %stack.72.refs_0_, bf16[16,3072]{1,0:T(8,128)(2,1)S(1)} %copy-done.2, bf16[1,3072]{1,0:T(2,128)(2,1)S(1)} %broadcast_in_dim.43.refs_2_, bf16[3072,2048]{1,0:T(8,128)(2,1)} %all-gather.2.cloned.1.call-done.refs_3_, bf16[256,3072]{1,0:T(8,128)(2,1)S(1)} %copy-done, ...), custom_call_target="tpu_custom_call" | custom-call | flops 2415919104 | bytes 12582912 | tf_op jit(solution)/shard_map/score/pallas_call | solution.py:323
  181.2 13.1 %all_to_all.5 = f32[8,8,512]{2,1,0:T(8,128)S(1)} all-to-all(f32[8,8,512]{2,1,0:T(8,128)S(1)} %broadcast_in_dim.46), channel_id=1, replica_groups=mesh['seq'=32,'tensor'=8] {'tensor'}, dimensions={0} | all-to-all | bytes 262144 | tf_op jit(solution)/shard_map/all_to_all | solution.py:530
  (113 shorter events, 27.7 us)
Async XLA Ops:
  7.2 149.6 %all-gather.2.cloned.1.call-start = ((), (), s32[]{:S(2)}) async-start(), calls=%async_computation.1 | async-start | bytes 12976128 | tf_op jit(solution)/shard_map/all_gather | solution.py:456
  8.3 3.3 %collective-permute-start = (bf16[2,128,384]{2,1,0:T(8,128)(2,1)S(1)}, bf16[2,128,384]{2,1,0:T(8,128)(2,1)S(1)}, u32[]{:S(2)}, u32[]{:S(2)}) collective-permute-start(bf16[2,128,384]{2,1,0:T(8,128)(2,1)S(1)} %get-tuple-element.66), channel_id=1, source_target_pairs={{0,8},{8,0},{16,24},{24,16},{32,40},{40,32},{48,56},{56,48},{64,72... | collective-permute-start | bytes 589832 | tf_op jit(solution)/shard_map/ppermute | solution.py:380
  9.6 40.5 %copy-start.10 = (bf16[384,512]{1,0:T(8,128)(2,1)}, bf16[384,512]{1,0:T(8,128)(2,1)S(1)}, u32[]{:S(2)}) copy-start(bf16[384,512]{1,0:T(8,128)(2,1)S(1)} %get-tuple-element.36.refs_4_) | copy-start | bytes 1179652
  9.6 11.8 %collective-permute-start.4 = (bf16[384,512]{1,0:T(8,128)(2,1)S(1)}, bf16[384,512]{1,0:T(8,128)(2,1)S(1)}, u32[]{:S(2)}, u32[]{:S(2)}) collective-permute-start(bf16[384,512]{1,0:T(8,128)(2,1)S(1)} %get-tuple-element.61.refs_2_), channel_id=1, source_target_pairs={{0,1},{1,0},{2,3},{3,2},{4,5},{5,4},{6,7},{7,6},{8,9},{9,8},{10,11... | collective-permute-start | bytes 1179656 | tf_op jit(solution)/shard_map/ppermute | solution.py:361
  11.7 12.4 %collective-permute-start.1 = (bf16[4,128,384]{2,1,0:T(8,128)(2,1)S(1)}, bf16[4,128,384]{2,1,0:T(8,128)(2,1)S(1)}, u32[]{:S(2)}, u32[]{:S(2)}) collective-permute-start(bf16[4,128,384]{2,1,0:T(8,128)(2,1)S(1)} %pad_maximum_fusion.1), channel_id=1, source_target_pairs={{0,48},{8,200},{16,0},{24,216},{32,16},{40,232},{48,32},{56,248},{... | collective-permute-start | bytes 1179656 | tf_op jit(solution)/shard_map/ppermute | solution.py:392
  14.5 9.5 %collective-permute-start.2 = (bf16[4,128,384]{2,1,0:T(8,128)(2,1)S(1)}, bf16[4,128,384]{2,1,0:T(8,128)(2,1)S(1)}, u32[]{:S(2)}, u32[]{:S(2)}) collective-permute-start(bf16[4,128,384]{2,1,0:T(8,128)(2,1)S(1)} %pad_maximum_fusion.1), channel_id=1, source_target_pairs={{0,32},{8,136},{16,48},{24,152},{32,0},{40,168},{48,16},{56,184},{... | collective-permute-start | bytes 1179656 | tf_op jit(solution)/shard_map/ppermute | solution.py:392
  15.3 12.7 %collective-permute-start.3 = (bf16[4,128,384]{2,1,0:T(8,128)(2,1)S(1)}, bf16[4,128,384]{2,1,0:T(8,128)(2,1)S(1)}, u32[]{:S(2)}, u32[]{:S(2)}) collective-permute-start(bf16[4,128,384]{2,1,0:T(8,128)(2,1)S(1)} %pad_maximum_fusion.1), channel_id=1, source_target_pairs={{0,16},{8,72},{16,32},{24,88},{32,48},{40,104},{48,0},{56,120},{64... | collective-permute-start | bytes 1179656 | tf_op jit(solution)/shard_map/ppermute | solution.py:392
  28.3 21.7 %collective-permute-start.5 = (bf16[16,128,384]{2,1,0:T(8,128)(2,1)S(1)}, bf16[16,128,384]{2,1,0:T(8,128)(2,1)S(1)}, u32[]{:S(2)}, u32[]{:S(2)}) collective-permute-start(bf16[16,128,384]{2,1,0:T(8,128)(2,1)S(1)} %pad_maximum_fusion.refs_5_), channel_id=1, source_target_pairs={{0,192},{8,56},{16,208},{24,8},{32,224},{40,24},{48,240},{56,40},{... | collective-permute-start | bytes 4718600 | tf_op jit(solution)/shard_map/ppermute | solution.py:392
  29.1 20.9 %collective-permute-start.6 = (bf16[16,128,384]{2,1,0:T(8,128)(2,1)S(1)}, bf16[16,128,384]{2,1,0:T(8,128)(2,1)}, u32[]{:S(2)}, u32[]{:S(2)}) collective-permute-start(bf16[16,128,384]{2,1,0:T(8,128)(2,1)S(1)} %pad_maximum_fusion.refs_5_), channel_id=1, source_target_pairs={{0,64},{8,24},{16,80},{24,40},{32,96},{40,56},{48,112},{56,8},{64,... | collective-permute-start | bytes 4718600 | tf_op jit(solution)/shard_map/ppermute | solution.py:392
  32.6 15.6 %collective-permute-start.7 = (bf16[384,1024]{1,0:T(8,128)(2,1)S(1)}, bf16[384,1024]{1,0:T(8,128)(2,1)S(1)}, u32[]{:S(2)}, u32[]{:S(2)}) collective-permute-start(bf16[384,1024]{1,0:T(8,128)(2,1)S(1)} %get-tuple-element.33.refs_3_), channel_id=1, source_target_pairs={{0,1},{1,0},{2,3},{3,2},{4,5},{5,4},{6,7},{7,6},{8,9},{9,8},{10,11... | collective-permute-start | bytes 2359304 | tf_op jit(solution)/shard_map/ppermute | solution.py:361
  50.0 25.7 %collective-permute-start.11 = (bf16[16,128,384]{2,1,0:T(8,128)(2,1)S(1)}, bf16[16,128,384]{2,1,0:T(8,128)(2,1)}, u32[]{:S(2)}, u32[]{:S(2)}) collective-permute-start(bf16[16,128,384]{2,1,0:T(8,128)(2,1)S(1)} %pad_maximum_fusion.refs_5_), channel_id=1, source_target_pairs={{0,8},{8,0},{16,24},{24,16},{32,40},{40,32},{48,56},{56,48},{64,72... | collective-permute-start | bytes 4718600 | tf_op jit(solution)/shard_map/ppermute | solution.py:380
  50.2 11.5 %collective-permute-start.10 = (bf16[384,512]{1,0:T(8,128)(2,1)S(1)}, bf16[384,512]{1,0:T(8,128)(2,1)S(1)}, u32[]{:S(2)}, u32[]{:S(2)}) collective-permute-start(bf16[384,512]{1,0:T(8,128)(2,1)S(1)} %get-tuple-element.36.refs_4_), channel_id=1, source_target_pairs={{0,1},{1,0},{2,3},{3,2},{4,5},{5,4},{6,7},{7,6},{8,9},{9,8},{10,11... | collective-permute-start | bytes 1179656 | tf_op jit(solution)/shard_map/ppermute | solution.py:361
  53.5 15.3 %collective-permute-start.8 = (bf16[8,128,384]{2,1,0:T(8,128)(2,1)}, bf16[8,128,384]{2,1,0:T(8,128)(2,1)}, u32[]{:S(2)}, u32[]{:S(2)}) collective-permute-start(bf16[8,128,384]{2,1,0:T(8,128)(2,1)} %slice.65), channel_id=1, source_target_pairs={{0,64},{8,24},{16,80},{24,40},{32,96},{40,56},{48,112},{56,8},{64,... | collective-permute-start | bytes 2359304 | tf_op jit(solution)/shard_map/ppermute | solution.py:392
  56.8 18.3 %collective-permute-start.9 = (bf16[8,128,384]{2,1,0:T(8,128)(2,1)}, bf16[8,128,384]{2,1,0:T(8,128)(2,1)}, u32[]{:S(2)}, u32[]{:S(2)}) collective-permute-start(bf16[8,128,384]{2,1,0:T(8,128)(2,1)} %slice.66), channel_id=1, source_target_pairs={{0,192},{8,56},{16,208},{24,8},{32,224},{40,24},{48,240},{56,40},{... | collective-permute-start | bytes 2359304 | tf_op jit(solution)/shard_map/ppermute | solution.py:392
  56.8 30.2 %collective-permute-start.12 = (bf16[16,128,384]{2,1,0:T(8,128)(2,1)}, bf16[16,128,384]{2,1,0:T(8,128)(2,1)}, u32[]{:S(2)}, u32[]{:S(2)}) collective-permute-start(bf16[16,128,384]{2,1,0:T(8,128)(2,1)} %copy-done.7), channel_id=1, source_target_pairs={{0,8},{8,0},{16,24},{24,16},{32,40},{40,32},{48,56},{56,48},{64,72... | collective-permute-start | bytes 4718600 | tf_op jit(solution)/shard_map/ppermute | solution.py:380
  62.4 24.7 %collective-permute-start.15 = (bf16[16,128,384]{2,1,0:T(8,128)(2,1)}, bf16[16,128,384]{2,1,0:T(8,128)(2,1)}, u32[]{:S(2)}, u32[]{:S(2)}) collective-permute-start(bf16[16,128,384]{2,1,0:T(8,128)(2,1)} %collective-permute-done.6.refs_9_), channel_id=1, source_target_pairs={{0,8},{8,0},{16,24},{24,16},{32,40},{40,32},{48,56},{56,48},{64,72... | collective-permute-start | bytes 4718600 | tf_op jit(solution)/shard_map/ppermute | solution.py:380
  75.1 12.0 %collective-permute-start.13 = (bf16[8,128,384]{2,1,0:T(8,128)(2,1)}, bf16[8,128,384]{2,1,0:T(8,128)(2,1)}, u32[]{:S(2)}, u32[]{:S(2)}) collective-permute-start(bf16[8,128,384]{2,1,0:T(8,128)(2,1)} %collective-permute-done.8.refs_7_), channel_id=1, source_target_pairs={{0,8},{8,0},{16,24},{24,16},{32,40},{40,32},{48,56},{56,48},{64,72... | collective-permute-start | bytes 2359304 | tf_op jit(solution)/shard_map/ppermute | solution.py:380
  75.1 12.0 %collective-permute-start.14 = (bf16[8,128,384]{2,1,0:T(8,128)(2,1)}, bf16[8,128,384]{2,1,0:T(8,128)(2,1)}, u32[]{:S(2)}, u32[]{:S(2)}) collective-permute-start(bf16[8,128,384]{2,1,0:T(8,128)(2,1)} %collective-permute-done.9.refs_8_), channel_id=1, source_target_pairs={{0,8},{8,0},{16,24},{24,16},{32,40},{40,32},{48,56},{56,48},{64,72... | collective-permute-start | bytes 2359304 | tf_op jit(solution)/shard_map/ppermute | solution.py:380
  75.8 22.9 %collective-permute-start.17 = (bf16[384,1152]{1,0:T(8,128)(2,1)}, bf16[384,1152]{1,0:T(8,128)(2,1)S(1)}, u32[]{:S(2)}, u32[]{:S(2)}) collective-permute-start(bf16[384,1152]{1,0:T(8,128)(2,1)} %fusion.1.refs_5_), channel_id=1, source_target_pairs={{0,1},{1,0},{2,3},{3,2},{4,5},{5,4},{6,7},{7,6},{8,9},{9,8},{10,11... | collective-permute-start | bytes 2654216 | tf_op jit(solution)/shard_map/ppermute | solution.py:361
  92.7 7.3 %collective-permute-start.16 = (bf16[128,384]{1,0:T(8,128)(2,1)S(1)}, bf16[128,384]{1,0:T(8,128)(2,1)S(1)}, u32[]{:S(2)}, u32[]{:S(2)}) collective-permute-start(bf16[128,384]{1,0:T(8,128)(2,1)S(1)} %get-tuple-element.67), channel_id=1, source_target_pairs={{0,1},{1,0},{2,3},{3,2},{4,5},{5,4},{6,7},{7,6},{8,9},{9,8},{10,11... | collective-permute-start | bytes 294920 | tf_op jit(solution)/shard_map/ppermute | solution.py:361
  103.6 53.1 %copy-start.2 = (bf16[16,3072]{1,0:T(8,128)(2,1)S(1)}, bf16[16,3072]{1,0:T(8,128)(2,1)}, u32[]{:S(2)}) copy-start(bf16[16,3072]{1,0:T(8,128)(2,1)} %refs_1_.5) | copy-start | bytes 294916
  104.3 18.8 %collective-permute-start.18 = (bf16[32,3200]{1,0:T(8,128)(2,1)}, bf16[32,3200]{1,0:T(8,128)(2,1)S(1)}, u32[]{:S(2)}, u32[]{:S(2)}) collective-permute-start(bf16[32,3200]{1,0:T(8,128)(2,1)} %get-tuple-element.64), channel_id=1, source_target_pairs={{0,4},{1,5},{2,6},{3,7},{4,0},{5,1},{6,2},{7,3},{8,12},{9,13},{10,... | collective-permute-start | bytes 614408 | tf_op jit(solution)/shard_map/ppermute | solution.py:357
  112.5 14.0 %collective-permute-start.19 = (bf16[32,3200]{1,0:T(8,128)(2,1)S(1)}, bf16[32,3200]{1,0:T(8,128)(2,1)S(1)}, u32[]{:S(2)}, u32[]{:S(2)}) collective-permute-start(bf16[32,3200]{1,0:T(8,128)(2,1)S(1)} %get-tuple-element.63), channel_id=1, source_target_pairs={{0,2},{1,3},{2,4},{3,5},{4,6},{5,7},{6,0},{7,1},{8,10},{9,11},{10,... | collective-permute-start | bytes 614408 | tf_op jit(solution)/shard_map/ppermute | solution.py:357
  114.3 16.9 %collective-permute-start.20 = (bf16[32,3200]{1,0:T(8,128)(2,1)S(1)}, bf16[32,3200]{1,0:T(8,128)(2,1)S(1)}, u32[]{:S(2)}, u32[]{:S(2)}) collective-permute-start(bf16[32,3200]{1,0:T(8,128)(2,1)S(1)} %get-tuple-element.62), channel_id=1, source_target_pairs={{0,6},{1,7},{2,0},{3,1},{4,2},{5,3},{6,4},{7,5},{8,14},{9,15},{10,... | collective-permute-start | bytes 614408 | tf_op jit(solution)/shard_map/ppermute | solution.py:357
  131.3 9.3 %collective-permute-start.21 = (bf16[32,3200]{1,0:T(8,128)(2,1)S(1)}, bf16[32,3200]{1,0:T(8,128)(2,1)S(1)}, u32[]{:S(2)}, u32[]{:S(2)}) collective-permute-start(bf16[32,3200]{1,0:T(8,128)(2,1)S(1)} %add_convert_fusion.refs_6_), channel_id=1, source_target_pairs={{0,7},{1,0},{2,1},{3,2},{4,3},{5,4},{6,5},{7,6},{8,15},{9,8},{10,9... | collective-permute-start | bytes 614408 | tf_op jit(solution)/shard_map/ppermute | solution.py:357
  134.2 10.3 %collective-permute-start.22 = (bf16[32,3200]{1,0:T(8,128)(2,1)S(1)}, bf16[32,3200]{1,0:T(8,128)(2,1)S(1)}, u32[]{:S(2)}, u32[]{:S(2)}) collective-permute-start(bf16[32,3200]{1,0:T(8,128)(2,1)S(1)} %add_convert_fusion.refs_6_), channel_id=1, source_target_pairs={{0,1},{1,2},{2,3},{3,4},{4,5},{5,6},{6,7},{7,0},{8,9},{9,10},{10,1... | collective-permute-start | bytes 614408 | tf_op jit(solution)/shard_map/ppermute | solution.py:357
  134.2 12.5 %collective-permute-start.23 = (bf16[32,3200]{1,0:T(8,128)(2,1)S(1)}, bf16[32,3200]{1,0:T(8,128)(2,1)S(1)}, u32[]{:S(2)}, u32[]{:S(2)}) collective-permute-start(bf16[32,3200]{1,0:T(8,128)(2,1)S(1)} %add_convert_fusion.refs_6_), channel_id=1, source_target_pairs={{0,6},{1,7},{2,0},{3,1},{4,2},{5,3},{6,4},{7,5},{8,14},{9,15},{10,... | collective-permute-start | bytes 614408 | tf_op jit(solution)/shard_map/ppermute | solution.py:357
  137.0 13.5 %collective-permute-start.24 = (bf16[32,3200]{1,0:T(8,128)(2,1)S(1)}, bf16[32,3200]{1,0:T(8,128)(2,1)S(1)}, u32[]{:S(2)}, u32[]{:S(2)}) collective-permute-start(bf16[32,3200]{1,0:T(8,128)(2,1)S(1)} %add_convert_fusion.refs_6_), channel_id=1, source_target_pairs={{0,2},{1,3},{2,4},{3,5},{4,6},{5,7},{6,0},{7,1},{8,10},{9,11},{10,... | collective-permute-start | bytes 614408 | tf_op jit(solution)/shard_map/ppermute | solution.py:357
  150.5 18.6 %collective-permute-start.25 = (bf16[32,3200]{1,0:T(8,128)(2,1)S(1)}, bf16[32,3200]{1,0:T(8,128)(2,1)S(1)}, u32[]{:S(2)}, u32[]{:S(2)}) collective-permute-start(bf16[32,3200]{1,0:T(8,128)(2,1)S(1)} %collective-permute-done.23.refs_15_), channel_id=1, source_target_pairs={{0,7},{1,0},{2,1},{3,2},{4,3},{5,4},{6,5},{7,6},{8,15},{9,8},{10,9... | collective-permute-start | bytes 614408 | tf_op jit(solution)/shard_map/ppermute | solution.py:357
  151.7 17.4 %collective-permute-start.26 = (bf16[32,3200]{1,0:T(8,128)(2,1)S(1)}, bf16[32,3200]{1,0:T(8,128)(2,1)S(1)}, u32[]{:S(2)}, u32[]{:S(2)}) collective-permute-start(bf16[32,3200]{1,0:T(8,128)(2,1)S(1)} %collective-permute-done.24.refs_18_), channel_id=1, source_target_pairs={{0,1},{1,2},{2,3},{3,4},{4,5},{5,6},{6,7},{7,0},{8,9},{9,10},{10,1... | collective-permute-start | bytes 614408 | tf_op jit(solution)/shard_map/ppermute | solution.py:357
  153.8 15.3 %collective-permute-start.27 = (bf16[16,3200]{1,0:T(8,128)(2,1)}, bf16[16,3200]{1,0:T(8,128)(2,1)S(1)}, u32[]{:S(2)}, u32[]{:S(2)}) collective-permute-start(bf16[16,3200]{1,0:T(8,128)(2,1)} %slice.69), channel_id=1, source_target_pairs={{0,6},{1,7},{2,0},{3,1},{4,2},{5,3},{6,4},{7,5},{8,14},{9,15},{10,... | collective-permute-start | bytes 307208 | tf_op jit(solution)/shard_map/ppermute | solution.py:357
  154.9 14.2 %collective-permute-start.28 = (bf16[16,3200]{1,0:T(8,128)(2,1)}, bf16[16,3200]{1,0:T(8,128)(2,1)S(1)}, u32[]{:S(2)}, u32[]{:S(2)}) collective-permute-start(bf16[16,3200]{1,0:T(8,128)(2,1)} %slice.70), channel_id=1, source_target_pairs={{0,2},{1,3},{2,4},{3,5},{4,6},{5,7},{6,0},{7,1},{8,10},{9,11},{10,... | collective-permute-start | bytes 307208 | tf_op jit(solution)/shard_map/ppermute | solution.py:357
  (17 other events, 240.6 us)
Sparse Core Ops, SparseCore 0:
  50.1 69.5 all-gather.1
where the time goes:
time: 202 us
  waiting for transfers between devices  77.9 us (39%)
  starting transfers between devices  39.6 us (20%)
  Pallas kernels  37.7 us (19%)
  between operations  14.4 us (7%)
  local copies, waits for them, and re-layouts  13.7 us (7%)
  blocking collectives  13.1 us (6%)
  other arithmetic  5.44 us (3%)
    ppermute x5, waiting for transfers between devices, partnered(): return lax.ppermute(value, 'tensor', [(i, i ^ 1) for i in range(ranks)])  32.5 us
    ppermute x11, waiting for transfers between devices, shifted(): lax.ppermute(value, 'tensor', [(i, (i + step) % ranks) for i in range(ran...  27.5 us
    pallas_call x2, Pallas kernels, score(): pl.pallas_call(score_kernel, grid_spec=pltpu.PrefetchScalarGridSpec(num_s...  23.9 us
    ppermute x11, starting transfers between devices, shifted(): lax.ppermute(value, 'tensor', [(i, (i + step) % ranks) for i in range(ran...  23 us
    ppermute x7, waiting for transfers between devices, turned(): return lax.ppermute(value, 'seq', [(i, target(i)) for i in range(32)])  17.8 us
    all_to_all x1, blocking collectives, local(): lax.all_to_all(jnp.broadcast_to(ordered[None], (ranks, 8, 2 * tok_rows)),...  13.1 us
    ppermute x7, starting transfers between devices, turned(): return lax.ppermute(value, 'seq', [(i, target(i)) for i in range(32)])  11.1 us
    pallas_call x1, Pallas kernels, attend(): pl.pallas_call(attend_kernel, grid_spec=pltpu.PrefetchScalarGridSpec(num_...  5.59 us
  transfers between devices with their start and end apart: 30, of which 17 were waited for; matrix products, arithmetic and copies ran while one was open for 6% of the time, Pallas kernels for 13%

commit v1 on v0

--- a/solution.py
+++ b/solution.py
@@ -79,9 +79,9 @@
 
 def attend_kernel(*refs):
     first_ref, counts_ref, index_ref, owner_ref = refs[:4]
-    qkv_ref = refs[4]
+    qkv_ref, cached_values_ref = refs[4:6]
     out_ref, keys, values, sems = refs[-4:]
-    pieces = refs[5:-4]
+    pieces = refs[6:-4]
     rollouts = keys.shape[0]
     width = qkv_ref.shape[2]
     heads = width // HEAD_WIDTH
@@ -91,27 +91,26 @@
 
     def start_copies(r, j):
         slot = index_ref[owner_ref[first + r] * MAXP + j]
-        device = slot // 2
+        device, path = slot // 2, slot % 2
         down_y = (device // 8 - my_y + 4) % 4
         down_x = (device // 2 % 4 - my_x + 4) % 4
-        other = (device % 2 != my_core).astype(jnp.int32)
+        far = jnp.where(path == 0, down_y, down_x)
+        near = jnp.where(path == 0, down_x, down_y)
+        at = near * 2 + (device % 2 != path).astype(jnp.int32)
+        high = ((far == 2) & (at >= 4)).astype(jnp.int32)
+        piece = far + high + (far == 3).astype(jnp.int32)
+        piece = piece + 5 * (my_core != path).astype(jnp.int32)
+        at = at - 4 * high
         rows = pl.ds(pl.multiple_of(j * PAGE, PAGE), PAGE)
-        for which, (buffer, far, near) in enumerate(
-            ((keys, down_y, down_x), (values, down_x, down_y))
-        ):
-            at = near * 4 + 2 * (device % 2 != which).astype(jnp.int32) + slot % 2
-            high = ((far == 2) & (at >= 8)).astype(jnp.int32)
-            piece = far + high + (far == 3).astype(jnp.int32)
-            piece = piece + 5 * (my_core != which).astype(jnp.int32)
-            at = at - 8 * high
-            for p, ref in enumerate(pieces):
-
-                @pl.when(piece == p)
-                def _():
-                    row = jnp.minimum(at, ref.shape[0] - 1)
-                    pltpu.make_async_copy(
-                        ref.at[row], buffer.at[r, rows], sems.at[r, which, j]
-                    ).start()
+        pltpu.make_async_copy(
+            cached_values_ref.at[slot], values.at[r, rows], sems.at[r, 1, j]
+        ).start()
+        for p, ref in enumerate(pieces):
+
+            @pl.when(piece == p)
+            def _():
+                row = jnp.minimum(at, ref.shape[0] - 1)
+                pltpu.make_async_copy(ref.at[row], keys.at[r, rows], sems.at[r, 0, j]).start()
 
         return 0
 
@@ -176,17 +175,19 @@
     lax.fori_loop(0, rollouts, mix_rollout, 0)
 
 
-def attend(first, counts, index, owner, qkv, pieces):
+def attend(first, counts, index, owner, qkv, cached_values, pieces):
     _, rows, width = qkv.shape
     rollouts = rows // LEN
     vmem = pl.BlockSpec(memory_space=pltpu.VMEM)
-    pieces = [pltpu.with_memory_space_constraint(piece, pltpu.HBM) for piece in pieces]
+    cached = [
+        pltpu.with_memory_space_constraint(piece, pltpu.HBM) for piece in [cached_values] + pieces
+    ]
     return pl.pallas_call(
         attend_kernel,
         grid_spec=pltpu.PrefetchScalarGridSpec(
             num_scalar_prefetch=4,
             grid=(),
-            in_specs=[vmem] + [pl.BlockSpec(memory_space=pltpu.HBM)] * len(pieces),
+            in_specs=[vmem] + [pl.BlockSpec(memory_space=pltpu.HBM)] * len(cached),
             out_specs=vmem,
             scratch_shapes=[
                 pltpu.VMEM((rollouts, MAXP * PAGE, width), BF16),
@@ -197,41 +198,33 @@
         out_shape=jax.ShapeDtypeStruct((2, rows // 2, width), BF16),
         compiler_params=pltpu.CompilerParams(vmem_limit_bytes=VMEM_LIMIT),
         name="attend",
-    )(first, counts, index, owner, qkv, *pieces)
-
-
-def branch_kernel(*refs):
-    mine_ref, theirs_ref = refs[:2]
-    out_ref = refs[-1]
-    chunks = refs[2:-1]
-    count = len(chunks) // 2
-    start = 0
-    for own, partner in zip(chunks[:count], chunks[count:]):
-        columns = slice(start, start + own.shape[1])
-        out_ref[:, columns] = (
-            jnp.dot(mine_ref[...], own[...], preferred_element_type=F32)
-            + jnp.dot(theirs_ref[...], partner[...], preferred_element_type=F32)
-        ).astype(BF16)
-        start += own.shape[1]
+    )(first, counts, index, owner, qkv, *cached)
+
+
+def branch_kernel(mine_ref, theirs_ref, own_ref, partner_ref, out_ref):
+    out_ref[...] = (
+        jnp.dot(mine_ref[...], own_ref[...], preferred_element_type=F32)
+        + jnp.dot(theirs_ref[...], partner_ref[...], preferred_element_type=F32)
+    ).astype(BF16)
 
 
 def branch_part(mine, theirs, own, partner):
-    width = sum(chunk.shape[1] for chunk in own)
-    operands = [mine, theirs] + [
-        pltpu.with_memory_space_constraint(chunk, pltpu.HBM)
-        for chunk in list(own) + list(partner)
-    ]
+    rows, width = mine.shape
+    columns = own.shape[1]
+    tile = columns // 5
+    own, partner = (pltpu.with_memory_space_constraint(w, pltpu.HBM) for w in (own, partner))
     whole = lambda i: (0, 0)
-    out = jax.ShapeDtypeStruct((mine.shape[0], width), BF16)
+    across = lambda i: (0, i)
     return pl.pallas_call(
         branch_kernel,
-        grid=(1,),
-        in_specs=[pl.BlockSpec(operand.shape, whole) for operand in operands],
-        out_specs=pl.BlockSpec(out.shape, whole),
-        out_shape=out,
+        grid=(columns // tile,),
+        in_specs=[pl.BlockSpec((rows, width), whole)] * 2
+        + [pl.BlockSpec((width, tile), across)] * 2,
+        out_specs=pl.BlockSpec((rows, tile), across),
+        out_shape=jax.ShapeDtypeStruct((rows, columns), BF16),
         compiler_params=pltpu.CompilerParams(vmem_limit_bytes=VMEM_LIMIT),
         name="branch",
-    )(*operands)
+    )(mine, theirs, own, partner)
 
 
 def two_parts(value):
@@ -241,11 +234,17 @@
 
 def score_kernel(*refs):
     place_ref, up_ref, gain_ref, head_ref = refs[:4]
-    out_ref, normed, deltas, scales, wanted, largest, total, picked = refs[-8:]
+    out_ref, normed, deltas, scales, wanted, logits, adapters, packed = refs[-8:]
     inputs = refs[4:-8]
     step = pl.program_id(0)
+    steps, _, depth = normed.shape
     rank, model = up_ref.shape
     rows = deltas.shape[0]
+    vocab = head_ref.shape[1]
+
+    def store_normed(at, value):
+        for k in range(steps):
+            normed[k, at, :] = value[:, k * depth : (k + 1) * depth]
 
     @pl.when(step == 0)
     def _():
@@ -262,44 +261,52 @@
                 jnp.mean(reference * reference, axis=1, keepdims=True) + EPSILON
             )
             policy_scale = lax.rsqrt(jnp.mean(policy * policy, axis=1, keepdims=True) + EPSILON)
-            normed[at, :] = (reference * reference_scale * gain).astype(BF16)
+            store_normed(at, (reference * reference_scale * gain).astype(BF16))
             deltas[at, :] = jnp.concatenate([delta, delta], axis=1)
             scales[0, at, :] = policy_scale / reference_scale
             scales[1, at, :] = policy_scale
-            wanted[at, :] = target_ref[...]
+            wanted[at, :] = target_ref[...] - place_ref[0] * vocab
         high, low = two_parts(up.astype(F32) * gain)
-        normed[rows : rows + rank, :] = high
-        normed[rows + rank :, :] = low
-        largest[...] = jnp.full_like(largest, NEGATIVE)
-        total[...] = jnp.zeros_like(total)
-        picked[...] = jnp.zeros_like(picked)
-
-    product = jnp.dot(normed[...], head_ref[...], preferred_element_type=F32)
-    reference_logits = product[:rows]
-    high, low = two_parts(product[rows : rows + rank] + product[rows + rank :])
-    adapted = jnp.dot(
-        deltas[...], jnp.concatenate([high, low], axis=0), preferred_element_type=F32
-    )
-    policy_logits = scales[0] * reference_logits + scales[1] * adapted
-    columns = lax.broadcasted_iota(jnp.int32, reference_logits.shape, 1)
-    tile = head_ref.shape[1]
-    hit = columns == wanted[...] - (place_ref[0] * pl.num_programs(0) + step) * tile
-    for which, logits in enumerate((policy_logits, reference_logits)):
-        picked[which] += jnp.sum(jnp.where(hit, logits, 0.0), axis=1, keepdims=True)
-        before = largest[which]
-        after = jnp.maximum(before, jnp.max(logits, axis=1, keepdims=True))
-        total[which] = total[which] * jnp.exp(before - after) + jnp.sum(
-            jnp.exp(logits - after), axis=1, keepdims=True
+        store_normed(slice(rows, rows + rank), high)
+        store_normed(slice(rows + rank, rows + 2 * rank), low)
+        logits[...] = jnp.zeros_like(logits)
+
+    tile = 256
+
+    def multiply(n, _):
+        columns = pl.ds(pl.multiple_of(n * tile, tile), tile)
+        logits[:, columns] += jnp.dot(
+            normed[step], head_ref[:, columns], preferred_element_type=F32
         )
-        largest[which] = after
-
-    @pl.when(step == pl.num_programs(0) - 1)
+        return 0
+
+    lax.fori_loop(0, vocab // tile, multiply, 0)
+
+    @pl.when(step == steps - 1)
     def _():
-        lane = lax.broadcasted_iota(jnp.int32, (2, rows, 128), 2)
-        packed = jnp.where(
-            lane == 0, largest[...], jnp.where(lane == 1, total[...], picked[...])
-        )
-        out_ref[...] = jnp.transpose(packed.reshape(2 * rows, 128))[:8, :]
+        high, low = two_parts(logits[rows : rows + rank, :] + logits[rows + rank :, :])
+        adapters[:rank, :] = high
+        adapters[rank:, :] = low
+        size = 32
+
+        def summarize(n, _):
+            at = pl.ds(pl.multiple_of(n * size, size), size)
+            reference_logits = logits[at, :]
+            adapted = jnp.dot(deltas[at, :], adapters[...], preferred_element_type=F32)
+            policy_logits = scales[0, at, :] * reference_logits + scales[1, at, :] * adapted
+            hit = lax.broadcasted_iota(jnp.int32, (size, vocab), 1) == wanted[at, :]
+            lane = lax.broadcasted_iota(jnp.int32, (size, 128), 1)
+            for which, here in enumerate((policy_logits, reference_logits)):
+                picked = jnp.sum(jnp.where(hit, here, 0.0), axis=1, keepdims=True)
+                largest = jnp.max(here, axis=1, keepdims=True)
+                total = jnp.sum(jnp.exp(here - largest), axis=1, keepdims=True)
+                packed[which, at, :] = jnp.where(
+                    lane == 0, largest, jnp.where(lane == 1, total, picked)
+                )
+            return 0
+
+        lax.fori_loop(0, rows // size, summarize, 0)
+        out_ref[...] = jnp.transpose(packed[...].reshape(2 * rows, 128))[:8, :]
 
 
 def score(place, hidden, up, gain, targets, head, blocks):
@@ -307,7 +314,8 @@
     vocab = head.shape[1]
     rank = up.shape[0]
     rows = sum(block.shape[0] for block in blocks)
-    tile = 256
+    steps = 4
+    depth = model // steps
     whole = lambda i, p: (0, 0)
     per_block, operands = [], []
     for k, block in enumerate(blocks):
@@ -319,27 +327,26 @@
             pl.BlockSpec(block.shape, whole),
         ]
         operands += [hidden, targets, block]
-    column = pltpu.VMEM((2, rows, 1), F32)
     return pl.pallas_call(
         score_kernel,
         grid_spec=pltpu.PrefetchScalarGridSpec(
             num_scalar_prefetch=1,
-            grid=(vocab // tile,),
+            grid=(steps,),
             in_specs=[
                 pl.BlockSpec(up.shape, whole),
                 pl.BlockSpec(gain.shape, whole),
-                pl.BlockSpec((model, tile), lambda i, p: (0, i)),
+                pl.BlockSpec((depth, vocab), lambda i, p: (i, 0)),
             ]
             + per_block,
             out_specs=pl.BlockSpec((8, 2 * rows), whole),
             scratch_shapes=[
-                pltpu.VMEM((rows + 2 * rank, model), BF16),
+                pltpu.VMEM((steps, rows + 2 * rank, depth), BF16),
                 pltpu.VMEM((rows, 2 * rank), BF16),
-                column,
+                pltpu.VMEM((2, rows, 1), F32),
                 pltpu.VMEM((rows, 1), jnp.int32),
-                column,
-                column,
-                column,
+                pltpu.VMEM((rows + 2 * rank, vocab), F32),
+                pltpu.VMEM((2 * rank, vocab), BF16),
+                pltpu.VMEM((2, rows, 128), F32),
             ],
         ),
         out_shape=jax.ShapeDtypeStruct((8, 2 * rows), F32),
@@ -392,33 +399,24 @@
     return lax.ppermute(value, "seq", [(i, target(i)) for i in range(32)])
 
 
-def gather_pages(keys, values, chunks, ranks):
-    first_core = lax.axis_index("seq") % 2 == 0
-    kept = jnp.where(first_core, keys, values)
-    sent = jnp.where(first_core, values, keys)
+def gather_keys(keys, weights, project_now, ranks):
+    core = lax.axis_index("seq") % 2
+    kept = lax.dynamic_slice_in_dim(keys, core, 1, 0)
+    sent = lax.dynamic_slice_in_dim(keys, 1 - core, 1, 0)
     pair = jnp.concatenate([kept, crossed(sent)])
-    partner = [partnered(chunks[0], ranks)]
-    line = [pair] + [turned(pair, 0, step) for step in (3, 2, 1)]
-    line, partner[0] = lax.optimization_barrier((line, partner[0]))
+    partner = partnered(weights, ranks)
+    line = lax.optimization_barrier([pair] + [turned(pair, 0, step) for step in (3, 2, 1)])
     line = lax.optimization_barrier(jnp.concatenate(line))
     front, behind = turned(line, 1, 3), turned(line, 1, 1)
     near = crossed(line)
-    sources = lax.optimization_barrier((chunks[1], line))
-    partner.append(partnered(sources[0], ranks))
-    front, behind, second = lax.optimization_barrier((front, behind, partner[1]))
-    partner[1] = second
+    front, behind, qkv = lax.optimization_barrier((front, behind, project_now()))
     middle = front.shape[0] // 2
     low, high = turned(behind[:middle], 1, 1), turned(front[middle:], 1, 3)
-    sources = lax.optimization_barrier((chunks[2], front))
-    partner.append(partnered(sources[0], ranks))
     far_front, far_behind = crossed(front), crossed(behind)
-    low, high, third = lax.optimization_barrier((low, high, partner[2]))
-    partner[2] = third
-    sources = lax.optimization_barrier((chunks[3], low))
-    partner.append(partnered(sources[0], ranks))
+    low, high, partner = lax.optimization_barrier((low, high, partner))
     pieces = [line, front, low, high, behind]
     pieces += [near, far_front, crossed(low), crossed(high), far_behind]
-    return pieces, partner, front
+    return pieces, partner, qkv
 
 
 def local(
@@ -446,15 +444,8 @@
     me = lax.axis_index("seq")
     rank = lax.axis_index("tensor")
     down = jnp.pad(adapter_down_weight, ((0, 0), (0, PAD - adapter_down_weight.shape[1])))
-    cuts = (0, model // 6, model // 6 * 3, model // 6 * 4, model)
-    chunks = [output_weight[:, a:b] for a, b in zip(cuts, cuts[1:])]
-    chunks[-1] = jnp.concatenate([chunks[-1], down], axis=1)
-    pieces, partner_chunks, stage = gather_pages(
-        prompt_key_slots, prompt_value_slots, chunks, ranks
-    )
-    head_rows, _ = lax.optimization_barrier((head.T, stage))
-    head_columns = lax.all_gather(head_rows, "seq", axis=0, tiled=True)
-
+    weights = jnp.concatenate([output_weight, down], axis=1)
+    cached_values = lax.all_gather(prompt_value_slots, "seq", axis=0, tiled=True)
     groups_iota = jnp.arange(counts.shape[0], dtype=jnp.int32)
     my_groups = lax.dynamic_slice_in_dim(owner, first, rollouts_here, 0)
     my_pages = jnp.sum(
@@ -465,26 +456,34 @@
     place_in_head = jnp.arange(width_here, dtype=jnp.int32) % half
     frequency = 10000.0 ** (-place_in_head.astype(F32) * 2.0 / HEAD_WIDTH)
     angles = positions.astype(F32)[:, None] * frequency[None, :]
-    qkv = project(
-        hidden,
-        attention_norm_gain[None, :],
-        query_key_value_weight,
-        jnp.cos(angles),
-        jnp.sin(angles),
+    pieces, partner_weights, qkv = gather_keys(
+        prompt_key_slots,
+        weights,
+        lambda: project(
+            hidden,
+            attention_norm_gain[None, :],
+            query_key_value_weight,
+            jnp.cos(angles),
+            jnp.sin(angles),
+        ),
+        ranks,
     )
+    head_rows, cached_values, pieces = lax.optimization_barrier((head.T, cached_values, pieces))
+    head_columns = lax.all_gather(head_rows, "seq", axis=0, tiled=True)
     attended = attend(
         jnp.stack([first, me // 8, me // 2 % 4, me % 2]).astype(jnp.int32),
         counts,
         page_slot_index,
         owner,
         qkv,
+        cached_values,
         pieces,
     )
     branch = branch_part(
         lax.dynamic_index_in_dim(attended, rank % 2, 0, False),
         partnered(lax.dynamic_index_in_dim(attended, 1 - rank % 2, 0, False), ranks),
-        chunks,
-        partner_chunks,
+        weights,
+        partner_weights,
     )
     mine = reduce_rows(branch, ranks)
     size = tok_rows // ranks

time: 202 us -> 193 us (0.955)
  waiting for transfers between devices: 77.9 us -> 64 us
  Pallas kernels: 37.7 us -> 41.1 us
  blocking collectives: 13.1 us -> 16.3 us
    ppermute x5 -> x2, waiting for transfers between devices: 32.5 us -> 7.51 us  [partnered(): return lax.ppermute(value, 'tensor', [(i, i ^ 1) for i in range(ranks)])]
    ppermute x7, waiting for transfers between devices: 17.8 us -> 24.7 us  [turned(): return lax.ppermute(value, 'seq', [(i, target(i)) for i in range(32)])]
    slice x4 -> x2, local copies, waits for them, and re-layouts: 5.28 us -> 2.07 us  [gather_keys(): low, high = (turned(behind[:middle], 1, 1), turned(front[middle:], 1, 3))]
    all_to_all x1, blocking collectives: 13.1 us -> 16.3 us  [local(): lax.all_to_all(jnp.broadcast_to(ordered[None], (ranks, 8, 2 * tok_rows)),...]
    unnamed x39 -> x35, local copies, waits for them, and re-layouts: 4.65 us -> 7.4 us
    all_gather x1, waiting for transfers between devices: 0.01 us -> 2.34 us  [local(): head_columns = lax.all_gather(head_rows, 'seq', axis=0, tiled=True)]
    ppermute x5 -> x2, starting transfers between devices: 4.69 us -> 3.74 us  [partnered(): return lax.ppermute(value, 'tensor', [(i, i ^ 1) for i in range(ranks)])]
  transfers between devices with their start and end apart: 30 -> 28, of which waited for: 17 -> 17; matrix products, arithmetic and copies ran while one was open for 6% -> 6% of each run, Pallas kernels for 13% -> 15%
where the time goes in v1:
time: 193 us; the launch traced here: 192 us
  waiting for transfers between devices  64 us (33%)
  Pallas kernels  41.1 us (21%)
  starting transfers between devices  37.7 us (20%)
  blocking collectives  16.3 us (8%)
  between operations  14.4 us (7%)
  local copies, waits for them, and re-layouts  13.2 us (7%)
  other arithmetic  5.47 us (3%)
    ppermute x11, waiting for transfers between devices, shifted(): lax.ppermute(value, 'tensor', [(i, (i + step) % ranks) for i in range(ran...  27.5 us
    pallas_call x2, Pallas kernels, score(): pl.pallas_call(score_kernel, grid_spec=pltpu.PrefetchScalarGridSpec(num_s...  25.9 us
    ppermute x7, waiting for transfers between devices, turned(): return lax.ppermute(value, 'seq', [(i, target(i)) for i in range(32)])  24.7 us
    ppermute x11, starting transfers between devices, shifted(): lax.ppermute(value, 'tensor', [(i, (i + step) % ranks) for i in range(ran...  22 us
    all_to_all x1, blocking collectives, local(): lax.all_to_all(jnp.broadcast_to(ordered[None], (ranks, 8, 2 * tok_rows)),...  16.3 us
    ppermute x7, starting transfers between devices, turned(): return lax.ppermute(value, 'seq', [(i, target(i)) for i in range(32)])  10.7 us
    ppermute x2, waiting for transfers between devices, partnered(): return lax.ppermute(value, 'tensor', [(i, i ^ 1) for i in range(ranks)])  7.51 us
    unnamed x35, local copies, waits for them, and re-layouts  7.4 us
  transfers between devices with their start and end apart: 28, of which 17 were waited for; matrix products, arithmetic and copies ran while one was open for 6% of the time, Pallas kernels for 15%

profile of v1, /device:TPU:24, one launch (start us, length us, event | category | flops | bytes accessed | tf_op | source)
XLA Modules:
  0.0 192.3 jit_solution(16176106538809597835)
XLA Ops:
  8.8 3.4 %fusion.1.own_ref = bf16[384,3200]{1,0:T(8,128)(2,1)} fusion(bf16[384,16]{1,0:T(8,128)(2,1)S(1)} %copy.50, bf16[384,3072]{1,0:T(8,128)(2,1)} %param.17), kind=kLoop, calls=%fused_computation.2 | loop fusion | flops 7372800 | bytes 4829184 | tf_op jit(solution)/shard_map/concatenate | solution.py:447
  12.2 1.9 collective-permute-start.8
  15.6 2.8 %collective-permute-start.1 = (bf16[2,128,384]{2,1,0:T(8,128)(2,1)S(1)}, bf16[2,128,384]{2,1,0:T(8,128)(2,1)S(1)}, u32[]{:S(2)}, u32[]{:S(2)}) collective-permute-start(bf16[2,128,384]{2,1,0:T(8,128)(2,1)S(1)} %pad_maximum_fusion.1), channel_id=1, source_target_pairs={{0,48},{8,200},{16,0},{24,216},{32,16},{40,232},{48,32},{56,248},{... | collective-permute-start | bytes 589832 | tf_op jit(solution)/shard_map/ppermute | solution.py:399
  20.4 3.4 %collective-permute-done.1 = bf16[2,128,384]{2,1,0:T(8,128)(2,1)S(1)} collective-permute-done((bf16[2,128,384]{2,1,0:T(8,128)(2,1)S(1)}, bf16[2,128,384]{2,1,0:T(8,128)(2,1)S(1)}, u32[]{:S(2)}, u32[]{:S(2)}) %collective-permute-start.1) | collective-permute-done | bytes 196640 | tf_op jit(solution)/shard_map/ppermute | solution.py:399
  23.8 1.9 %collective-permute-done.2 = bf16[2,128,384]{2,1,0:T(8,128)(2,1)S(1)} collective-permute-done((bf16[2,128,384]{2,1,0:T(8,128)(2,1)S(1)}, bf16[2,128,384]{2,1,0:T(8,128)(2,1)S(1)}, u32[]{:S(2)}, u32[]{:S(2)}) %collective-permute-start.2) | collective-permute-done | bytes 196640 | tf_op jit(solution)/shard_map/ppermute | solution.py:399
  25.7 2.0 %collective-permute-done.3 = bf16[2,128,384]{2,1,0:T(8,128)(2,1)S(1)} collective-permute-done((bf16[2,128,384]{2,1,0:T(8,128)(2,1)S(1)}, bf16[2,128,384]{2,1,0:T(8,128)(2,1)S(1)}, u32[]{:S(2)}, u32[]{:S(2)}) %collective-permute-start.3) | collective-permute-done | bytes 196640 | tf_op jit(solution)/shard_map/ppermute | solution.py:399
  28.7 2.5 %collective-permute-start.5 = (bf16[8,128,384]{2,1,0:T(8,128)(2,1)S(1)}, bf16[8,128,384]{2,1,0:T(8,128)(2,1)}, u32[]{:S(2)}, u32[]{:S(2)}) collective-permute-start(bf16[8,128,384]{2,1,0:T(8,128)(2,1)S(1)} %pad_maximum_fusion.refs_6_), channel_id=1, source_target_pairs={{0,64},{8,24},{16,80},{24,40},{32,96},{40,56},{48,112},{56,8},{64,... | collective-permute-start | bytes 2359304 | tf_op jit(solution)/shard_map/ppermute | solution.py:399
  32.8 3.1 %copy-done.1 = bf16[3,3072,384]{2,1,0:T(8,128)(2,1)S(1)} copy-done((bf16[3,3072,384]{2,1,0:T(8,128)(2,1)S(1)}, bf16[3,3072,384]{2,1,0:T(8,128)(2,1)}, u32[]{:S(2)}) %copy-start.1) | copy-done | bytes 7077912
  35.9 4.6 %project.1.refs_4_ = bf16[3,256,384]{2,1,0:T(8,128)(2,1)S(1)} custom-call(bf16[256,3072]{1,0:T(8,128)(2,1)S(1)} %copy-done, bf16[1,3072]{1,0:T(2,128)(2,1)S(1)} %broadcast_in_dim.39.gain_ref, bf16[3,3072,384]{2,1,0:T(8,128)(2,1)S(1)} %copy-done.1, f32[256,384]{1,0:T(8,128)S(1)} %get-tuple-element.88.cos_ref, f32[256,384]{1,0:T(8,128)S(1)} %get-tuple-element.87.sin_ref), custom_call_target="tpu_custom_call" | custom-call | tf_op jit(solution)/shard_map/project/pallas_call | solution.py:58
  40.5 2.3 %collective-permute-done.4.refs_7_ = bf16[8,128,384]{2,1,0:T(8,128)(2,1)} collective-permute-done((bf16[8,128,384]{2,1,0:T(8,128)(2,1)S(1)}, bf16[8,128,384]{2,1,0:T(8,128)(2,1)}, u32[]{:S(2)}, u32[]{:S(2)}) %collective-permute-start.4) | collective-permute-done | bytes 786464 | tf_op jit(solution)/shard_map/ppermute | solution.py:399
  43.8 2.8 %collective-permute-start.6 = (bf16[4,128,384]{2,1,0:T(8,128)(2,1)S(1)}, bf16[4,128,384]{2,1,0:T(8,128)(2,1)S(1)}, u32[]{:S(2)}, u32[]{:S(2)}) collective-permute-start(bf16[4,128,384]{2,1,0:T(8,128)(2,1)S(1)} %slice.51), channel_id=1, source_target_pairs={{0,64},{8,24},{16,80},{24,40},{32,96},{40,56},{48,112},{56,8},{64,... | collective-permute-start | bytes 1179656 | tf_op jit(solution)/shard_map/ppermute | solution.py:399
  48.4 8.3 %collective-permute-done.6.refs_8_ = bf16[4,128,384]{2,1,0:T(8,128)(2,1)S(1)} collective-permute-done((bf16[4,128,384]{2,1,0:T(8,128)(2,1)S(1)}, bf16[4,128,384]{2,1,0:T(8,128)(2,1)S(1)}, u32[]{:S(2)}, u32[]{:S(2)}) %collective-permute-start.6) | collective-permute-done | bytes 393248 | tf_op jit(solution)/shard_map/ppermute | solution.py:399
  56.7 6.8 %collective-permute-done.7.refs_9_ = bf16[4,128,384]{2,1,0:T(8,128)(2,1)S(1)} collective-permute-done((bf16[4,128,384]{2,1,0:T(8,128)(2,1)S(1)}, bf16[4,128,384]{2,1,0:T(8,128)(2,1)S(1)}, u32[]{:S(2)}, u32[]{:S(2)}) %collective-permute-start.7) | collective-permute-done | bytes 393248 | tf_op jit(solution)/shard_map/ppermute | solution.py:399
  63.5 4.3 %collective-permute-done.8.partner_ref = bf16[384,3200]{1,0:T(8,128)(2,1)} collective-permute-done((bf16[384,3200]{1,0:T(8,128)(2,1)}, bf16[384,3200]{1,0:T(8,128)(2,1)}, u32[]{:S(2)}, u32[]{:S(2)}) %collective-permute-start.8) | collective-permute-done | bytes 2457632 | tf_op jit(solution)/shard_map/ppermute | solution.py:368
  72.0 5.8 %attend.1 = bf16[2,128,384]{2,1,0:T(8,128)(2,1)S(1)} custom-call(s32[4]{0:T(128)S(1)} %pad_add_fusion.refs_0_, s32[8]{0:T(128)S(1)} %copy-done.3, s32[64]{0:T(128)S(1)} %copy-done.4, s32[128]{0:T(128)S(1)} %copy-done.5, bf16[3,256,384]{2,1,0:T(8,128)(2,1)S(1)} %project.1.refs_4_, bf16[64,128,384]{2,1,0:T(8,128)(2,1)} %all-gather.3.cloned.1.call-done.refs_5_, ...), custom_call_target="tpu_custom_call" | custom-call | tf_op jit(solution)/shard_map/attend/pallas_call | solution.py:185
  77.9 1.8 collective-permute-start.14
  79.7 3.2 %collective-permute-done.14.theirs_ref = bf16[128,384]{1,0:T(8,128)(2,1)S(1)} collective-permute-done((bf16[128,384]{1,0:T(8,128)(2,1)S(1)}, bf16[128,384]{1,0:T(8,128)(2,1)S(1)}, u32[]{:S(2)}, u32[]{:S(2)}) %collective-permute-start.14) | collective-permute-done | bytes 98336 | tf_op jit(solution)/shard_map/ppermute | solution.py:368
  82.9 4.8 %branch.1 = bf16[128,3200]{1,0:T(8,128)(2,1)S(1)} custom-call(bf16[128,384]{1,0:T(8,128)(2,1)S(1)} %get-tuple-element.76.mine_ref, bf16[128,384]{1,0:T(8,128)(2,1)S(1)} %collective-permute-done.14.theirs_ref, bf16[384,3200]{1,0:T(8,128)(2,1)} %fusion.1.own_ref, bf16[384,3200]{1,0:T(8,128)(2,1)} %collective-permute-done.8.partner_ref), custom_call_target="tpu_custom_call" | custom-call | tf_op jit(solution)/shard_map/branch/pallas_call | solution.py:218
  88.5 7.1 %collective-permute-start.15 = (bf16[32,3200]{1,0:T(8,128)(2,1)}, bf16[32,3200]{1,0:T(8,128)(2,1)S(1)}, u32[]{:S(2)}, u32[]{:S(2)}) collective-permute-start(bf16[32,3200]{1,0:T(8,128)(2,1)} %get-tuple-element.74), channel_id=1, source_target_pairs={{0,4},{1,5},{2,6},{3,7},{4,0},{5,1},{6,2},{7,3},{8,12},{9,13},{10,... | collective-permute-start | bytes 614408 | tf_op jit(solution)/shard_map/ppermute | solution.py:364
  97.0 2.7 %collective-permute-start.17 = (bf16[32,3200]{1,0:T(8,128)(2,1)S(1)}, bf16[32,3200]{1,0:T(8,128)(2,1)S(1)}, u32[]{:S(2)}, u32[]{:S(2)}) collective-permute-start(bf16[32,3200]{1,0:T(8,128)(2,1)S(1)} %get-tuple-element.72), channel_id=1, source_target_pairs={{0,6},{1,7},{2,0},{3,1},{4,2},{5,3},{6,4},{7,5},{8,14},{9,15},{10,... | collective-permute-start | bytes 614408 | tf_op jit(solution)/shard_map/ppermute | solution.py:364
  99.7 6.9 %collective-permute-done.15 = bf16[32,3200]{1,0:T(8,128)(2,1)S(1)} collective-permute-done((bf16[32,3200]{1,0:T(8,128)(2,1)}, bf16[32,3200]{1,0:T(8,128)(2,1)S(1)}, u32[]{:S(2)}, u32[]{:S(2)}) %collective-permute-start.15) | collective-permute-done | bytes 204832 | tf_op jit(solution)/shard_map/ppermute | solution.py:364
  106.6 4.3 %collective-permute-done.16 = bf16[32,3200]{1,0:T(8,128)(2,1)S(1)} collective-permute-done((bf16[32,3200]{1,0:T(8,128)(2,1)S(1)}, bf16[32,3200]{1,0:T(8,128)(2,1)S(1)}, u32[]{:S(2)}, u32[]{:S(2)}) %collective-permute-start.16) | collective-permute-done | bytes 204832 | tf_op jit(solution)/shard_map/ppermute | solution.py:364
  110.9 3.3 %collective-permute-done.17 = bf16[32,3200]{1,0:T(8,128)(2,1)S(1)} collective-permute-done((bf16[32,3200]{1,0:T(8,128)(2,1)S(1)}, bf16[32,3200]{1,0:T(8,128)(2,1)S(1)}, u32[]{:S(2)}, u32[]{:S(2)}) %collective-permute-start.17) | collective-permute-done | bytes 204832 | tf_op jit(solution)/shard_map/ppermute | solution.py:364
  114.3 2.9 %collective-permute-start.18 = (bf16[32,3200]{1,0:T(8,128)(2,1)S(1)}, bf16[32,3200]{1,0:T(8,128)(2,1)S(1)}, u32[]{:S(2)}, u32[]{:S(2)}) collective-permute-start(bf16[32,3200]{1,0:T(8,128)(2,1)S(1)} %add_convert_fusion.refs_6_), channel_id=1, source_target_pairs={{0,7},{1,0},{2,1},{3,2},{4,3},{5,4},{6,5},{7,6},{8,15},{9,8},{10,9... | collective-permute-start | bytes 614408 | tf_op jit(solution)/shard_map/ppermute | solution.py:364
  117.2 2.8 %collective-permute-start.20 = (bf16[32,3200]{1,0:T(8,128)(2,1)S(1)}, bf16[32,3200]{1,0:T(8,128)(2,1)S(1)}, u32[]{:S(2)}, u32[]{:S(2)}) collective-permute-start(bf16[32,3200]{1,0:T(8,128)(2,1)S(1)} %add_convert_fusion.refs_6_), channel_id=1, source_target_pairs={{0,6},{1,7},{2,0},{3,1},{4,2},{5,3},{6,4},{7,5},{8,14},{9,15},{10,... | collective-permute-start | bytes 614408 | tf_op jit(solution)/shard_map/ppermute | solution.py:364
  120.5 3.3 %collective-permute-done.18.refs_9_ = bf16[32,3200]{1,0:T(8,128)(2,1)S(1)} collective-permute-done((bf16[32,3200]{1,0:T(8,128)(2,1)S(1)}, bf16[32,3200]{1,0:T(8,128)(2,1)S(1)}, u32[]{:S(2)}, u32[]{:S(2)}) %collective-permute-start.18) | collective-permute-done | bytes 204832 | tf_op jit(solution)/shard_map/ppermute | solution.py:364
  123.8 4.6 %collective-permute-done.19.refs_12_ = bf16[32,3200]{1,0:T(8,128)(2,1)S(1)} collective-permute-done((bf16[32,3200]{1,0:T(8,128)(2,1)S(1)}, bf16[32,3200]{1,0:T(8,128)(2,1)S(1)}, u32[]{:S(2)}, u32[]{:S(2)}) %collective-permute-start.19) | collective-permute-done | bytes 204832 | tf_op jit(solution)/shard_map/ppermute | solution.py:364
  129.5 3.9 %collective-permute-done.21.refs_18_ = bf16[32,3200]{1,0:T(8,128)(2,1)S(1)} collective-permute-done((bf16[32,3200]{1,0:T(8,128)(2,1)S(1)}, bf16[32,3200]{1,0:T(8,128)(2,1)S(1)}, u32[]{:S(2)}, u32[]{:S(2)}) %collective-permute-start.21) | collective-permute-done | bytes 204832 | tf_op jit(solution)/shard_map/ppermute | solution.py:364
  139.7 2.3 %all-gather.5.cloned.1.call-done.refs_3_ = bf16[3072,2048]{1,0:T(8,128)(2,1)} async-done(((bf16[96,2048]{1,0:T(8,128)(2,1)}), bf16[3072,2048]{1,0:T(8,128)(2,1)}) %all-gather.5.cloned.1.call-update) | async-done | bytes 12582928 | tf_op jit(solution)/shard_map/all_gather | solution.py:472
  142.0 14.1 %score.2 = f32[8,320]{1,0:T(8,128)S(1)} custom-call(s32[6]{0:T(128)S(1)} %stack.67.refs_0_, bf16[16,3072]{1,0:T(8,128)(2,1)S(1)} %copy-done.2, bf16[1,3072]{1,0:T(2,128)(2,1)S(1)} %broadcast_in_dim.43.refs_2_, bf16[3072,2048]{1,0:T(8,128)(2,1)} %all-gather.5.cloned.1.call-done.refs_3_, bf16[256,3072]{1,0:T(8,128)(2,1)S(1)} %copy-done, ...), custom_call_target="tpu_custom_call" | custom-call | flops 4026531840 | bytes 12582912 | tf_op jit(solution)/shard_map/score/pallas_call | solution.py:330
  156.1 11.8 %score.3 = f32[8,192]{1,0:T(8,128)S(1)} custom-call(s32[5]{0:T(128)S(1)} %stack.72.refs_0_, bf16[16,3072]{1,0:T(8,128)(2,1)S(1)} %copy-done.2, bf16[1,3072]{1,0:T(2,128)(2,1)S(1)} %broadcast_in_dim.43.refs_2_, bf16[3072,2048]{1,0:T(8,128)(2,1)} %all-gather.5.cloned.1.call-done.refs_3_, bf16[256,3072]{1,0:T(8,128)(2,1)S(1)} %copy-done, ...), custom_call_target="tpu_custom_call" | custom-call | flops 2415919104 | bytes 12582912 | tf_op jit(solution)/shard_map/score/pallas_call | solution.py:330
  168.5 16.3 %all_to_all.5 = f32[8,8,512]{2,1,0:T(8,128)S(1)} all-to-all(f32[8,8,512]{2,1,0:T(8,128)S(1)} %broadcast_in_dim.46), channel_id=1, replica_groups=mesh['seq'=32,'tensor'=8] {'tensor'}, dimensions={0} | all-to-all | bytes 262144 | tf_op jit(solution)/shard_map/all_to_all | solution.py:529
  (104 shorter events, 25.8 us)
Async XLA Ops:
  7.2 64.6 %all-gather.3.cloned.1.call-start = ((), (), s32[]{:S(2)}) async-start(), calls=%async_computation.1 | async-start | bytes 6488064 | tf_op jit(solution)/shard_map/all_gather | solution.py:448
  7.9 134.1 %all-gather.5.cloned.1.call-start = ((), (), s32[]{:S(2)}) async-start(), calls=%async_computation.2 | async-start | bytes 12976128 | tf_op jit(solution)/shard_map/all_gather | solution.py:472
  12.2 55.6 %collective-permute-start.8 = (bf16[384,3200]{1,0:T(8,128)(2,1)}, bf16[384,3200]{1,0:T(8,128)(2,1)}, u32[]{:S(2)}, u32[]{:S(2)}) collective-permute-start(bf16[384,3200]{1,0:T(8,128)(2,1)} %fusion.1.own_ref), channel_id=1, source_target_pairs={{0,1},{1,0},{2,3},{3,2},{4,5},{5,4},{6,7},{7,6},{8,9},{9,8},{10,11... | collective-permute-start | bytes 7372808 | tf_op jit(solution)/shard_map/ppermute | solution.py:368
  14.2 1.4 collective-permute-start
  15.6 8.2 %collective-permute-start.1 = (bf16[2,128,384]{2,1,0:T(8,128)(2,1)S(1)}, bf16[2,128,384]{2,1,0:T(8,128)(2,1)S(1)}, u32[]{:S(2)}, u32[]{:S(2)}) collective-permute-start(bf16[2,128,384]{2,1,0:T(8,128)(2,1)S(1)} %pad_maximum_fusion.1), channel_id=1, source_target_pairs={{0,48},{8,200},{16,0},{24,216},{32,16},{40,232},{48,32},{56,248},{... | collective-permute-start | bytes 589832 | tf_op jit(solution)/shard_map/ppermute | solution.py:399
  18.4 7.3 %collective-permute-start.2 = (bf16[2,128,384]{2,1,0:T(8,128)(2,1)S(1)}, bf16[2,128,384]{2,1,0:T(8,128)(2,1)S(1)}, u32[]{:S(2)}, u32[]{:S(2)}) collective-permute-start(bf16[2,128,384]{2,1,0:T(8,128)(2,1)S(1)} %pad_maximum_fusion.1), channel_id=1, source_target_pairs={{0,32},{8,136},{16,48},{24,152},{32,0},{40,168},{48,16},{56,184},{... | collective-permute-start | bytes 589832 | tf_op jit(solution)/shard_map/ppermute | solution.py:399
  19.2 8.5 %collective-permute-start.3 = (bf16[2,128,384]{2,1,0:T(8,128)(2,1)S(1)}, bf16[2,128,384]{2,1,0:T(8,128)(2,1)S(1)}, u32[]{:S(2)}, u32[]{:S(2)}) collective-permute-start(bf16[2,128,384]{2,1,0:T(8,128)(2,1)S(1)} %pad_maximum_fusion.1), channel_id=1, source_target_pairs={{0,16},{8,72},{16,32},{24,88},{32,48},{40,104},{48,0},{56,120},{64... | collective-permute-start | bytes 589832 | tf_op jit(solution)/shard_map/ppermute | solution.py:399
  27.8 14.9 %collective-permute-start.4 = (bf16[8,128,384]{2,1,0:T(8,128)(2,1)S(1)}, bf16[8,128,384]{2,1,0:T(8,128)(2,1)}, u32[]{:S(2)}, u32[]{:S(2)}) collective-permute-start(bf16[8,128,384]{2,1,0:T(8,128)(2,1)S(1)} %pad_maximum_fusion.refs_6_), channel_id=1, source_target_pairs={{0,192},{8,56},{16,208},{24,8},{32,224},{40,24},{48,240},{56,40},{... | collective-permute-start | bytes 2359304 | tf_op jit(solution)/shard_map/ppermute | solution.py:399
  28.7 14.1 %collective-permute-start.5 = (bf16[8,128,384]{2,1,0:T(8,128)(2,1)S(1)}, bf16[8,128,384]{2,1,0:T(8,128)(2,1)}, u32[]{:S(2)}, u32[]{:S(2)}) collective-permute-start(bf16[8,128,384]{2,1,0:T(8,128)(2,1)S(1)} %pad_maximum_fusion.refs_6_), channel_id=1, source_target_pairs={{0,64},{8,24},{16,80},{24,40},{32,96},{40,56},{48,112},{56,8},{64,... | collective-permute-start | bytes 2359304 | tf_op jit(solution)/shard_map/ppermute | solution.py:399
  35.9 36.1 %copy-start.4 = (s32[64]{0:T(128)S(1)}, s32[64]{0:T(128)}, u32[]{:S(2)}) copy-start(s32[64]{0:T(128)} %refs_2_.1) | copy-start | bytes 772
  43.8 12.9 %collective-permute-start.6 = (bf16[4,128,384]{2,1,0:T(8,128)(2,1)S(1)}, bf16[4,128,384]{2,1,0:T(8,128)(2,1)S(1)}, u32[]{:S(2)}, u32[]{:S(2)}) collective-permute-start(bf16[4,128,384]{2,1,0:T(8,128)(2,1)S(1)} %slice.51), channel_id=1, source_target_pairs={{0,64},{8,24},{16,80},{24,40},{32,96},{40,56},{48,112},{56,8},{64,... | collective-permute-start | bytes 1179656 | tf_op jit(solution)/shard_map/ppermute | solution.py:399
  47.7 15.8 %collective-permute-start.7 = (bf16[4,128,384]{2,1,0:T(8,128)(2,1)S(1)}, bf16[4,128,384]{2,1,0:T(8,128)(2,1)S(1)}, u32[]{:S(2)}, u32[]{:S(2)}) collective-permute-start(bf16[4,128,384]{2,1,0:T(8,128)(2,1)S(1)} %slice.52), channel_id=1, source_target_pairs={{0,192},{8,56},{16,208},{24,8},{32,224},{40,24},{48,240},{56,40},{... | collective-permute-start | bytes 1179656 | tf_op jit(solution)/shard_map/ppermute | solution.py:399
  47.8 20.5 %collective-permute-start.9 = (bf16[8,128,384]{2,1,0:T(8,128)(2,1)S(1)}, bf16[8,128,384]{2,1,0:T(8,128)(2,1)S(1)}, u32[]{:S(2)}, u32[]{:S(2)}) collective-permute-start(bf16[8,128,384]{2,1,0:T(8,128)(2,1)S(1)} %pad_maximum_fusion.refs_6_), channel_id=1, source_target_pairs={{0,8},{8,0},{16,24},{24,16},{32,40},{40,32},{48,56},{56,48},{64,72... | collective-permute-start | bytes 2359304 | tf_op jit(solution)/shard_map/ppermute | solution.py:387
  47.9 21.3 %collective-permute-start.10 = (bf16[8,128,384]{2,1,0:T(8,128)(2,1)}, bf16[8,128,384]{2,1,0:T(8,128)(2,1)S(1)}, u32[]{:S(2)}, u32[]{:S(2)}) collective-permute-start(bf16[8,128,384]{2,1,0:T(8,128)(2,1)} %collective-permute-done.4.refs_7_), channel_id=1, source_target_pairs={{0,8},{8,0},{16,24},{24,16},{32,40},{40,32},{48,56},{56,48},{64,72... | collective-permute-start | bytes 2359304 | tf_op jit(solution)/shard_map/ppermute | solution.py:387
  56.7 13.4 %collective-permute-start.13 = (bf16[8,128,384]{2,1,0:T(8,128)(2,1)}, bf16[8,128,384]{2,1,0:T(8,128)(2,1)S(1)}, u32[]{:S(2)}, u32[]{:S(2)}) collective-permute-start(bf16[8,128,384]{2,1,0:T(8,128)(2,1)} %collective-permute-done.5.refs_10_), channel_id=1, source_target_pairs={{0,8},{8,0},{16,24},{24,16},{32,40},{40,32},{48,56},{56,48},{64,72... | collective-permute-start | bytes 2359304 | tf_op jit(solution)/shard_map/ppermute | solution.py:387
  67.8 3.2 %collective-permute-start.11 = (bf16[4,128,384]{2,1,0:T(8,128)(2,1)S(1)}, bf16[4,128,384]{2,1,0:T(8,128)(2,1)S(1)}, u32[]{:S(2)}, u32[]{:S(2)}) collective-permute-start(bf16[4,128,384]{2,1,0:T(8,128)(2,1)S(1)} %collective-permute-done.6.refs_8_), channel_id=1, source_target_pairs={{0,8},{8,0},{16,24},{24,16},{32,40},{40,32},{48,56},{56,48},{64,72... | collective-permute-start | bytes 1179656 | tf_op jit(solution)/shard_map/ppermute | solution.py:387
  67.8 4.0 %collective-permute-start.12 = (bf16[4,128,384]{2,1,0:T(8,128)(2,1)S(1)}, bf16[4,128,384]{2,1,0:T(8,128)(2,1)}, u32[]{:S(2)}, u32[]{:S(2)}) collective-permute-start(bf16[4,128,384]{2,1,0:T(8,128)(2,1)S(1)} %collective-permute-done.7.refs_9_), channel_id=1, source_target_pairs={{0,8},{8,0},{16,24},{24,16},{32,40},{40,32},{48,56},{56,48},{64,72... | collective-permute-start | bytes 1179656 | tf_op jit(solution)/shard_map/ppermute | solution.py:387
  77.9 5.0 %collective-permute-start.14 = (bf16[128,384]{1,0:T(8,128)(2,1)S(1)}, bf16[128,384]{1,0:T(8,128)(2,1)S(1)}, u32[]{:S(2)}, u32[]{:S(2)}) collective-permute-start(bf16[128,384]{1,0:T(8,128)(2,1)S(1)} %get-tuple-element.75), channel_id=1, source_target_pairs={{0,1},{1,0},{2,3},{3,2},{4,5},{5,4},{6,7},{7,6},{8,9},{9,8},{10,11... | collective-permute-start | bytes 294920 | tf_op jit(solution)/shard_map/ppermute | solution.py:368
  82.9 37.2 %copy-start.16 = (s32[256]{0:T(256)S(1)}, s32[256]{0:T(256)}, u32[]{:S(2)}) copy-start(s32[256]{0:T(256)} %param.27) | copy-start | bytes 3076
  87.7 32.5 %copy-start.15 = (bf16[3072]{0:T(1024)(128)(2,1)S(1)}, bf16[3072]{0:T(1024)(128)(2,1)}, u32[]{:S(2)}) copy-start(bf16[3072]{0:T(1024)(128)(2,1)} %param.20) | copy-start | bytes 18436
  87.7 54.3 %copy-start.2 = (bf16[16,3072]{1,0:T(8,128)(2,1)S(1)}, bf16[16,3072]{1,0:T(8,128)(2,1)}, u32[]{:S(2)}) copy-start(bf16[16,3072]{1,0:T(8,128)(2,1)} %refs_1_.5) | copy-start | bytes 294916
  88.5 18.1 %collective-permute-start.15 = (bf16[32,3200]{1,0:T(8,128)(2,1)}, bf16[32,3200]{1,0:T(8,128)(2,1)S(1)}, u32[]{:S(2)}, u32[]{:S(2)}) collective-permute-start(bf16[32,3200]{1,0:T(8,128)(2,1)} %get-tuple-element.74), channel_id=1, source_target_pairs={{0,4},{1,5},{2,6},{3,7},{4,0},{5,1},{6,2},{7,3},{8,12},{9,13},{10,... | collective-permute-start | bytes 614408 | tf_op jit(solution)/shard_map/ppermute | solution.py:364
  95.5 15.4 %collective-permute-start.16 = (bf16[32,3200]{1,0:T(8,128)(2,1)S(1)}, bf16[32,3200]{1,0:T(8,128)(2,1)S(1)}, u32[]{:S(2)}, u32[]{:S(2)}) collective-permute-start(bf16[32,3200]{1,0:T(8,128)(2,1)S(1)} %get-tuple-element.73), channel_id=1, source_target_pairs={{0,2},{1,3},{2,4},{3,5},{4,6},{5,7},{6,0},{7,1},{8,10},{9,11},{10,... | collective-permute-start | bytes 614408 | tf_op jit(solution)/shard_map/ppermute | solution.py:364
  97.0 17.2 %collective-permute-start.17 = (bf16[32,3200]{1,0:T(8,128)(2,1)S(1)}, bf16[32,3200]{1,0:T(8,128)(2,1)S(1)}, u32[]{:S(2)}, u32[]{:S(2)}) collective-permute-start(bf16[32,3200]{1,0:T(8,128)(2,1)S(1)} %get-tuple-element.72), channel_id=1, source_target_pairs={{0,6},{1,7},{2,0},{3,1},{4,2},{5,3},{6,4},{7,5},{8,14},{9,15},{10,... | collective-permute-start | bytes 614408 | tf_op jit(solution)/shard_map/ppermute | solution.py:364
  114.3 9.5 %collective-permute-start.18 = (bf16[32,3200]{1,0:T(8,128)(2,1)S(1)}, bf16[32,3200]{1,0:T(8,128)(2,1)S(1)}, u32[]{:S(2)}, u32[]{:S(2)}) collective-permute-start(bf16[32,3200]{1,0:T(8,128)(2,1)S(1)} %add_convert_fusion.refs_6_), channel_id=1, source_target_pairs={{0,7},{1,0},{2,1},{3,2},{4,3},{5,4},{6,5},{7,6},{8,15},{9,8},{10,9... | collective-permute-start | bytes 614408 | tf_op jit(solution)/shard_map/ppermute | solution.py:364
  117.2 11.2 %collective-permute-start.19 = (bf16[32,3200]{1,0:T(8,128)(2,1)S(1)}, bf16[32,3200]{1,0:T(8,128)(2,1)S(1)}, u32[]{:S(2)}, u32[]{:S(2)}) collective-permute-start(bf16[32,3200]{1,0:T(8,128)(2,1)S(1)} %add_convert_fusion.refs_6_), channel_id=1, source_target_pairs={{0,1},{1,2},{2,3},{3,4},{4,5},{5,6},{6,7},{7,0},{8,9},{9,10},{10,1... | collective-permute-start | bytes 614408 | tf_op jit(solution)/shard_map/ppermute | solution.py:364
  117.2 12.4 %collective-permute-start.20 = (bf16[32,3200]{1,0:T(8,128)(2,1)S(1)}, bf16[32,3200]{1,0:T(8,128)(2,1)S(1)}, u32[]{:S(2)}, u32[]{:S(2)}) collective-permute-start(bf16[32,3200]{1,0:T(8,128)(2,1)S(1)} %add_convert_fusion.refs_6_), channel_id=1, source_target_pairs={{0,6},{1,7},{2,0},{3,1},{4,2},{5,3},{6,4},{7,5},{8,14},{9,15},{10,... | collective-permute-start | bytes 614408 | tf_op jit(solution)/shard_map/ppermute | solution.py:364
  120.0 13.5 %collective-permute-start.21 = (bf16[32,3200]{1,0:T(8,128)(2,1)S(1)}, bf16[32,3200]{1,0:T(8,128)(2,1)S(1)}, u32[]{:S(2)}, u32[]{:S(2)}) collective-permute-start(bf16[32,3200]{1,0:T(8,128)(2,1)S(1)} %add_convert_fusion.refs_6_), channel_id=1, source_target_pairs={{0,2},{1,3},{2,4},{3,5},{4,6},{5,7},{6,0},{7,1},{8,10},{9,11},{10,... | collective-permute-start | bytes 614408 | tf_op jit(solution)/shard_map/ppermute | solution.py:364
  133.4 22.7 %collective-permute-start.22 = (bf16[32,3200]{1,0:T(8,128)(2,1)S(1)}, bf16[32,3200]{1,0:T(8,128)(2,1)S(1)}, u32[]{:S(2)}, u32[]{:S(2)}) collective-permute-start(bf16[32,3200]{1,0:T(8,128)(2,1)S(1)} %collective-permute-done.20.refs_15_), channel_id=1, source_target_pairs={{0,7},{1,0},{2,1},{3,2},{4,3},{5,4},{6,5},{7,6},{8,15},{9,8},{10,9... | collective-permute-start | bytes 614408 | tf_op jit(solution)/shard_map/ppermute | solution.py:364
  134.6 21.6 %collective-permute-start.23 = (bf16[32,3200]{1,0:T(8,128)(2,1)S(1)}, bf16[32,3200]{1,0:T(8,128)(2,1)S(1)}, u32[]{:S(2)}, u32[]{:S(2)}) collective-permute-start(bf16[32,3200]{1,0:T(8,128)(2,1)S(1)} %collective-permute-done.21.refs_18_), channel_id=1, source_target_pairs={{0,1},{1,2},{2,3},{3,4},{4,5},{5,6},{6,7},{7,0},{8,9},{9,10},{10,1... | collective-permute-start | bytes 614408 | tf_op jit(solution)/shard_map/ppermute | solution.py:364
  136.8 19.3 %collective-permute-start.24 = (bf16[16,3200]{1,0:T(8,128)(2,1)}, bf16[16,3200]{1,0:T(8,128)(2,1)S(1)}, u32[]{:S(2)}, u32[]{:S(2)}) collective-permute-start(bf16[16,3200]{1,0:T(8,128)(2,1)} %slice.53), channel_id=1, source_target_pairs={{0,6},{1,7},{2,0},{3,1},{4,2},{5,3},{6,4},{7,5},{8,14},{9,15},{10,... | collective-permute-start | bytes 307208 | tf_op jit(solution)/shard_map/ppermute | solution.py:364
  137.9 18.2 %collective-permute-start.25 = (bf16[16,3200]{1,0:T(8,128)(2,1)}, bf16[16,3200]{1,0:T(8,128)(2,1)S(1)}, u32[]{:S(2)}, u32[]{:S(2)}) collective-permute-start(bf16[16,3200]{1,0:T(8,128)(2,1)} %slice.54), channel_id=1, source_target_pairs={{0,2},{1,3},{2,4},{3,5},{4,6},{5,7},{6,0},{7,1},{8,10},{9,11},{10,... | collective-permute-start | bytes 307208 | tf_op jit(solution)/shard_map/ppermute | solution.py:364
  (13 other events, 120.4 us)
Sparse Core Ops, SparseCore 0:
  10.5 59.5 all-gather.2
  72.7 69.2 all-gather.4

commit v2 on v1

--- a/solution.py
+++ b/solution.py
@@ -97,10 +97,7 @@
         far = jnp.where(path == 0, down_y, down_x)
         near = jnp.where(path == 0, down_x, down_y)
         at = near * 2 + (device % 2 != path).astype(jnp.int32)
-        high = ((far == 2) & (at >= 4)).astype(jnp.int32)
-        piece = far + high + (far == 3).astype(jnp.int32)
-        piece = piece + 5 * (my_core != path).astype(jnp.int32)
-        at = at - 4 * high
+        piece = far + 4 * (my_core != path).astype(jnp.int32)
         rows = pl.ds(pl.multiple_of(j * PAGE, PAGE), PAGE)
         pltpu.make_async_copy(
             cached_values_ref.at[slot], values.at[r, rows], sems.at[r, 1, j]
@@ -109,8 +106,7 @@
 
             @pl.when(piece == p)
             def _():
-                row = jnp.minimum(at, ref.shape[0] - 1)
-                pltpu.make_async_copy(ref.at[row], keys.at[r, rows], sems.at[r, 0, j]).start()
+                pltpu.make_async_copy(ref.at[at], keys.at[r, rows], sems.at[r, 0, j]).start()
 
         return 0
 
@@ -201,152 +197,158 @@
     )(first, counts, index, owner, qkv, *cached)
 
 
-def branch_kernel(mine_ref, theirs_ref, own_ref, partner_ref, out_ref):
-    out_ref[...] = (
-        jnp.dot(mine_ref[...], own_ref[...], preferred_element_type=F32)
-        + jnp.dot(theirs_ref[...], partner_ref[...], preferred_element_type=F32)
-    ).astype(BF16)
-
-
-def branch_part(mine, theirs, own, partner):
-    rows, width = mine.shape
-    columns = own.shape[1]
-    tile = columns // 5
-    own, partner = (pltpu.with_memory_space_constraint(w, pltpu.HBM) for w in (own, partner))
-    whole = lambda i: (0, 0)
-    across = lambda i: (0, i)
-    return pl.pallas_call(
-        branch_kernel,
-        grid=(columns // tile,),
-        in_specs=[pl.BlockSpec((rows, width), whole)] * 2
-        + [pl.BlockSpec((width, tile), across)] * 2,
-        out_specs=pl.BlockSpec((rows, tile), across),
-        out_shape=jax.ShapeDtypeStruct((rows, columns), BF16),
-        compiler_params=pltpu.CompilerParams(vmem_limit_bytes=VMEM_LIMIT),
-        name="branch",
-    )(mine, theirs, own, partner)
-
-
 def two_parts(value):
     high = value.astype(BF16)
     return high, (value - high.astype(F32)).astype(BF16)
 
 
+def settle_kernel(place_ref, hidden_ref, up_ref, gain_ref, *refs):
+    *parts, out_ref = refs
+    model = hidden_ref.shape[1]
+    rank = up_ref.shape[0]
+    total = parts[0][...].astype(F32)
+    for part in parts[1:]:
+        total = total + part[...].astype(F32)
+    reference = hidden_ref[...].astype(F32) + total[:, :model]
+    delta = total[:, model:]
+    high, low = two_parts(delta)
+    policy = (
+        reference
+        + jnp.dot(high[:, :rank], up_ref[...], preferred_element_type=F32)
+        + jnp.dot(low[:, :rank], up_ref[...], preferred_element_type=F32)
+    )
+    reference_scale = lax.rsqrt(jnp.mean(reference * reference, axis=1, keepdims=True) + EPSILON)
+    policy_scale = lax.rsqrt(jnp.mean(policy * policy, axis=1, keepdims=True) + EPSILON)
+    out_ref[:, :model] = (reference * reference_scale * gain_ref[...].astype(F32)).astype(BF16)
+    lane = lax.broadcasted_iota(jnp.int32, delta.shape, 1)
+    beside = high.astype(F32) + pltpu.roll(low.astype(F32), rank, 1)
+    at = 2 * rank
+    for scale in (policy_scale / reference_scale, policy_scale):
+        for _ in range(3):
+            part = scale.astype(BF16).astype(F32)
+            beside = jnp.where(lane == at, part, beside)
+            scale = scale - part
+            at += 1
+    out_ref[:, model:] = beside.astype(BF16)
+
+
+def settle(place, hidden, up, gain, *parts):
+    whole = lambda i, p: (0, 0)
+    size, width = parts[0].shape
+    return pl.pallas_call(
+        settle_kernel,
+        grid_spec=pltpu.PrefetchScalarGridSpec(
+            num_scalar_prefetch=1,
+            grid=(1,),
+            in_specs=[
+                pl.BlockSpec((size, hidden.shape[1]), lambda i, p: (p[0], 0)),
+                pl.BlockSpec(up.shape, whole),
+                pl.BlockSpec(gain.shape, whole),
+            ]
+            + [pl.BlockSpec(part.shape, whole) for part in parts],
+            out_specs=pl.BlockSpec((size, width), whole),
+        ),
+        out_shape=jax.ShapeDtypeStruct((size, width), BF16),
+        compiler_params=pltpu.CompilerParams(vmem_limit_bytes=VMEM_LIMIT),
+        name="settle",
+    )(place, hidden, up, gain, *parts)
+
+
 def score_kernel(*refs):
     place_ref, up_ref, gain_ref, head_ref = refs[:4]
-    out_ref, normed, deltas, scales, wanted, logits, adapters, packed = refs[-8:]
+    out_ref, normed, deltas, scales, wanted, largest, total, picked = refs[-8:]
     inputs = refs[4:-8]
     step = pl.program_id(0)
-    steps, _, depth = normed.shape
     rank, model = up_ref.shape
     rows = deltas.shape[0]
-    vocab = head_ref.shape[1]
-
-    def store_normed(at, value):
-        for k in range(steps):
-            normed[k, at, :] = value[:, k * depth : (k + 1) * depth]
+    tile = head_ref.shape[1]
 
     @pl.when(step == 0)
     def _():
         start = 0
-        gain = gain_ref[...].astype(F32)
-        up = up_ref[...]
-        for hidden_ref, target_ref, block in zip(inputs[::3], inputs[1::3], inputs[2::3]):
+        for target_ref, block in zip(inputs[::2], inputs[1::2]):
             at = slice(start, start + block.shape[0])
             start += block.shape[0]
-            delta = block[:, model : model + rank]
-            reference = hidden_ref[...].astype(F32) + block[:, :model].astype(F32)
-            policy = reference + jnp.dot(delta, up, preferred_element_type=F32)
-            reference_scale = lax.rsqrt(
-                jnp.mean(reference * reference, axis=1, keepdims=True) + EPSILON
-            )
-            policy_scale = lax.rsqrt(jnp.mean(policy * policy, axis=1, keepdims=True) + EPSILON)
-            store_normed(at, (reference * reference_scale * gain).astype(BF16))
-            deltas[at, :] = jnp.concatenate([delta, delta], axis=1)
-            scales[0, at, :] = policy_scale / reference_scale
-            scales[1, at, :] = policy_scale
-            wanted[at, :] = target_ref[...] - place_ref[0] * vocab
-        high, low = two_parts(up.astype(F32) * gain)
-        store_normed(slice(rows, rows + rank), high)
-        store_normed(slice(rows + rank, rows + 2 * rank), low)
-        logits[...] = jnp.zeros_like(logits)
-
-    tile = 256
-
-    def multiply(n, _):
-        columns = pl.ds(pl.multiple_of(n * tile, tile), tile)
-        logits[:, columns] += jnp.dot(
-            normed[step], head_ref[:, columns], preferred_element_type=F32
+            normed[at, :] = block[:, :model]
+            beside = block[:, model:]
+            deltas[at, :] = beside[:, : 2 * rank]
+            beside = beside.astype(F32)
+            lane = lax.broadcasted_iota(jnp.int32, beside.shape, 1) - 2 * rank
+            for which in range(2):
+                parts = (lane >= 3 * which) & (lane < 3 * which + 3)
+                scales[which, at, :] = jnp.sum(
+                    jnp.where(parts, beside, 0.0), axis=1, keepdims=True
+                )
+            wanted[at, :] = target_ref[...] - place_ref[0] * pl.num_programs(0) * tile
+        high, low = two_parts(up_ref[...].astype(F32) * gain_ref[...].astype(F32))
+        normed[rows : rows + rank, :] = high
+        normed[rows + rank :, :] = low
+        largest[...] = jnp.full_like(largest, NEGATIVE)
+        total[...] = jnp.zeros_like(total)
+        picked[...] = jnp.zeros_like(picked)
+
+    product = jnp.dot(normed[...], head_ref[...], preferred_element_type=F32)
+    reference_logits = product[:rows]
+    adapted = jnp.zeros_like(reference_logits)
+    for part in two_parts(product[rows : rows + rank] + product[rows + rank :]):
+        adapted += jnp.dot(
+            deltas[...], jnp.concatenate([part, part], axis=0), preferred_element_type=F32
         )
-        return 0
-
-    lax.fori_loop(0, vocab // tile, multiply, 0)
-
-    @pl.when(step == steps - 1)
+    policy_logits = scales[0] * reference_logits + scales[1] * adapted
+    columns = lax.broadcasted_iota(jnp.int32, reference_logits.shape, 1)
+    hit = columns == wanted[...] - step * tile
+    for which, logits in enumerate((policy_logits, reference_logits)):
+        picked[which] += jnp.sum(jnp.where(hit, logits, 0.0), axis=1, keepdims=True)
+        before = largest[which]
+        after = jnp.maximum(before, jnp.max(logits, axis=1, keepdims=True))
+        total[which] = total[which] * jnp.exp(before - after) + jnp.sum(
+            jnp.exp(logits - after), axis=1, keepdims=True
+        )
+        largest[which] = after
+
+    @pl.when(step == pl.num_programs(0) - 1)
     def _():
-        high, low = two_parts(logits[rows : rows + rank, :] + logits[rows + rank :, :])
-        adapters[:rank, :] = high
-        adapters[rank:, :] = low
-        size = 32
-
-        def summarize(n, _):
-            at = pl.ds(pl.multiple_of(n * size, size), size)
-            reference_logits = logits[at, :]
-            adapted = jnp.dot(deltas[at, :], adapters[...], preferred_element_type=F32)
-            policy_logits = scales[0, at, :] * reference_logits + scales[1, at, :] * adapted
-            hit = lax.broadcasted_iota(jnp.int32, (size, vocab), 1) == wanted[at, :]
-            lane = lax.broadcasted_iota(jnp.int32, (size, 128), 1)
-            for which, here in enumerate((policy_logits, reference_logits)):
-                picked = jnp.sum(jnp.where(hit, here, 0.0), axis=1, keepdims=True)
-                largest = jnp.max(here, axis=1, keepdims=True)
-                total = jnp.sum(jnp.exp(here - largest), axis=1, keepdims=True)
-                packed[which, at, :] = jnp.where(
-                    lane == 0, largest, jnp.where(lane == 1, total, picked)
-                )
-            return 0
-
-        lax.fori_loop(0, rows // size, summarize, 0)
-        out_ref[...] = jnp.transpose(packed[...].reshape(2 * rows, 128))[:8, :]
-
-
-def score(place, hidden, up, gain, targets, head, blocks):
-    model = hidden.shape[1]
+        lane = lax.broadcasted_iota(jnp.int32, (2, rows, 128), 2)
+        packed = jnp.where(
+            lane == 0, largest[...], jnp.where(lane == 1, total[...], picked[...])
+        )
+        out_ref[...] = jnp.transpose(packed.reshape(2 * rows, 128))[:8, :]
+
+
+def score(place, up, gain, targets, head, blocks):
+    rank, model = up.shape
     vocab = head.shape[1]
-    rank = up.shape[0]
     rows = sum(block.shape[0] for block in blocks)
-    steps = 4
-    depth = model // steps
+    tile = 512
     whole = lambda i, p: (0, 0)
     per_block, operands = [], []
     for k, block in enumerate(blocks):
-        size = block.shape[0]
-        here = lambda i, p, k=k: (p[1 + k], 0)
         per_block += [
-            pl.BlockSpec((size, model), here),
-            pl.BlockSpec((size, 1), here),
+            pl.BlockSpec((block.shape[0], 1), lambda i, p, k=k: (p[1 + k], 0)),
             pl.BlockSpec(block.shape, whole),
         ]
-        operands += [hidden, targets, block]
+        operands += [targets, block]
+    column = pltpu.VMEM((2, rows, 1), F32)
     return pl.pallas_call(
         score_kernel,
         grid_spec=pltpu.PrefetchScalarGridSpec(
             num_scalar_prefetch=1,
-            grid=(steps,),
+            grid=(vocab // tile,),
             in_specs=[
                 pl.BlockSpec(up.shape, whole),
                 pl.BlockSpec(gain.shape, whole),
-                pl.BlockSpec((depth, vocab), lambda i, p: (i, 0)),
+                pl.BlockSpec((model, tile), lambda i, p: (0, i)),
             ]
             + per_block,
             out_specs=pl.BlockSpec((8, 2 * rows), whole),
             scratch_shapes=[
-                pltpu.VMEM((steps, rows + 2 * rank, depth), BF16),
+                pltpu.VMEM((rows + 2 * rank, model), BF16),
                 pltpu.VMEM((rows, 2 * rank), BF16),
-                pltpu.VMEM((2, rows, 1), F32),
+                column,
                 pltpu.VMEM((rows, 1), jnp.int32),
-                pltpu.VMEM((rows + 2 * rank, vocab), F32),
-                pltpu.VMEM((2 * rank, vocab), BF16),
-                pltpu.VMEM((2, rows, 128), F32),
+                column,
+                column,
+                column,
             ],
         ),
         out_shape=jax.ShapeDtypeStruct((8, 2 * rows), F32),
@@ -377,10 +379,7 @@
         return lax.dynamic_slice_in_dim(branch, at, size, 0)
 
     arrived = [shifted(block(step), ranks, step) for step in (ranks // 2, 2, ranks - 2)]
-    total = block(0).astype(F32)
-    for value in lax.optimization_barrier(arrived):
-        total = total + value.astype(F32)
-    return total.astype(BF16)
+    return [block(0)] + list(lax.optimization_barrier(arrived))
 
 
 def crossed(value):
@@ -407,15 +406,10 @@
     partner = partnered(weights, ranks)
     line = lax.optimization_barrier([pair] + [turned(pair, 0, step) for step in (3, 2, 1)])
     line = lax.optimization_barrier(jnp.concatenate(line))
-    front, behind = turned(line, 1, 3), turned(line, 1, 1)
+    ahead = [turned(line, 1, step) for step in (3, 2, 1)]
     near = crossed(line)
-    front, behind, qkv = lax.optimization_barrier((front, behind, project_now()))
-    middle = front.shape[0] // 2
-    low, high = turned(behind[:middle], 1, 1), turned(front[middle:], 1, 3)
-    far_front, far_behind = crossed(front), crossed(behind)
-    low, high, partner = lax.optimization_barrier((low, high, partner))
-    pieces = [line, front, low, high, behind]
-    pieces += [near, far_front, crossed(low), crossed(high), far_behind]
+    ahead, qkv = lax.optimization_barrier((ahead, project_now()))
+    pieces = [line] + ahead + [near] + [crossed(piece) for piece in ahead]
     return pieces, partner, qkv
 
 
@@ -468,7 +462,9 @@
         ),
         ranks,
     )
-    head_rows, cached_values, pieces = lax.optimization_barrier((head.T, cached_values, pieces))
+    head_rows, cached_values, pieces, partner_weights = lax.optimization_barrier(
+        (head.T, cached_values, pieces, partner_weights)
+    )
     head_columns = lax.all_gather(head_rows, "seq", axis=0, tiled=True)
     attended = attend(
         jnp.stack([first, me // 8, me // 2 % 4, me % 2]).astype(jnp.int32),
@@ -479,13 +475,18 @@
         cached_values,
         pieces,
     )
-    branch = branch_part(
-        lax.dynamic_index_in_dim(attended, rank % 2, 0, False),
-        partnered(lax.dynamic_index_in_dim(attended, 1 - rank % 2, 0, False), ranks),
-        weights,
-        partner_weights,
-    )
-    mine = reduce_rows(branch, ranks)
+    theirs = partnered(lax.dynamic_index_in_dim(attended, 1 - rank % 2, 0, False), ranks)
+    own = lax.dynamic_index_in_dim(attended, rank % 2, 0, False)
+    branch = jnp.dot(own, weights, preferred_element_type=F32)
+    branch = branch + jnp.dot(theirs, partner_weights, preferred_element_type=F32)
+    branch = branch.astype(BF16)
+    mine = settle(
+        rank[None].astype(jnp.int32),
+        hidden,
+        adapter_up_weight,
+        final_norm_gain[None, :],
+        *reduce_rows(branch, ranks),
+    )
     size = tok_rows // ranks
     half = size // 2
     head_columns = pltpu.with_memory_space_constraint(head_columns, pltpu.HBM)
@@ -493,7 +494,6 @@
     def score_blocks(places, blocks):
         return score(
             jnp.stack([rank] + places).astype(jnp.int32),
-            hidden,
             adapter_up_weight,
             final_norm_gain[None, :],
             targets[:, None],

time: 193 us -> 191 us (0.990)
  waiting for transfers between devices: 64 us -> 80.1 us
  Pallas kernels: 41.1 us -> 27.6 us
  starting transfers between devices: 37.7 us -> 33.6 us
  local copies, waits for them, and re-layouts: 13.2 us -> 9.31 us
  matrix products: 0 us -> 2.96 us
    all_gather x1, waiting for transfers between devices: 0.01 us -> 10.7 us  [local(): lax.all_gather(prompt_value_slots, 'seq', axis=0, tiled=True)]
    pallas_call x2, Pallas kernels: 25.9 us -> 16.9 us  [score(): pl.pallas_call(score_kernel, grid_spec=pltpu.PrefetchScalarGridSpec(num_s...]
    ppermute x7 -> x6, waiting for transfers between devices: 24.7 us -> 17.7 us  [turned(): return lax.ppermute(value, 'seq', [(i, target(i)) for i in range(32)])]
    ppermute x2, waiting for transfers between devices: 7.51 us -> 13.3 us  [partnered(): return lax.ppermute(value, 'tensor', [(i, i ^ 1) for i in range(ranks)])]
    all_gather x1, waiting for transfers between devices: 2.34 us -> 7.4 us  [local(): head_columns = lax.all_gather(head_rows, 'seq', axis=0, tiled=True)]
    pallas_call x1, Pallas kernels: 4.8 us -> 0.42 us  [settle(): pl.pallas_call(settle_kernel, grid_spec=pltpu.PrefetchScalarGridSpec(num_...]
    dot_general x0 -> x2, matrix products: none -> 2.96 us  [the longest x1 2.34 us: local(): jnp.dot(theirs, partner_weights, preferred_element_type=F32)]
    ppermute x7 -> x6, starting transfers between devices: 10.7 us -> 8.46 us  [turned(): return lax.ppermute(value, 'seq', [(i, target(i)) for i in range(32)])]
  transfers between devices with their start and end apart: 28 -> 26, of which waited for: 17 -> 20; matrix products, arithmetic and copies ran while one was open for 6% -> 5% of each run, Pallas kernels for 15% -> 10%
where the time goes in v2:
time: 191 us; the launch traced here: 190 us
  waiting for transfers between devices  80.1 us (42%)
  starting transfers between devices  33.6 us (18%)
  Pallas kernels  27.6 us (14%)
  blocking collectives  16.3 us (9%)
  between operations  14.6 us (8%)
  local copies, waits for them, and re-layouts  9.31 us (5%)
  other arithmetic  5.36 us (3%)
  matrix products  2.96 us (2%)
    ppermute x11, waiting for transfers between devices, shifted(): lax.ppermute(value, 'tensor', [(i, (i + step) % ranks) for i in range(ran...  27.4 us
    ppermute x11, starting transfers between devices, shifted(): lax.ppermute(value, 'tensor', [(i, (i + step) % ranks) for i in range(ran...  20.8 us
    ppermute x6, waiting for transfers between devices, turned(): return lax.ppermute(value, 'seq', [(i, target(i)) for i in range(32)])  17.7 us
    pallas_call x2, Pallas kernels, score(): pl.pallas_call(score_kernel, grid_spec=pltpu.PrefetchScalarGridSpec(num_s...  16.9 us
    all_to_all x1, blocking collectives, local(): lax.all_to_all(jnp.broadcast_to(ordered[None], (ranks, 8, 2 * tok_rows)),...  16.3 us
    ppermute x2, waiting for transfers between devices, partnered(): return lax.ppermute(value, 'tensor', [(i, i ^ 1) for i in range(ranks)])  13.3 us
    all_gather x1, waiting for transfers between devices, local(): lax.all_gather(prompt_value_slots, 'seq', axis=0, tiled=True)  10.7 us
    ppermute x6, starting transfers between devices, turned(): return lax.ppermute(value, 'seq', [(i, target(i)) for i in range(32)])  8.46 us
  transfers between devices with their start and end apart: 26, of which 20 were waited for; matrix products, arithmetic and copies ran while one was open for 5% of the time, Pallas kernels for 10%

profile of v2, /device:TPU:24, one launch (start us, length us, event | category | flops | bytes accessed | tf_op | source)
XLA Modules:
  0.0 189.7 jit_solution(17204252518721919456)
XLA Ops:
  8.8 3.4 %fusion.2 = bf16[384,3200]{1,0:T(8,128)(2,1)} fusion(bf16[384,16]{1,0:T(8,128)(2,1)S(1)} %copy.65, bf16[384,3072]{1,0:T(8,128)(2,1)} %param.17), kind=kLoop, calls=%fused_computation.4 | loop fusion | flops 7372800 | bytes 4829184 | tf_op jit(solution)/shard_map/concatenate | solution.py:441
  12.2 1.9 %collective-permute-start.11 = (bf16[384,3200]{1,0:T(8,128)(2,1)}, bf16[384,3200]{1,0:T(8,128)(2,1)}, u32[]{:S(2)}, u32[]{:S(2)}) collective-permute-start(bf16[384,3200]{1,0:T(8,128)(2,1)} %fusion.2), channel_id=1, source_target_pairs={{0,1},{1,0},{2,3},{3,2},{4,5},{5,4},{6,7},{7,6},{8,9},{9,8},{10,11... | collective-permute-start | bytes 7372808 | tf_op jit(solution)/shard_map/ppermute | solution.py:370
  15.6 2.8 %collective-permute-start.1 = (bf16[2,128,384]{2,1,0:T(8,128)(2,1)S(1)}, bf16[2,128,384]{2,1,0:T(8,128)(2,1)S(1)}, u32[]{:S(2)}, u32[]{:S(2)}) collective-permute-start(bf16[2,128,384]{2,1,0:T(8,128)(2,1)S(1)} %pad_maximum_fusion.1), channel_id=1, source_target_pairs={{0,48},{8,200},{16,0},{24,216},{32,16},{40,232},{48,32},{56,248},{... | collective-permute-start | bytes 589832 | tf_op jit(solution)/shard_map/ppermute | solution.py:398
  20.4 3.4 %collective-permute-done.1 = bf16[2,128,384]{2,1,0:T(8,128)(2,1)S(1)} collective-permute-done((bf16[2,128,384]{2,1,0:T(8,128)(2,1)S(1)}, bf16[2,128,384]{2,1,0:T(8,128)(2,1)S(1)}, u32[]{:S(2)}, u32[]{:S(2)}) %collective-permute-start.1) | collective-permute-done | bytes 196640 | tf_op jit(solution)/shard_map/ppermute | solution.py:398
  23.7 1.9 %collective-permute-done.2 = bf16[2,128,384]{2,1,0:T(8,128)(2,1)S(1)} collective-permute-done((bf16[2,128,384]{2,1,0:T(8,128)(2,1)S(1)}, bf16[2,128,384]{2,1,0:T(8,128)(2,1)S(1)}, u32[]{:S(2)}, u32[]{:S(2)}) %collective-permute-start.2) | collective-permute-done | bytes 196640 | tf_op jit(solution)/shard_map/ppermute | solution.py:398
  25.7 2.0 %collective-permute-done.3 = bf16[2,128,384]{2,1,0:T(8,128)(2,1)S(1)} collective-permute-done((bf16[2,128,384]{2,1,0:T(8,128)(2,1)S(1)}, bf16[2,128,384]{2,1,0:T(8,128)(2,1)S(1)}, u32[]{:S(2)}, u32[]{:S(2)}) %collective-permute-start.3) | collective-permute-done | bytes 196640 | tf_op jit(solution)/shard_map/ppermute | solution.py:398
  29.6 2.2 %collective-permute-start.6 = (bf16[8,128,384]{2,1,0:T(8,128)(2,1)S(1)}, bf16[8,128,384]{2,1,0:T(8,128)(2,1)}, u32[]{:S(2)}, u32[]{:S(2)}) collective-permute-start(bf16[8,128,384]{2,1,0:T(8,128)(2,1)S(1)} %pad_maximum_fusion.refs_6_), channel_id=1, source_target_pairs={{0,64},{8,24},{16,80},{24,40},{32,96},{40,56},{48,112},{56,8},{64,... | collective-permute-start | bytes 2359304 | tf_op jit(solution)/shard_map/ppermute | solution.py:398
  33.5 3.0 %copy-done = bf16[3,3072,384]{2,1,0:T(8,128)(2,1)S(1)} copy-done((bf16[3,3072,384]{2,1,0:T(8,128)(2,1)S(1)}, bf16[3,3072,384]{2,1,0:T(8,128)(2,1)}, u32[]{:S(2)}) %copy-start) | copy-done | bytes 7077912
  36.5 4.6 %project.1.refs_4_ = bf16[3,256,384]{2,1,0:T(8,128)(2,1)S(1)} custom-call(bf16[256,3072]{1,0:T(8,128)(2,1)S(1)} %copy-done.1, bf16[1,3072]{1,0:T(2,128)(2,1)S(1)} %broadcast_in_dim.45.gain_ref, bf16[3,3072,384]{2,1,0:T(8,128)(2,1)S(1)} %copy-done, f32[256,384]{1,0:T(8,128)S(1)} %get-tuple-element.81.cos_ref, f32[256,384]{1,0:T(8,128)S(1)} %get-tuple-element.80.sin_ref), custom_call_target="tpu_custom_call" | custom-call | tf_op jit(solution)/shard_map/project/pallas_call | solution.py:58
  41.2 10.0 %collective-permute-done.4.refs_7_ = bf16[8,128,384]{2,1,0:T(8,128)(2,1)} collective-permute-done((bf16[8,128,384]{2,1,0:T(8,128)(2,1)S(1)}, bf16[8,128,384]{2,1,0:T(8,128)(2,1)}, u32[]{:S(2)}, u32[]{:S(2)}) %collective-permute-start.4) | collective-permute-done | bytes 786464 | tf_op jit(solution)/shard_map/ppermute | solution.py:398
  57.2 10.6 %collective-permute-done.11 = bf16[384,3200]{1,0:T(8,128)(2,1)} collective-permute-done((bf16[384,3200]{1,0:T(8,128)(2,1)}, bf16[384,3200]{1,0:T(8,128)(2,1)}, u32[]{:S(2)}, u32[]{:S(2)}) %collective-permute-start.11) | collective-permute-done | bytes 2457632 | tf_op jit(solution)/shard_map/ppermute | solution.py:370
  67.8 10.7 %all-gather.3.cloned.1.call-done.refs_5_ = bf16[64,128,384]{2,1,0:T(8,128)(2,1)} async-done(((bf16[2,128,384]{2,1,0:T(8,128)(2,1)}), bf16[64,128,384]{2,1,0:T(8,128)(2,1)}) %all-gather.3.cloned.1.call-update) | async-done | bytes 6291472 | tf_op jit(solution)/shard_map/all_gather | solution.py:442
  78.8 5.6 %attend.1 = bf16[2,128,384]{2,1,0:T(8,128)(2,1)S(1)} custom-call(s32[4]{0:T(128)S(1)} %pad_add_fusion.refs_0_, s32[8]{0:T(128)S(1)} %copy-done.3, s32[64]{0:T(128)S(1)} %copy-done.4, s32[128]{0:T(128)S(1)} %copy-done.5, bf16[3,256,384]{2,1,0:T(8,128)(2,1)S(1)} %project.1.refs_4_, bf16[64,128,384]{2,1,0:T(8,128)(2,1)} %all-gather.3.cloned.1.call-done.refs_5_, ...), custom_call_target="tpu_custom_call" | custom-call | tf_op jit(solution)/shard_map/attend/pallas_call | solution.py:181
  84.5 1.6 collective-permute-start.12
  86.8 2.7 %collective-permute-done.12 = bf16[128,384]{1,0:T(8,128)(2,1)S(1)} collective-permute-done((bf16[128,384]{1,0:T(8,128)(2,1)S(1)}, bf16[128,384]{1,0:T(8,128)(2,1)S(1)}, u32[]{:S(2)}, u32[]{:S(2)}) %collective-permute-start.12) | collective-permute-done | bytes 98336 | tf_op jit(solution)/shard_map/ppermute | solution.py:370
  89.6 2.3 %fusion.1 = bf16[128,3200]{1,0:T(8,128)(2,1)S(1)} fusion(f32[128,3200]{1,0:T(8,128)S(1)} %fusion.3, bf16[128,384]{1,0:T(8,128)(2,1)S(1)} %collective-permute-done.12, bf16[384,3200]{1,0:T(8,128)(2,1)} %collective-permute-done.11), kind=kOutput, calls=%fused_computation.3 | convolution fusion | flops 315392000 | bytes 5013504 | tf_op jit(solution)/shard_map/dot_general | solution.py:481
  92.0 5.8 %collective-permute-start.13 = (bf16[32,3200]{1,0:T(8,128)(2,1)S(1)}, bf16[32,3200]{1,0:T(8,128)(2,1)S(1)}, u32[]{:S(2)}, u32[]{:S(2)}) collective-permute-start(bf16[32,3200]{1,0:T(8,128)(2,1)S(1)} %get-tuple-element.68), channel_id=1, source_target_pairs={{0,4},{1,5},{2,6},{3,7},{4,0},{5,1},{6,2},{7,3},{8,12},{9,13},{10,... | collective-permute-start | bytes 614408 | tf_op jit(solution)/shard_map/ppermute | solution.py:366
  98.6 3.4 %collective-permute-start.15 = (bf16[32,3200]{1,0:T(8,128)(2,1)S(1)}, bf16[32,3200]{1,0:T(8,128)(2,1)S(1)}, u32[]{:S(2)}, u32[]{:S(2)}) collective-permute-start(bf16[32,3200]{1,0:T(8,128)(2,1)S(1)} %get-tuple-element.66), channel_id=1, source_target_pairs={{0,6},{1,7},{2,0},{3,1},{4,2},{5,3},{6,4},{7,5},{8,14},{9,15},{10,... | collective-permute-start | bytes 614408 | tf_op jit(solution)/shard_map/ppermute | solution.py:366
  102.0 6.7 %collective-permute-done.13.refs_1_ = bf16[32,3200]{1,0:T(8,128)(2,1)S(1)} collective-permute-done((bf16[32,3200]{1,0:T(8,128)(2,1)S(1)}, bf16[32,3200]{1,0:T(8,128)(2,1)S(1)}, u32[]{:S(2)}, u32[]{:S(2)}) %collective-permute-start.13) | collective-permute-done | bytes 204832 | tf_op jit(solution)/shard_map/ppermute | solution.py:366
  108.7 3.8 %collective-permute-done.14.refs_2_ = bf16[32,3200]{1,0:T(8,128)(2,1)S(1)} collective-permute-done((bf16[32,3200]{1,0:T(8,128)(2,1)S(1)}, bf16[32,3200]{1,0:T(8,128)(2,1)S(1)}, u32[]{:S(2)}, u32[]{:S(2)}) %collective-permute-start.14) | collective-permute-done | bytes 204832 | tf_op jit(solution)/shard_map/ppermute | solution.py:366
  112.5 3.8 %collective-permute-done.15.refs_3_ = bf16[32,3200]{1,0:T(8,128)(2,1)S(1)} collective-permute-done((bf16[32,3200]{1,0:T(8,128)(2,1)S(1)}, bf16[32,3200]{1,0:T(8,128)(2,1)S(1)}, u32[]{:S(2)}, u32[]{:S(2)}) %collective-permute-start.15) | collective-permute-done | bytes 204832 | tf_op jit(solution)/shard_map/ppermute | solution.py:366
  116.8 2.0 %collective-permute-start.17 = (bf16[32,3200]{1,0:T(8,128)(2,1)S(1)}, bf16[32,3200]{1,0:T(8,128)(2,1)S(1)}, u32[]{:S(2)}, u32[]{:S(2)}) collective-permute-start(bf16[32,3200]{1,0:T(8,128)(2,1)S(1)} %settle.1.refs_5_), channel_id=1, source_target_pairs={{0,1},{1,2},{2,3},{3,4},{4,5},{5,6},{6,7},{7,0},{8,9},{9,10},{10,1... | collective-permute-start | bytes 614408 | tf_op jit(solution)/shard_map/ppermute | solution.py:366
  118.8 3.4 %collective-permute-start.18 = (bf16[32,3200]{1,0:T(8,128)(2,1)S(1)}, bf16[32,3200]{1,0:T(8,128)(2,1)S(1)}, u32[]{:S(2)}, u32[]{:S(2)}) collective-permute-start(bf16[32,3200]{1,0:T(8,128)(2,1)S(1)} %settle.1.refs_5_), channel_id=1, source_target_pairs={{0,6},{1,7},{2,0},{3,1},{4,2},{5,3},{6,4},{7,5},{8,14},{9,15},{10,... | collective-permute-start | bytes 614408 | tf_op jit(solution)/shard_map/ppermute | solution.py:366
  122.6 2.5 %collective-permute-done.16.refs_7_ = bf16[32,3200]{1,0:T(8,128)(2,1)S(1)} collective-permute-done((bf16[32,3200]{1,0:T(8,128)(2,1)S(1)}, bf16[32,3200]{1,0:T(8,128)(2,1)S(1)}, u32[]{:S(2)}, u32[]{:S(2)}) %collective-permute-start.16) | collective-permute-done | bytes 204832 | tf_op jit(solution)/shard_map/ppermute | solution.py:366
  126.7 6.2 %collective-permute-done.18.refs_11_ = bf16[32,3200]{1,0:T(8,128)(2,1)S(1)} collective-permute-done((bf16[32,3200]{1,0:T(8,128)(2,1)S(1)}, bf16[32,3200]{1,0:T(8,128)(2,1)S(1)}, u32[]{:S(2)}, u32[]{:S(2)}) %collective-permute-start.18) | collective-permute-done | bytes 204832 | tf_op jit(solution)/shard_map/ppermute | solution.py:366
  132.8 2.9 %collective-permute-done.19.refs_13_ = bf16[32,3200]{1,0:T(8,128)(2,1)S(1)} collective-permute-done((bf16[32,3200]{1,0:T(8,128)(2,1)S(1)}, bf16[32,3200]{1,0:T(8,128)(2,1)S(1)}, u32[]{:S(2)}, u32[]{:S(2)}) %collective-permute-start.19) | collective-permute-done | bytes 204832 | tf_op jit(solution)/shard_map/ppermute | solution.py:366
  136.2 1.6 collective-permute-start.21
  139.2 1.8 collective-permute-start.23
  141.0 7.4 %all-gather.5.cloned.1.call-done.refs_3_ = bf16[3072,2048]{1,0:T(8,128)(2,1)} async-done(((bf16[96,2048]{1,0:T(8,128)(2,1)}), bf16[3072,2048]{1,0:T(8,128)(2,1)}) %all-gather.5.cloned.1.call-update) | async-done | bytes 12582928 | tf_op jit(solution)/shard_map/all_gather | solution.py:468
  148.4 8.8 %score.2 = f32[8,320]{1,0:T(8,128)S(1)} custom-call(s32[6]{0:T(128)S(1)} %stack.64.refs_0_, bf16[16,3072]{1,0:T(8,128)(2,1)S(1)} %copy-done.2, bf16[1,3072]{1,0:T(2,128)(2,1)S(1)} %broadcast_in_dim.44.gain_ref.refs_2_, bf16[3072,2048]{1,0:T(8,128)(2,1)} %all-gather.5.cloned.1.call-done.refs_3_, s32[256,1]{1,0:T(8,128)S(1)} %copy.51.refs_4_.refs_6_.refs_8_.refs_10_.refs_12_, ...), custom_call_target="tpu_custom_call" | custom-call | flops 4026531840 | bytes 12582912 | tf_op jit(solution)/shard_map/score/pallas_call | solution.py:332
  157.3 8.1 %score.3 = f32[8,192]{1,0:T(8,128)S(1)} custom-call(s32[5]{0:T(128)S(1)} %stack.69.refs_0_, bf16[16,3072]{1,0:T(8,128)(2,1)S(1)} %copy-done.2, bf16[1,3072]{1,0:T(2,128)(2,1)S(1)} %broadcast_in_dim.44.gain_ref.refs_2_, bf16[3072,2048]{1,0:T(8,128)(2,1)} %all-gather.5.cloned.1.call-done.refs_3_, s32[256,1]{1,0:T(8,128)S(1)} %copy.51.refs_4_.refs_6_.refs_8_.refs_10_.refs_12_, ...), custom_call_target="tpu_custom_call" | custom-call | flops 2415919104 | bytes 12582912 | tf_op jit(solution)/shard_map/score/pallas_call | solution.py:332
  165.9 16.3 %all_to_all.5 = f32[8,8,512]{2,1,0:T(8,128)S(1)} all-to-all(f32[8,8,512]{2,1,0:T(8,128)S(1)} %broadcast_in_dim.51), channel_id=1, replica_groups=mesh['seq'=32,'tensor'=8] {'tensor'}, dimensions={0} | all-to-all | bytes 262144 | tf_op jit(solution)/shard_map/all_to_all | solution.py:529
  (97 shorter events, 21.6 us)
Async XLA Ops:
  7.2 71.4 %all-gather.3.cloned.1.call-start = ((), (), s32[]{:S(2)}) async-start(), calls=%async_computation.1 | async-start | bytes 6488064 | tf_op jit(solution)/shard_map/all_gather | solution.py:442
  7.9 140.5 %all-gather.5.cloned.1.call-start = ((), (), s32[]{:S(2)}) async-start(), calls=%async_computation.2 | async-start | bytes 12976128 | tf_op jit(solution)/shard_map/all_gather | solution.py:468
  8.8 23.1 %copy-start.13 = (bf16[3072]{0:T(1024)(128)(2,1)S(1)}, bf16[3072]{0:T(1024)(128)(2,1)}, u32[]{:S(2)}) copy-start(bf16[3072]{0:T(1024)(128)(2,1)} %param.15) | copy-start | bytes 18436
  12.2 21.2 %copy-start.1 = (bf16[256,3072]{1,0:T(8,128)(2,1)S(1)}, bf16[256,3072]{1,0:T(8,128)(2,1)}, u32[]{:S(2)}) copy-start(bf16[256,3072]{1,0:T(8,128)(2,1)} %hidden_ref.3) | copy-start | bytes 4718596
  12.2 55.6 %collective-permute-start.11 = (bf16[384,3200]{1,0:T(8,128)(2,1)}, bf16[384,3200]{1,0:T(8,128)(2,1)}, u32[]{:S(2)}, u32[]{:S(2)}) collective-permute-start(bf16[384,3200]{1,0:T(8,128)(2,1)} %fusion.2), channel_id=1, source_target_pairs={{0,1},{1,0},{2,3},{3,2},{4,5},{5,4},{6,7},{7,6},{8,9},{9,8},{10,11... | collective-permute-start | bytes 7372808 | tf_op jit(solution)/shard_map/ppermute | solution.py:370
  14.2 1.4 collective-permute-start
  15.6 8.2 %collective-permute-start.1 = (bf16[2,128,384]{2,1,0:T(8,128)(2,1)S(1)}, bf16[2,128,384]{2,1,0:T(8,128)(2,1)S(1)}, u32[]{:S(2)}, u32[]{:S(2)}) collective-permute-start(bf16[2,128,384]{2,1,0:T(8,128)(2,1)S(1)} %pad_maximum_fusion.1), channel_id=1, source_target_pairs={{0,48},{8,200},{16,0},{24,216},{32,16},{40,232},{48,32},{56,248},{... | collective-permute-start | bytes 589832 | tf_op jit(solution)/shard_map/ppermute | solution.py:398
  18.4 7.3 %collective-permute-start.2 = (bf16[2,128,384]{2,1,0:T(8,128)(2,1)S(1)}, bf16[2,128,384]{2,1,0:T(8,128)(2,1)S(1)}, u32[]{:S(2)}, u32[]{:S(2)}) collective-permute-start(bf16[2,128,384]{2,1,0:T(8,128)(2,1)S(1)} %pad_maximum_fusion.1), channel_id=1, source_target_pairs={{0,32},{8,136},{16,48},{24,152},{32,0},{40,168},{48,16},{56,184},{... | collective-permute-start | bytes 589832 | tf_op jit(solution)/shard_map/ppermute | solution.py:398
  19.2 8.5 %collective-permute-start.3 = (bf16[2,128,384]{2,1,0:T(8,128)(2,1)S(1)}, bf16[2,128,384]{2,1,0:T(8,128)(2,1)S(1)}, u32[]{:S(2)}, u32[]{:S(2)}) collective-permute-start(bf16[2,128,384]{2,1,0:T(8,128)(2,1)S(1)} %pad_maximum_fusion.1), channel_id=1, source_target_pairs={{0,16},{8,72},{16,32},{24,88},{32,48},{40,104},{48,0},{56,120},{64... | collective-permute-start | bytes 589832 | tf_op jit(solution)/shard_map/ppermute | solution.py:398
  27.8 23.4 %collective-permute-start.4 = (bf16[8,128,384]{2,1,0:T(8,128)(2,1)S(1)}, bf16[8,128,384]{2,1,0:T(8,128)(2,1)}, u32[]{:S(2)}, u32[]{:S(2)}) collective-permute-start(bf16[8,128,384]{2,1,0:T(8,128)(2,1)S(1)} %pad_maximum_fusion.refs_6_), channel_id=1, source_target_pairs={{0,192},{8,56},{16,208},{24,8},{32,224},{40,24},{48,240},{56,40},{... | collective-permute-start | bytes 2359304 | tf_op jit(solution)/shard_map/ppermute | solution.py:398
  28.7 22.5 %collective-permute-start.5 = (bf16[8,128,384]{2,1,0:T(8,128)(2,1)S(1)}, bf16[8,128,384]{2,1,0:T(8,128)(2,1)}, u32[]{:S(2)}, u32[]{:S(2)}) collective-permute-start(bf16[8,128,384]{2,1,0:T(8,128)(2,1)S(1)} %pad_maximum_fusion.refs_6_), channel_id=1, source_target_pairs={{0,128},{8,40},{16,144},{24,56},{32,160},{40,8},{48,176},{56,24},{... | collective-permute-start | bytes 2359304 | tf_op jit(solution)/shard_map/ppermute | solution.py:398
  29.6 22.0 %collective-permute-start.6 = (bf16[8,128,384]{2,1,0:T(8,128)(2,1)S(1)}, bf16[8,128,384]{2,1,0:T(8,128)(2,1)}, u32[]{:S(2)}, u32[]{:S(2)}) collective-permute-start(bf16[8,128,384]{2,1,0:T(8,128)(2,1)S(1)} %pad_maximum_fusion.refs_6_), channel_id=1, source_target_pairs={{0,64},{8,24},{16,80},{24,40},{32,96},{40,56},{48,112},{56,8},{64,... | collective-permute-start | bytes 2359304 | tf_op jit(solution)/shard_map/ppermute | solution.py:398
  36.5 42.4 %copy-start.4 = (s32[64]{0:T(128)S(1)}, s32[64]{0:T(128)}, u32[]{:S(2)}) copy-start(s32[64]{0:T(128)} %refs_2_.1) | copy-start | bytes 772
  41.1 11.0 %collective-permute-start.7 = (bf16[8,128,384]{2,1,0:T(8,128)(2,1)S(1)}, bf16[8,128,384]{2,1,0:T(8,128)(2,1)S(1)}, u32[]{:S(2)}, u32[]{:S(2)}) collective-permute-start(bf16[8,128,384]{2,1,0:T(8,128)(2,1)S(1)} %pad_maximum_fusion.refs_6_), channel_id=1, source_target_pairs={{0,8},{8,0},{16,24},{24,16},{32,40},{40,32},{48,56},{56,48},{64,72... | collective-permute-start | bytes 2359304 | tf_op jit(solution)/shard_map/ppermute | solution.py:386
  51.6 2.5 %collective-permute-start.10 = (bf16[8,128,384]{2,1,0:T(8,128)(2,1)}, bf16[8,128,384]{2,1,0:T(8,128)(2,1)S(1)}, u32[]{:S(2)}, u32[]{:S(2)}) collective-permute-start(bf16[8,128,384]{2,1,0:T(8,128)(2,1)} %collective-permute-done.6.refs_9_), channel_id=1, source_target_pairs={{0,8},{8,0},{16,24},{24,16},{32,40},{40,32},{48,56},{56,48},{64,72... | collective-permute-start | bytes 2359304 | tf_op jit(solution)/shard_map/ppermute | solution.py:386
  51.6 3.6 %collective-permute-start.8 = (bf16[8,128,384]{2,1,0:T(8,128)(2,1)}, bf16[8,128,384]{2,1,0:T(8,128)(2,1)S(1)}, u32[]{:S(2)}, u32[]{:S(2)}) collective-permute-start(bf16[8,128,384]{2,1,0:T(8,128)(2,1)} %collective-permute-done.4.refs_7_), channel_id=1, source_target_pairs={{0,8},{8,0},{16,24},{24,16},{32,40},{40,32},{48,56},{56,48},{64,72... | collective-permute-start | bytes 2359304 | tf_op jit(solution)/shard_map/ppermute | solution.py:386
  52.1 4.2 %collective-permute-start.9 = (bf16[8,128,384]{2,1,0:T(8,128)(2,1)}, bf16[8,128,384]{2,1,0:T(8,128)(2,1)S(1)}, u32[]{:S(2)}, u32[]{:S(2)}) collective-permute-start(bf16[8,128,384]{2,1,0:T(8,128)(2,1)} %collective-permute-done.5.refs_8_), channel_id=1, source_target_pairs={{0,8},{8,0},{16,24},{24,16},{32,40},{40,32},{48,56},{56,48},{64,72... | collective-permute-start | bytes 2359304 | tf_op jit(solution)/shard_map/ppermute | solution.py:386
  84.5 5.0 %collective-permute-start.12 = (bf16[128,384]{1,0:T(8,128)(2,1)S(1)}, bf16[128,384]{1,0:T(8,128)(2,1)S(1)}, u32[]{:S(2)}, u32[]{:S(2)}) collective-permute-start(bf16[128,384]{1,0:T(8,128)(2,1)S(1)} %dynamic-slice_bitcast_fusion), channel_id=1, source_target_pairs={{0,1},{1,0},{2,3},{3,2},{4,5},{5,4},{6,7},{7,6},{8,9},{9,8},{10,11... | collective-permute-start | bytes 294920 | tf_op jit(solution)/shard_map/ppermute | solution.py:370
  86.8 15.2 %copy-start.14 = (bf16[3072]{0:T(1024)(128)(2,1)S(1)}, bf16[3072]{0:T(1024)(128)(2,1)}, u32[]{:S(2)}) copy-start(bf16[3072]{0:T(1024)(128)(2,1)} %param.20) | copy-start | bytes 18436
  86.8 29.5 %copy-start.2 = (bf16[16,3072]{1,0:T(8,128)(2,1)S(1)}, bf16[16,3072]{1,0:T(8,128)(2,1)}, u32[]{:S(2)}) copy-start(bf16[16,3072]{1,0:T(8,128)(2,1)} %refs_1_.5) | copy-start | bytes 294916
  91.9 30.3 %copy-start.15 = (s32[256]{0:T(256)S(1)}, s32[256]{0:T(256)}, u32[]{:S(2)}) copy-start(s32[256]{0:T(256)} %param.27) | copy-start | bytes 3076
  92.0 16.7 %collective-permute-start.13 = (bf16[32,3200]{1,0:T(8,128)(2,1)S(1)}, bf16[32,3200]{1,0:T(8,128)(2,1)S(1)}, u32[]{:S(2)}, u32[]{:S(2)}) collective-permute-start(bf16[32,3200]{1,0:T(8,128)(2,1)S(1)} %get-tuple-element.68), channel_id=1, source_target_pairs={{0,4},{1,5},{2,6},{3,7},{4,0},{5,1},{6,2},{7,3},{8,12},{9,13},{10,... | collective-permute-start | bytes 614408 | tf_op jit(solution)/shard_map/ppermute | solution.py:366
  97.8 14.7 %collective-permute-start.14 = (bf16[32,3200]{1,0:T(8,128)(2,1)S(1)}, bf16[32,3200]{1,0:T(8,128)(2,1)S(1)}, u32[]{:S(2)}, u32[]{:S(2)}) collective-permute-start(bf16[32,3200]{1,0:T(8,128)(2,1)S(1)} %get-tuple-element.67), channel_id=1, source_target_pairs={{0,2},{1,3},{2,4},{3,5},{4,6},{5,7},{6,0},{7,1},{8,10},{9,11},{10,... | collective-permute-start | bytes 614408 | tf_op jit(solution)/shard_map/ppermute | solution.py:366
  98.6 17.7 %collective-permute-start.15 = (bf16[32,3200]{1,0:T(8,128)(2,1)S(1)}, bf16[32,3200]{1,0:T(8,128)(2,1)S(1)}, u32[]{:S(2)}, u32[]{:S(2)}) collective-permute-start(bf16[32,3200]{1,0:T(8,128)(2,1)S(1)} %get-tuple-element.66), channel_id=1, source_target_pairs={{0,6},{1,7},{2,0},{3,1},{4,2},{5,3},{6,4},{7,5},{8,14},{9,15},{10,... | collective-permute-start | bytes 614408 | tf_op jit(solution)/shard_map/ppermute | solution.py:366
  116.7 8.4 %collective-permute-start.16 = (bf16[32,3200]{1,0:T(8,128)(2,1)S(1)}, bf16[32,3200]{1,0:T(8,128)(2,1)S(1)}, u32[]{:S(2)}, u32[]{:S(2)}) collective-permute-start(bf16[32,3200]{1,0:T(8,128)(2,1)S(1)} %settle.1.refs_5_), channel_id=1, source_target_pairs={{0,7},{1,0},{2,1},{3,2},{4,3},{5,4},{6,5},{7,6},{8,15},{9,8},{10,9... | collective-permute-start | bytes 614408 | tf_op jit(solution)/shard_map/ppermute | solution.py:366
  116.8 9.9 %collective-permute-start.17 = (bf16[32,3200]{1,0:T(8,128)(2,1)S(1)}, bf16[32,3200]{1,0:T(8,128)(2,1)S(1)}, u32[]{:S(2)}, u32[]{:S(2)}) collective-permute-start(bf16[32,3200]{1,0:T(8,128)(2,1)S(1)} %settle.1.refs_5_), channel_id=1, source_target_pairs={{0,1},{1,2},{2,3},{3,4},{4,5},{5,6},{6,7},{7,0},{8,9},{9,10},{10,1... | collective-permute-start | bytes 614408 | tf_op jit(solution)/shard_map/ppermute | solution.py:366
  118.8 14.0 %collective-permute-start.18 = (bf16[32,3200]{1,0:T(8,128)(2,1)S(1)}, bf16[32,3200]{1,0:T(8,128)(2,1)S(1)}, u32[]{:S(2)}, u32[]{:S(2)}) collective-permute-start(bf16[32,3200]{1,0:T(8,128)(2,1)S(1)} %settle.1.refs_5_), channel_id=1, source_target_pairs={{0,6},{1,7},{2,0},{3,1},{4,2},{5,3},{6,4},{7,5},{8,14},{9,15},{10,... | collective-permute-start | bytes 614408 | tf_op jit(solution)/shard_map/ppermute | solution.py:366
  122.2 13.5 %collective-permute-start.19 = (bf16[32,3200]{1,0:T(8,128)(2,1)S(1)}, bf16[32,3200]{1,0:T(8,128)(2,1)S(1)}, u32[]{:S(2)}, u32[]{:S(2)}) collective-permute-start(bf16[32,3200]{1,0:T(8,128)(2,1)S(1)} %settle.1.refs_5_), channel_id=1, source_target_pairs={{0,2},{1,3},{2,4},{3,5},{4,6},{5,7},{6,0},{7,1},{8,10},{9,11},{10,... | collective-permute-start | bytes 614408 | tf_op jit(solution)/shard_map/ppermute | solution.py:366
  135.7 21.5 %collective-permute-start.20 = (bf16[32,3200]{1,0:T(8,128)(2,1)S(1)}, bf16[32,3200]{1,0:T(8,128)(2,1)S(1)}, u32[]{:S(2)}, u32[]{:S(2)}) collective-permute-start(bf16[32,3200]{1,0:T(8,128)(2,1)S(1)} %collective-permute-done.18.refs_11_), channel_id=1, source_target_pairs={{0,7},{1,0},{2,1},{3,2},{4,3},{5,4},{6,5},{7,6},{8,15},{9,8},{10,9... | collective-permute-start | bytes 614408 | tf_op jit(solution)/shard_map/ppermute | solution.py:366
  136.2 21.1 %collective-permute-start.21 = (bf16[32,3200]{1,0:T(8,128)(2,1)S(1)}, bf16[32,3200]{1,0:T(8,128)(2,1)S(1)}, u32[]{:S(2)}, u32[]{:S(2)}) collective-permute-start(bf16[32,3200]{1,0:T(8,128)(2,1)S(1)} %collective-permute-done.19.refs_13_), channel_id=1, source_target_pairs={{0,1},{1,2},{2,3},{3,4},{4,5},{5,6},{6,7},{7,0},{8,9},{9,10},{10,1... | collective-permute-start | bytes 614408 | tf_op jit(solution)/shard_map/ppermute | solution.py:366
  137.8 19.4 %collective-permute-start.22 = (bf16[16,3200]{1,0:T(8,128)(2,1)S(1)}, bf16[16,3200]{1,0:T(8,128)(2,1)S(1)}, u32[]{:S(2)}, u32[]{:S(2)}) collective-permute-start(bf16[16,3200]{1,0:T(8,128)(2,1)S(1)} %slice.45), channel_id=1, source_target_pairs={{0,6},{1,7},{2,0},{3,1},{4,2},{5,3},{6,4},{7,5},{8,14},{9,15},{10,... | collective-permute-start | bytes 307208 | tf_op jit(solution)/shard_map/ppermute | solution.py:366
  139.2 18.0 %collective-permute-start.23 = (bf16[16,3200]{1,0:T(8,128)(2,1)S(1)}, bf16[16,3200]{1,0:T(8,128)(2,1)S(1)}, u32[]{:S(2)}, u32[]{:S(2)}) collective-permute-start(bf16[16,3200]{1,0:T(8,128)(2,1)S(1)} %slice.46), channel_id=1, source_target_pairs={{0,2},{1,3},{2,4},{3,5},{4,6},{5,7},{6,0},{7,1},{8,10},{9,11},{10,... | collective-permute-start | bytes 307208 | tf_op jit(solution)/shard_map/ppermute | solution.py:366
  (10 other events, 55.4 us)
Sparse Core Ops, SparseCore 0:
  10.5 67.9 all-gather.2
  81.1 67.3 all-gather.4

commit v3 on v2

--- a/solution.py
+++ b/solution.py
@@ -79,9 +79,9 @@
 
 def attend_kernel(*refs):
     first_ref, counts_ref, index_ref, owner_ref = refs[:4]
-    qkv_ref, cached_values_ref = refs[4:6]
+    qkv_ref = refs[4]
     out_ref, keys, values, sems = refs[-4:]
-    pieces = refs[6:-4]
+    pieces = refs[5:-4]
     rollouts = keys.shape[0]
     width = qkv_ref.shape[2]
     heads = width // HEAD_WIDTH
@@ -91,22 +91,22 @@
 
     def start_copies(r, j):
         slot = index_ref[owner_ref[first + r] * MAXP + j]
-        device, path = slot // 2, slot % 2
+        device = slot // 2
         down_y = (device // 8 - my_y + 4) % 4
         down_x = (device // 2 % 4 - my_x + 4) % 4
-        far = jnp.where(path == 0, down_y, down_x)
-        near = jnp.where(path == 0, down_x, down_y)
-        at = near * 2 + (device % 2 != path).astype(jnp.int32)
-        piece = far + 4 * (my_core != path).astype(jnp.int32)
         rows = pl.ds(pl.multiple_of(j * PAGE, PAGE), PAGE)
-        pltpu.make_async_copy(
-            cached_values_ref.at[slot], values.at[r, rows], sems.at[r, 1, j]
-        ).start()
-        for p, ref in enumerate(pieces):
-
-            @pl.when(piece == p)
-            def _():
-                pltpu.make_async_copy(ref.at[at], keys.at[r, rows], sems.at[r, 0, j]).start()
+        for path, (buffer, far, near) in enumerate(
+            ((keys, down_y, down_x), (values, down_x, down_y))
+        ):
+            at = near * 4 + 2 * (device % 2 != path).astype(jnp.int32) + slot % 2
+            piece = far + 4 * (my_core != path).astype(jnp.int32)
+            for p, ref in enumerate(pieces):
+
+                @pl.when(piece == p)
+                def _():
+                    pltpu.make_async_copy(
+                        ref.at[at], buffer.at[r, rows], sems.at[r, path, j]
+                    ).start()
 
         return 0
 
@@ -171,19 +171,17 @@
     lax.fori_loop(0, rollouts, mix_rollout, 0)
 
 
-def attend(first, counts, index, owner, qkv, cached_values, pieces):
+def attend(first, counts, index, owner, qkv, pieces):
     _, rows, width = qkv.shape
     rollouts = rows // LEN
     vmem = pl.BlockSpec(memory_space=pltpu.VMEM)
-    cached = [
-        pltpu.with_memory_space_constraint(piece, pltpu.HBM) for piece in [cached_values] + pieces
-    ]
+    pieces = [pltpu.with_memory_space_constraint(piece, pltpu.HBM) for piece in pieces]
     return pl.pallas_call(
         attend_kernel,
         grid_spec=pltpu.PrefetchScalarGridSpec(
             num_scalar_prefetch=4,
             grid=(),
-            in_specs=[vmem] + [pl.BlockSpec(memory_space=pltpu.HBM)] * len(cached),
+            in_specs=[vmem] + [pl.BlockSpec(memory_space=pltpu.HBM)] * len(pieces),
             out_specs=vmem,
             scratch_shapes=[
                 pltpu.VMEM((rollouts, MAXP * PAGE, width), BF16),
@@ -194,7 +192,7 @@
         out_shape=jax.ShapeDtypeStruct((2, rows // 2, width), BF16),
         compiler_params=pltpu.CompilerParams(vmem_limit_bytes=VMEM_LIMIT),
         name="attend",
-    )(first, counts, index, owner, qkv, *cached)
+    )(first, counts, index, owner, qkv, *pieces)
 
 
 def two_parts(value):
@@ -255,76 +253,106 @@
 
 
 def score_kernel(*refs):
-    place_ref, up_ref, gain_ref, head_ref = refs[:4]
-    out_ref, normed, deltas, scales, wanted, largest, total, picked = refs[-8:]
-    inputs = refs[4:-8]
-    step = pl.program_id(0)
+    place_ref, up_ref, gain_ref = refs[:3]
+    pieces = refs[3:11]
+    out_ref, normed, deltas, scales, wanted, largest, total, picked, head, sems = refs[-10:]
+    inputs = refs[11:-10]
     rank, model = up_ref.shape
     rows = deltas.shape[0]
-    tile = head_ref.shape[1]
-
-    @pl.when(step == 0)
-    def _():
-        start = 0
-        for target_ref, block in zip(inputs[::2], inputs[1::2]):
-            at = slice(start, start + block.shape[0])
-            start += block.shape[0]
-            normed[at, :] = block[:, :model]
-            beside = block[:, model:]
-            deltas[at, :] = beside[:, : 2 * rank]
-            beside = beside.astype(F32)
-            lane = lax.broadcasted_iota(jnp.int32, beside.shape, 1) - 2 * rank
-            for which in range(2):
-                parts = (lane >= 3 * which) & (lane < 3 * which + 3)
-                scales[which, at, :] = jnp.sum(
-                    jnp.where(parts, beside, 0.0), axis=1, keepdims=True
-                )
-            wanted[at, :] = target_ref[...] - place_ref[0] * pl.num_programs(0) * tile
-        high, low = two_parts(up_ref[...].astype(F32) * gain_ref[...].astype(F32))
-        normed[rows : rows + rank, :] = high
-        normed[rows + rank :, :] = low
-        largest[...] = jnp.full_like(largest, NEGATIVE)
-        total[...] = jnp.zeros_like(total)
-        picked[...] = jnp.zeros_like(picked)
-
-    product = jnp.dot(normed[...], head_ref[...], preferred_element_type=F32)
-    reference_logits = product[:rows]
-    adapted = jnp.zeros_like(reference_logits)
-    for part in two_parts(product[rows : rows + rank] + product[rows + rank :]):
-        adapted += jnp.dot(
-            deltas[...], jnp.concatenate([part, part], axis=0), preferred_element_type=F32
+    vocab = head.shape[1]
+    part_rows = pieces[0].shape[0] // 8
+    spans = sems.shape[0]
+    span = vocab // spans
+    my_y, my_x, my_core = place_ref[1], place_ref[2], place_ref[3]
+
+    for which in range(spans):
+        columns = slice(which * span, (which + 1) * span)
+        for p, piece in enumerate(pieces):
+            path = my_core if p < 4 else 1 - my_core
+
+            def start_part(n, _, piece=piece, far=p % 4, path=path, which=which, columns=columns):
+                near = n // 2
+                y = (my_y + jnp.where(path == 0, far, near)) % 4
+                x = (my_x + jnp.where(path == 0, near, far)) % 4
+                core = jnp.where(n % 2 == 0, path, 1 - path)
+                row = (y * 8 + x * 2 + core) * 2 * part_rows + path * part_rows
+                pltpu.make_async_copy(
+                    piece.at[pl.ds(pl.multiple_of(n * part_rows, 16), part_rows), columns],
+                    head.at[pl.ds(pl.multiple_of(row, 16), part_rows), columns],
+                    sems.at[which],
+                ).start()
+                return 0
+
+            lax.fori_loop(0, 8, start_part, 0)
+
+    start = 0
+    for target_ref, block in zip(inputs[::2], inputs[1::2]):
+        at = slice(start, start + block.shape[0])
+        start += block.shape[0]
+        normed[at, :] = block[:, :model]
+        beside = block[:, model:]
+        deltas[at, :] = beside[:, : 2 * rank]
+        beside = beside.astype(F32)
+        lane = lax.broadcasted_iota(jnp.int32, beside.shape, 1) - 2 * rank
+        for which in range(2):
+            parts = (lane >= 3 * which) & (lane < 3 * which + 3)
+            scales[which, at, :] = jnp.sum(jnp.where(parts, beside, 0.0), axis=1, keepdims=True)
+        wanted[at, :] = target_ref[...] - place_ref[0] * vocab
+    high, low = two_parts(up_ref[...].astype(F32) * gain_ref[...].astype(F32))
+    normed[rows : rows + rank, :] = high
+    normed[rows + rank :, :] = low
+    largest[...] = jnp.full_like(largest, NEGATIVE)
+    total[...] = jnp.zeros_like(total)
+    picked[...] = jnp.zeros_like(picked)
+    tile = 512
+
+    def score_tile(n, _):
+        product = jnp.dot(
+            normed[...],
+            head[:, pl.ds(pl.multiple_of(n * tile, tile), tile)],
+            preferred_element_type=F32,
         )
-    policy_logits = scales[0] * reference_logits + scales[1] * adapted
-    columns = lax.broadcasted_iota(jnp.int32, reference_logits.shape, 1)
-    hit = columns == wanted[...] - step * tile
-    for which, logits in enumerate((policy_logits, reference_logits)):
-        picked[which] += jnp.sum(jnp.where(hit, logits, 0.0), axis=1, keepdims=True)
-        before = largest[which]
-        after = jnp.maximum(before, jnp.max(logits, axis=1, keepdims=True))
-        total[which] = total[which] * jnp.exp(before - after) + jnp.sum(
-            jnp.exp(logits - after), axis=1, keepdims=True
-        )
-        largest[which] = after
-
-    @pl.when(step == pl.num_programs(0) - 1)
-    def _():
-        lane = lax.broadcasted_iota(jnp.int32, (2, rows, 128), 2)
-        packed = jnp.where(
-            lane == 0, largest[...], jnp.where(lane == 1, total[...], picked[...])
-        )
-        out_ref[...] = jnp.transpose(packed.reshape(2 * rows, 128))[:8, :]
-
-
-def score(place, up, gain, targets, head, blocks):
+        reference_logits = product[:rows]
+        adapted = jnp.zeros_like(reference_logits)
+        for part in two_parts(product[rows : rows + rank] + product[rows + rank :]):
+            adapted += jnp.dot(
+                deltas[...], jnp.concatenate([part, part], axis=0), preferred_element_type=F32
+            )
+        policy_logits = scales[0] * reference_logits + scales[1] * adapted
+        columns = lax.broadcasted_iota(jnp.int32, reference_logits.shape, 1)
+        hit = columns == wanted[...] - n * tile
+        for which, logits in enumerate((policy_logits, reference_logits)):
+            picked[which] += jnp.sum(jnp.where(hit, logits, 0.0), axis=1, keepdims=True)
+            before = largest[which]
+            after = jnp.maximum(before, jnp.max(logits, axis=1, keepdims=True))
+            total[which] = total[which] * jnp.exp(before - after) + jnp.sum(
+                jnp.exp(logits - after), axis=1, keepdims=True
+            )
+            largest[which] = after
+        return 0
+
+    def score_span(which, _):
+        columns = pl.ds(pl.multiple_of(which * span, span), span)
+        pltpu.make_async_copy(head.at[:, columns], head.at[:, columns], sems.at[which]).wait()
+        per_span = span // tile
+        return lax.fori_loop(which * per_span, (which + 1) * per_span, score_tile, 0)
+
+    lax.fori_loop(0, spans, score_span, 0)
+    lane = lax.broadcasted_iota(jnp.int32, (2, rows, 128), 2)
+    packed = jnp.where(lane == 0, largest[...], jnp.where(lane == 1, total[...], picked[...]))
+    out_ref[...] = jnp.transpose(packed.reshape(2 * rows, 128))[:8, :]
+
+
+def score(place, up, gain, targets, pieces, blocks):
     rank, model = up.shape
-    vocab = head.shape[1]
+    vocab = pieces[0].shape[1]
     rows = sum(block.shape[0] for block in blocks)
-    tile = 512
     whole = lambda i, p: (0, 0)
+    pieces = [pltpu.with_memory_space_constraint(piece, pltpu.HBM) for piece in pieces]
     per_block, operands = [], []
     for k, block in enumerate(blocks):
         per_block += [
-            pl.BlockSpec((block.shape[0], 1), lambda i, p, k=k: (p[1 + k], 0)),
+            pl.BlockSpec((block.shape[0], 1), lambda i, p, k=k: (p[4 + k], 0)),
             pl.BlockSpec(block.shape, whole),
         ]
         operands += [targets, block]
@@ -333,12 +361,9 @@
         score_kernel,
         grid_spec=pltpu.PrefetchScalarGridSpec(
             num_scalar_prefetch=1,
-            grid=(vocab // tile,),
-            in_specs=[
-                pl.BlockSpec(up.shape, whole),
-                pl.BlockSpec(gain.shape, whole),
-                pl.BlockSpec((model, tile), lambda i, p: (0, i)),
-            ]
+            grid=(1,),
+            in_specs=[pl.BlockSpec(up.shape, whole), pl.BlockSpec(gain.shape, whole)]
+            + [pl.BlockSpec(memory_space=pltpu.HBM)] * len(pieces)
             + per_block,
             out_specs=pl.BlockSpec((8, 2 * rows), whole),
             scratch_shapes=[
@@ -349,6 +374,8 @@
                 column,
                 column,
                 column,
+                pltpu.VMEM((model, vocab), BF16),
+                pltpu.SemaphoreType.DMA((2,)),
             ],
         ),
         out_shape=jax.ShapeDtypeStruct((8, 2 * rows), F32),
@@ -359,7 +386,7 @@
             bytes_accessed=2 * model * vocab,
         ),
         name="score",
-    )(place, up, gain, head, *operands)
+    )(place, up, gain, *pieces, *operands)
 
 
 def shifted(value, ranks, step):
@@ -379,7 +406,7 @@
         return lax.dynamic_slice_in_dim(branch, at, size, 0)
 
     arrived = [shifted(block(step), ranks, step) for step in (ranks // 2, 2, ranks - 2)]
-    return [block(0)] + list(lax.optimization_barrier(arrived))
+    return [block(0)] + arrived
 
 
 def crossed(value):
@@ -398,19 +425,15 @@
     return lax.ppermute(value, "seq", [(i, target(i)) for i in range(32)])
 
 
-def gather_keys(keys, weights, project_now, ranks):
-    core = lax.axis_index("seq") % 2
-    kept = lax.dynamic_slice_in_dim(keys, core, 1, 0)
-    sent = lax.dynamic_slice_in_dim(keys, 1 - core, 1, 0)
-    pair = jnp.concatenate([kept, crossed(sent)])
-    partner = partnered(weights, ranks)
-    line = lax.optimization_barrier([pair] + [turned(pair, 0, step) for step in (3, 2, 1)])
-    line = lax.optimization_barrier(jnp.concatenate(line))
-    ahead = [turned(line, 1, step) for step in (3, 2, 1)]
-    near = crossed(line)
-    ahead, qkv = lax.optimization_barrier((ahead, project_now()))
-    pieces = [line] + ahead + [near] + [crossed(piece) for piece in ahead]
-    return pieces, partner, qkv
+def start_pair(first, second):
+    first_core = lax.axis_index("seq") % 2 == 0
+    kept = jnp.where(first_core, first, second)
+    sent = jnp.where(first_core, second, first)
+    return jnp.concatenate([kept, crossed(sent)])
+
+
+def along_first(pair):
+    return [pair] + [turned(pair, 0, step) for step in (3, 2, 1)]
 
 
 def local(
@@ -439,7 +462,6 @@
     rank = lax.axis_index("tensor")
     down = jnp.pad(adapter_down_weight, ((0, 0), (0, PAD - adapter_down_weight.shape[1])))
     weights = jnp.concatenate([output_weight, down], axis=1)
-    cached_values = lax.all_gather(prompt_value_slots, "seq", axis=0, tiled=True)
     groups_iota = jnp.arange(counts.shape[0], dtype=jnp.int32)
     my_groups = lax.dynamic_slice_in_dim(owner, first, rollouts_here, 0)
     my_pages = jnp.sum(
@@ -450,54 +472,62 @@
     place_in_head = jnp.arange(width_here, dtype=jnp.int32) % half
     frequency = 10000.0 ** (-place_in_head.astype(F32) * 2.0 / HEAD_WIDTH)
     angles = positions.astype(F32)[:, None] * frequency[None, :]
-    pieces, partner_weights, qkv = gather_keys(
-        prompt_key_slots,
-        weights,
-        lambda: project(
-            hidden,
-            attention_norm_gain[None, :],
-            query_key_value_weight,
-            jnp.cos(angles),
-            jnp.sin(angles),
-        ),
-        ranks,
-    )
-    head_rows, cached_values, pieces, partner_weights = lax.optimization_barrier(
-        (head.T, cached_values, pieces, partner_weights)
-    )
-    head_columns = lax.all_gather(head_rows, "seq", axis=0, tiled=True)
+    pair = start_pair(prompt_key_slots, prompt_value_slots)
+    partner_weights = partnered(weights, ranks)
+    line = lax.optimization_barrier(along_first(pair))
+    line = lax.optimization_barrier(jnp.concatenate(line))
+    ahead = [turned(line, 1, step) for step in (3, 2, 1)]
+    near = crossed(line)
+    qkv = project(
+        hidden,
+        attention_norm_gain[None, :],
+        query_key_value_weight,
+        jnp.cos(angles),
+        jnp.sin(angles),
+    )
+    ahead, qkv, head_columns = lax.optimization_barrier((ahead, qkv, head.T))
+    pieces = [line] + ahead + [near] + [crossed(piece) for piece in ahead]
+    half = head_columns.shape[0] // 2
+    head_pair = start_pair(head_columns[:half], head_columns[half:])
+    pieces, head_pair = lax.optimization_barrier((pieces, head_pair))
+    head_line = along_first(head_pair)
     attended = attend(
         jnp.stack([first, me // 8, me // 2 % 4, me % 2]).astype(jnp.int32),
         counts,
         page_slot_index,
         owner,
         qkv,
-        cached_values,
         pieces,
     )
     theirs = partnered(lax.dynamic_index_in_dim(attended, 1 - rank % 2, 0, False), ranks)
     own = lax.dynamic_index_in_dim(attended, rank % 2, 0, False)
+    theirs, head_line, partner_weights = lax.optimization_barrier(
+        (theirs, head_line, partner_weights)
+    )
+    head_line = lax.optimization_barrier(jnp.concatenate(head_line))
+    head_ahead = [turned(head_line, 1, 3), turned(head_line, 1, 1)]
     branch = jnp.dot(own, weights, preferred_element_type=F32)
     branch = branch + jnp.dot(theirs, partner_weights, preferred_element_type=F32)
-    branch = branch.astype(BF16)
+    parts, head_line, head_ahead = lax.optimization_barrier(
+        (reduce_rows(branch.astype(BF16), ranks), head_line, head_ahead)
+    )
     mine = settle(
         rank[None].astype(jnp.int32),
         hidden,
         adapter_up_weight,
         final_norm_gain[None, :],
-        *reduce_rows(branch, ranks),
+        *parts,
     )
     size = tok_rows // ranks
     half = size // 2
-    head_columns = pltpu.with_memory_space_constraint(head_columns, pltpu.HBM)
 
     def score_blocks(places, blocks):
         return score(
-            jnp.stack([rank] + places).astype(jnp.int32),
+            jnp.stack([rank, me // 8, me // 2 % 4, me % 2] + places).astype(jnp.int32),
             adapter_up_weight,
             final_norm_gain[None, :],
             targets[:, None],
-            head_columns,
+            head_pieces,
             blocks,
         )
 
@@ -508,9 +538,27 @@
     def place(offset):
         return (rank + offset) % ranks
 
-    near = [shifted(mine, ranks, step) for step in (-1, 1, -2, 2)]
-    near = lax.optimization_barrier(near)
-    _, _, after_two, before_two = near
+    head_opposite = turned(head_line, 1, 2)
+    after_one, before_one, line_swapped, first_swapped, third = lax.optimization_barrier(
+        (
+            shifted(mine, ranks, -1),
+            shifted(mine, ranks, 1),
+            crossed(head_line),
+            crossed(head_ahead[0]),
+            head_ahead[1],
+        )
+    )
+    after_two, before_two, head_opposite, third_swapped = lax.optimization_barrier(
+        (
+            shifted(after_one, ranks, -1),
+            shifted(before_one, ranks, 1),
+            head_opposite,
+            crossed(third),
+        )
+    )
+    near = [after_one, before_one, after_two, before_two]
+    head_pieces = [head_line, head_ahead[0], head_opposite, head_ahead[1]]
+    head_pieces += [line_swapped, first_swapped, crossed(head_opposite), third_swapped]
     far = [
         shifted(after_two, ranks, -1),
         shifted(before_two, ranks, 1),

time: 191 us -> 190 us (level)
  between operations: 14.6 us -> 1.14 us
  starting transfers between devices: 33.6 us -> 44.2 us
  other arithmetic: 5.36 us -> 10.2 us
  local copies, waits for them, and re-layouts: 9.31 us -> 6.75 us
    ppermute x6 -> x12, waiting for transfers between devices: 17.7 us -> 44.5 us  [turned(): return lax.ppermute(value, 'seq', [(i, target(i)) for i in range(32)])]
    all_gather x2 -> x0, waiting for transfers between devices: 18.1 us -> none  [the longest x1 10.7 us: local(): lax.all_gather(prompt_value_slots, 'seq', axis=0, tiled=True)]
    ppermute x2, waiting for transfers between devices: 13.3 us -> 3.23 us  [partnered(): return lax.ppermute(value, 'tensor', [(i, i ^ 1) for i in range(ranks)])]
    ppermute x5 -> x10, waiting for transfers between devices: 2.78 us -> 10.9 us  [crossed(): return lax.ppermute(value, 'seq', [(i, i ^ 1) for i in range(32)])]
    ppermute x11, waiting for transfers between devices: 27.4 us -> 20 us  [shifted(): lax.ppermute(value, 'tensor', [(i, (i + step) % ranks) for i in range(ran...]
    ppermute x6 -> x12, starting transfers between devices: 8.46 us -> 15.1 us  [turned(): return lax.ppermute(value, 'seq', [(i, target(i)) for i in range(32)])]
    concatenate x2 -> x4, other arithmetic: 0.15 us -> 3.83 us  [the longest x1 2.32 us: local(): head_line = lax.optimization_barrier(jnp.concatenate(head_line))]
    unnamed x33 -> x47, local copies, waits for them, and re-layouts: 7.53 us -> 4.99 us
  transfers between devices with their start and end apart: 26 -> 35, of which waited for: 20 -> 17; matrix products, arithmetic and copies ran while one was open for 5% -> 6% of each run, Pallas kernels for 10% -> 11%
where the time goes in v3:
time: 190 us
  waiting for transfers between devices  78.7 us (41%)
  starting transfers between devices  44.2 us (23%)
  Pallas kernels  29.5 us (16%)
  blocking collectives  14.6 us (8%)
  other arithmetic  10.2 us (5%)
  local copies, waits for them, and re-layouts  6.75 us (4%)
  matrix products  4.68 us (2%)
    ppermute x12, waiting for transfers between devices, turned(): return lax.ppermute(value, 'seq', [(i, target(i)) for i in range(32)])  44.5 us
    ppermute x11, starting transfers between devices, shifted(): lax.ppermute(value, 'tensor', [(i, (i + step) % ranks) for i in range(ran...  23.2 us
    ppermute x11, waiting for transfers between devices, shifted(): lax.ppermute(value, 'tensor', [(i, (i + step) % ranks) for i in range(ran...  20 us
    pallas_call x2, Pallas kernels, score(): pl.pallas_call(score_kernel, grid_spec=pltpu.PrefetchScalarGridSpec(num_s...  17.3 us
    ppermute x12, starting transfers between devices, turned(): return lax.ppermute(value, 'seq', [(i, target(i)) for i in range(32)])  15.1 us
    all_to_all x1, blocking collectives, local(): lax.all_to_all(jnp.broadcast_to(ordered[None], (ranks, 8, 2 * tok_rows)),...  14.6 us
    ppermute x10, waiting for transfers between devices, crossed(): return lax.ppermute(value, 'seq', [(i, i ^ 1) for i in range(32)])  10.9 us
    pallas_call x1, Pallas kernels, attend(): pl.pallas_call(attend_kernel, grid_spec=pltpu.PrefetchScalarGridSpec(num_...  7.2 us
  transfers between devices with their start and end apart: 35, of which 17 were waited for; matrix products, arithmetic and copies ran while one was open for 6% of the time, Pallas kernels for 11%

profile of v3, /device:TPU:24, one launch (start us, length us, event | category | flops | bytes accessed | tf_op | source)
XLA Modules:
  0.0 189.7 jit_solution(4460788550301943318)
XLA Ops:
  3.3 2.8 %collective-permute-start.1 = (bf16[4,128,384]{2,1,0:T(8,128)(2,1)S(1)}, bf16[4,128,384]{2,1,0:T(8,128)(2,1)S(1)}, u32[]{:S(2)}, u32[]{:S(2)}) collective-permute-start(bf16[4,128,384]{2,1,0:T(8,128)(2,1)S(1)} %pad_maximum_fusion.2), channel_id=1, source_target_pairs={{0,48},{8,200},{16,0},{24,216},{32,16},{40,232},{48,32},{56,248},{... | collective-permute-start | bytes 1179656 | tf_op jit(solution)/shard_map/ppermute | solution.py:425
  7.8 7.9 %collective-permute-done.1 = bf16[4,128,384]{2,1,0:T(8,128)(2,1)S(1)} collective-permute-done((bf16[4,128,384]{2,1,0:T(8,128)(2,1)S(1)}, bf16[4,128,384]{2,1,0:T(8,128)(2,1)S(1)}, u32[]{:S(2)}, u32[]{:S(2)}) %collective-permute-start.1) | collective-permute-done | bytes 393248 | tf_op jit(solution)/shard_map/ppermute | solution.py:425
  15.7 3.9 %collective-permute-done.3 = bf16[4,128,384]{2,1,0:T(8,128)(2,1)S(1)} collective-permute-done((bf16[4,128,384]{2,1,0:T(8,128)(2,1)S(1)}, bf16[4,128,384]{2,1,0:T(8,128)(2,1)S(1)}, u32[]{:S(2)}, u32[]{:S(2)}) %collective-permute-start.3) | collective-permute-done | bytes 393248 | tf_op jit(solution)/shard_map/ppermute | solution.py:425
  22.8 2.2 %collective-permute-start.6 = (bf16[16,128,384]{2,1,0:T(8,128)(2,1)}, bf16[16,128,384]{2,1,0:T(8,128)(2,1)}, u32[]{:S(2)}, u32[]{:S(2)}) collective-permute-start(bf16[16,128,384]{2,1,0:T(8,128)(2,1)} %pad_maximum_fusion.refs_5_), channel_id=1, source_target_pairs={{0,64},{8,24},{16,80},{24,40},{32,96},{40,56},{48,112},{56,8},{64,... | collective-permute-start | bytes 4718600 | tf_op jit(solution)/shard_map/ppermute | solution.py:425
  25.1 3.5 %fusion.2 = bf16[384,3200]{1,0:T(8,128)(2,1)} fusion(bf16[384,16]{1,0:T(8,128)(2,1)S(1)} %copy.54, bf16[384,3072]{1,0:T(8,128)(2,1)} %param.17), kind=kLoop, calls=%fused_computation.4 | loop fusion | flops 7372800 | bytes 4829184 | tf_op jit(solution)/shard_map/concatenate | solution.py:464
  32.4 3.0 %copy-done = bf16[3,3072,384]{2,1,0:T(8,128)(2,1)S(1)} copy-done((bf16[3,3072,384]{2,1,0:T(8,128)(2,1)S(1)}, bf16[3,3072,384]{2,1,0:T(8,128)(2,1)}, u32[]{:S(2)}) %copy-start) | copy-done | bytes 7077912
  35.4 4.6 %project.1.refs_4_ = bf16[3,256,384]{2,1,0:T(8,128)(2,1)S(1)} custom-call(bf16[256,3072]{1,0:T(8,128)(2,1)S(1)} %copy-done.1, bf16[1,3072]{1,0:T(2,128)(2,1)S(1)} %broadcast_in_dim.45.gain_ref, bf16[3,3072,384]{2,1,0:T(8,128)(2,1)S(1)} %copy-done, f32[256,384]{1,0:T(8,128)S(1)} %get-tuple-element.111.cos_ref, f32[256,384]{1,0:T(8,128)S(1)} %get-tuple-element.110.sin_ref), custom_call_target="tpu_custom_call" | custom-call | tf_op jit(solution)/shard_map/project/pallas_call | solution.py:58
  40.1 19.8 %collective-permute-done.4.refs_6_ = bf16[16,128,384]{2,1,0:T(8,128)(2,1)} collective-permute-done((bf16[16,128,384]{2,1,0:T(8,128)(2,1)}, bf16[16,128,384]{2,1,0:T(8,128)(2,1)}, u32[]{:S(2)}, u32[]{:S(2)}) %collective-permute-start.4) | collective-permute-done | bytes 1572896 | tf_op jit(solution)/shard_map/ppermute | solution.py:425
  62.5 2.3 %collective-permute-done.7.refs_9_ = bf16[16,128,384]{2,1,0:T(8,128)(2,1)S(1)} collective-permute-done((bf16[16,128,384]{2,1,0:T(8,128)(2,1)}, bf16[16,128,384]{2,1,0:T(8,128)(2,1)S(1)}, u32[]{:S(2)}, u32[]{:S(2)}) %collective-permute-start.7) | collective-permute-done | bytes 1572896 | tf_op jit(solution)/shard_map/ppermute | solution.py:413
  64.8 2.2 %collective-permute-done.10.refs_12_ = bf16[16,128,384]{2,1,0:T(8,128)(2,1)S(1)} collective-permute-done((bf16[16,128,384]{2,1,0:T(8,128)(2,1)}, bf16[16,128,384]{2,1,0:T(8,128)(2,1)S(1)}, u32[]{:S(2)}, u32[]{:S(2)}) %collective-permute-start.10) | collective-permute-done | bytes 1572896 | tf_op jit(solution)/shard_map/ppermute | solution.py:413
  67.0 2.2 %collective-permute-done.8.refs_10_ = bf16[16,128,384]{2,1,0:T(8,128)(2,1)S(1)} collective-permute-done((bf16[16,128,384]{2,1,0:T(8,128)(2,1)}, bf16[16,128,384]{2,1,0:T(8,128)(2,1)S(1)}, u32[]{:S(2)}, u32[]{:S(2)}) %collective-permute-start.8) | collective-permute-done | bytes 1572896 | tf_op jit(solution)/shard_map/ppermute | solution.py:413
  69.3 2.2 %collective-permute-done.9.refs_11_ = bf16[16,128,384]{2,1,0:T(8,128)(2,1)S(1)} collective-permute-done((bf16[16,128,384]{2,1,0:T(8,128)(2,1)}, bf16[16,128,384]{2,1,0:T(8,128)(2,1)S(1)}, u32[]{:S(2)}, u32[]{:S(2)}) %collective-permute-start.9) | collective-permute-done | bytes 1572896 | tf_op jit(solution)/shard_map/ppermute | solution.py:413
  73.9 7.2 %attend.1 = bf16[2,128,384]{2,1,0:T(8,128)(2,1)S(1)} custom-call(s32[4]{0:T(128)S(1)} %pad_add_fusion.refs_0_, s32[8]{0:T(128)S(1)} %copy-done.3, s32[64]{0:T(128)S(1)} %copy-done.4, s32[128]{0:T(128)S(1)} %copy-done.5, bf16[3,256,384]{2,1,0:T(8,128)(2,1)S(1)} %project.1.refs_4_, bf16[16,128,384]{2,1,0:T(8,128)(2,1)} %pad_maximum_fusion.refs_5_, ...), custom_call_target="tpu_custom_call" | custom-call | tf_op jit(solution)/shard_map/attend/pallas_call | solution.py:179
  81.2 2.0 %collective-permute-start.12 = (bf16[128,384]{1,0:T(8,128)(2,1)S(1)}, bf16[128,384]{1,0:T(8,128)(2,1)S(1)}, u32[]{:S(2)}, u32[]{:S(2)}) collective-permute-start(bf16[128,384]{1,0:T(8,128)(2,1)S(1)} %dynamic-slice_bitcast_fusion), channel_id=1, source_target_pairs={{0,1},{1,0},{2,3},{3,2},{4,5},{5,4},{6,7},{7,6},{8,9},{9,8},{10,11... | collective-permute-start | bytes 294920 | tf_op jit(solution)/shard_map/ppermute | solution.py:397
  83.2 3.2 %collective-permute-done.12 = bf16[128,384]{1,0:T(8,128)(2,1)S(1)} collective-permute-done((bf16[128,384]{1,0:T(8,128)(2,1)S(1)}, bf16[128,384]{1,0:T(8,128)(2,1)S(1)}, u32[]{:S(2)}, u32[]{:S(2)}) %collective-permute-start.12) | collective-permute-done | bytes 98336 | tf_op jit(solution)/shard_map/ppermute | solution.py:397
  87.0 2.3 %pad_maximum_fusion.1.refs_3_ = bf16[384,2048]{1,0:T(8,128)(2,1)} fusion(bf16[96,2048]{1,0:T(8,128)(2,1)} %collective-permute-done.15, bf16[96,2048]{1,0:T(8,128)(2,1)S(1)} %collective-permute-done.14, bf16[96,2048]{1,0:T(8,128)(2,1)S(1)} %collective-permute-done.13, bf16[96,2048]{1,0:T(8,128)(2,1)S(1)} %pad_maximum_fusion.3), kind=kLoop, calls=%fused_computation.6 | loop fusion | flops 6291456 | bytes 3145728 | tf_op jit(solution)/shard_map/concatenate | solution.py:507
  89.4 3.2 %collective-permute-start.21 = (bf16[384,2048]{1,0:T(8,128)(2,1)}, bf16[384,2048]{1,0:T(8,128)(2,1)}, u32[]{:S(2)}, u32[]{:S(2)}) collective-permute-start(bf16[384,2048]{1,0:T(8,128)(2,1)} %pad_maximum_fusion.1.refs_3_), channel_id=1, source_target_pairs={{0,64},{8,24},{16,80},{24,40},{32,96},{40,56},{48,112},{56,8},{64,... | collective-permute-start | bytes 4718600 | tf_op jit(solution)/shard_map/ppermute | solution.py:425
  92.6 2.3 %fusion.3 = f32[128,3200]{1,0:T(8,128)S(1)} fusion(bf16[2,128,384]{2,1,0:T(8,128)(2,1)S(1)} %attend.1, s32[]{:T(128)S(6)} %select_n.180, bf16[384,16]{1,0:T(8,128)(2,1)S(1)} %copy-done.16, bf16[384,3072]{1,0:T(8,128)(2,1)} %param.17), kind=kOutput, calls=%fused_computation.15 | convolution fusion | flops 321945600 | bytes 4194308 | tf_op jit(solution)/shard_map/dot_general | solution.py:509
  94.9 2.4 %fusion.1 = bf16[128,3200]{1,0:T(8,128)(2,1)S(1)} fusion(f32[128,3200]{1,0:T(8,128)S(1)} %fusion.3, bf16[128,384]{1,0:T(8,128)(2,1)S(1)} %copy-done.18, bf16[384,3200]{1,0:T(8,128)(2,1)} %collective-permute-done.16), kind=kOutput, calls=%fused_computation.3 | convolution fusion | flops 315392000 | bytes 5013504 | tf_op jit(solution)/shard_map/dot_general | solution.py:510
  97.4 7.5 %collective-permute-start.17 = (bf16[32,3200]{1,0:T(8,128)(2,1)S(1)}, bf16[32,3200]{1,0:T(8,128)(2,1)S(1)}, u32[]{:S(2)}, u32[]{:S(2)}) collective-permute-start(bf16[32,3200]{1,0:T(8,128)(2,1)S(1)} %get-tuple-element.96), channel_id=1, source_target_pairs={{0,4},{1,5},{2,6},{3,7},{4,0},{5,1},{6,2},{7,3},{8,12},{9,13},{10,... | collective-permute-start | bytes 614408 | tf_op jit(solution)/shard_map/ppermute | solution.py:393
  106.4 2.7 %collective-permute-start.19 = (bf16[32,3200]{1,0:T(8,128)(2,1)S(1)}, bf16[32,3200]{1,0:T(8,128)(2,1)S(1)}, u32[]{:S(2)}, u32[]{:S(2)}) collective-permute-start(bf16[32,3200]{1,0:T(8,128)(2,1)S(1)} %get-tuple-element.94), channel_id=1, source_target_pairs={{0,6},{1,7},{2,0},{3,1},{4,2},{5,3},{6,4},{7,5},{8,14},{9,15},{10,... | collective-permute-start | bytes 614408 | tf_op jit(solution)/shard_map/ppermute | solution.py:393
  109.0 6.3 %collective-permute-done.17.refs_1_ = bf16[32,3200]{1,0:T(8,128)(2,1)S(1)} collective-permute-done((bf16[32,3200]{1,0:T(8,128)(2,1)S(1)}, bf16[32,3200]{1,0:T(8,128)(2,1)S(1)}, u32[]{:S(2)}, u32[]{:S(2)}) %collective-permute-start.17) | collective-permute-done | bytes 204832 | tf_op jit(solution)/shard_map/ppermute | solution.py:393
  115.4 2.4 %collective-permute-done.18.refs_2_ = bf16[32,3200]{1,0:T(8,128)(2,1)S(1)} collective-permute-done((bf16[32,3200]{1,0:T(8,128)(2,1)S(1)}, bf16[32,3200]{1,0:T(8,128)(2,1)S(1)}, u32[]{:S(2)}, u32[]{:S(2)}) %collective-permute-start.18) | collective-permute-done | bytes 204832 | tf_op jit(solution)/shard_map/ppermute | solution.py:393
  117.8 4.5 %collective-permute-done.19.refs_3_ = bf16[32,3200]{1,0:T(8,128)(2,1)S(1)} collective-permute-done((bf16[32,3200]{1,0:T(8,128)(2,1)S(1)}, bf16[32,3200]{1,0:T(8,128)(2,1)S(1)}, u32[]{:S(2)}, u32[]{:S(2)}) %collective-permute-start.19) | collective-permute-done | bytes 204832 | tf_op jit(solution)/shard_map/ppermute | solution.py:393
  123.3 3.1 %collective-permute-start.22 = (bf16[32,3200]{1,0:T(8,128)(2,1)S(1)}, bf16[32,3200]{1,0:T(8,128)(2,1)S(1)}, u32[]{:S(2)}, u32[]{:S(2)}) collective-permute-start(bf16[32,3200]{1,0:T(8,128)(2,1)S(1)} %settle.1.refs_12_), channel_id=1, source_target_pairs={{0,7},{1,0},{2,1},{3,2},{4,3},{5,4},{6,5},{7,6},{8,15},{9,8},{10,9... | collective-permute-start | bytes 614408 | tf_op jit(solution)/shard_map/ppermute | solution.py:393
  127.7 3.4 %collective-permute-done.22.refs_14_ = bf16[32,3200]{1,0:T(8,128)(2,1)S(1)} collective-permute-done((bf16[32,3200]{1,0:T(8,128)(2,1)S(1)}, bf16[32,3200]{1,0:T(8,128)(2,1)S(1)}, u32[]{:S(2)}, u32[]{:S(2)}) %collective-permute-start.22) | collective-permute-done | bytes 204832 | tf_op jit(solution)/shard_map/ppermute | solution.py:393
  131.0 3.4 %collective-permute-done.23.refs_16_ = bf16[32,3200]{1,0:T(8,128)(2,1)S(1)} collective-permute-done((bf16[32,3200]{1,0:T(8,128)(2,1)S(1)}, bf16[32,3200]{1,0:T(8,128)(2,1)S(1)}, u32[]{:S(2)}, u32[]{:S(2)}) %collective-permute-start.23) | collective-permute-done | bytes 204832 | tf_op jit(solution)/shard_map/ppermute | solution.py:393
  136.7 12.0 %collective-permute-done.28.refs_5_ = bf16[384,2048]{1,0:T(8,128)(2,1)} collective-permute-done((bf16[384,2048]{1,0:T(8,128)(2,1)}, bf16[384,2048]{1,0:T(8,128)(2,1)}, u32[]{:S(2)}, u32[]{:S(2)}) %collective-permute-start.28) | collective-permute-done | bytes 1572896 | tf_op jit(solution)/shard_map/ppermute | solution.py:425
  150.2 3.2 %collective-permute-start.30 = (bf16[32,3200]{1,0:T(8,128)(2,1)S(1)}, bf16[32,3200]{1,0:T(8,128)(2,1)S(1)}, u32[]{:S(2)}, u32[]{:S(2)}) collective-permute-start(bf16[32,3200]{1,0:T(8,128)(2,1)S(1)} %collective-permute-done.26.refs_18_), channel_id=1, source_target_pairs={{0,7},{1,0},{2,1},{3,2},{4,3},{5,4},{6,5},{7,6},{8,15},{9,8},{10,9... | collective-permute-start | bytes 614408 | tf_op jit(solution)/shard_map/ppermute | solution.py:393
  156.6 9.1 %score.2 = f32[8,320]{1,0:T(8,128)S(1)} custom-call(s32[9]{0:T(128)S(1)} %stack.70.refs_0_, bf16[16,3072]{1,0:T(8,128)(2,1)S(1)} %copy-done.2, bf16[1,3072]{1,0:T(2,128)(2,1)S(1)} %broadcast_in_dim.44.gain_ref.refs_2_, bf16[384,2048]{1,0:T(8,128)(2,1)} %pad_maximum_fusion.1.refs_3_, bf16[384,2048]{1,0:T(8,128)(2,1)} %copy-done.6, ...), custom_call_target="tpu_custom_call" | custom-call | flops 4026531840 | bytes 12582912 | tf_op jit(solution)/shard_map/score/pallas_call | solution.py:360
  165.8 8.2 %score.3 = f32[8,192]{1,0:T(8,128)S(1)} custom-call(s32[8]{0:T(128)S(1)} %stack.75.refs_0_, bf16[16,3072]{1,0:T(8,128)(2,1)S(1)} %copy-done.2, bf16[1,3072]{1,0:T(2,128)(2,1)S(1)} %broadcast_in_dim.44.gain_ref.refs_2_, bf16[384,2048]{1,0:T(8,128)(2,1)} %pad_maximum_fusion.1.refs_3_, bf16[384,2048]{1,0:T(8,128)(2,1)} %copy-done.6, ...), custom_call_target="tpu_custom_call" | custom-call | flops 2415919104 | bytes 12582912 | tf_op jit(solution)/shard_map/score/pallas_call | solution.py:360
  174.5 14.6 %all_to_all.5 = f32[8,8,512]{2,1,0:T(8,128)S(1)} all-to-all(f32[8,8,512]{2,1,0:T(8,128)S(1)} %broadcast_in_dim.51), channel_id=1, replica_groups=mesh['seq'=32,'tensor'=8] {'tensor'}, dimensions={0} | all-to-all | bytes 262144 | tf_op jit(solution)/shard_map/all_to_all | solution.py:577
  (130 shorter events, 28.9 us)
Async XLA Ops:
  3.3 12.4 %collective-permute-start.1 = (bf16[4,128,384]{2,1,0:T(8,128)(2,1)S(1)}, bf16[4,128,384]{2,1,0:T(8,128)(2,1)S(1)}, u32[]{:S(2)}, u32[]{:S(2)}) collective-permute-start(bf16[4,128,384]{2,1,0:T(8,128)(2,1)S(1)} %pad_maximum_fusion.2), channel_id=1, source_target_pairs={{0,48},{8,200},{16,0},{24,216},{32,16},{40,232},{48,32},{56,248},{... | collective-permute-start | bytes 1179656 | tf_op jit(solution)/shard_map/ppermute | solution.py:425
  6.1 9.5 %collective-permute-start.2 = (bf16[4,128,384]{2,1,0:T(8,128)(2,1)S(1)}, bf16[4,128,384]{2,1,0:T(8,128)(2,1)S(1)}, u32[]{:S(2)}, u32[]{:S(2)}) collective-permute-start(bf16[4,128,384]{2,1,0:T(8,128)(2,1)S(1)} %pad_maximum_fusion.2), channel_id=1, source_target_pairs={{0,32},{8,136},{16,48},{24,152},{32,0},{40,168},{48,16},{56,184},{... | collective-permute-start | bytes 1179656 | tf_op jit(solution)/shard_map/ppermute | solution.py:425
  6.9 12.7 %collective-permute-start.3 = (bf16[4,128,384]{2,1,0:T(8,128)(2,1)S(1)}, bf16[4,128,384]{2,1,0:T(8,128)(2,1)S(1)}, u32[]{:S(2)}, u32[]{:S(2)}) collective-permute-start(bf16[4,128,384]{2,1,0:T(8,128)(2,1)S(1)} %pad_maximum_fusion.2), channel_id=1, source_target_pairs={{0,16},{8,72},{16,32},{24,88},{32,48},{40,104},{48,0},{56,120},{64... | collective-permute-start | bytes 1179656 | tf_op jit(solution)/shard_map/ppermute | solution.py:425
  21.1 38.8 %collective-permute-start.4 = (bf16[16,128,384]{2,1,0:T(8,128)(2,1)}, bf16[16,128,384]{2,1,0:T(8,128)(2,1)}, u32[]{:S(2)}, u32[]{:S(2)}) collective-permute-start(bf16[16,128,384]{2,1,0:T(8,128)(2,1)} %pad_maximum_fusion.refs_5_), channel_id=1, source_target_pairs={{0,192},{8,56},{16,208},{24,8},{32,224},{40,24},{48,240},{56,40},{... | collective-permute-start | bytes 4718600 | tf_op jit(solution)/shard_map/ppermute | solution.py:425
  21.8 38.1 %collective-permute-start.5 = (bf16[16,128,384]{2,1,0:T(8,128)(2,1)}, bf16[16,128,384]{2,1,0:T(8,128)(2,1)}, u32[]{:S(2)}, u32[]{:S(2)}) collective-permute-start(bf16[16,128,384]{2,1,0:T(8,128)(2,1)} %pad_maximum_fusion.refs_5_), channel_id=1, source_target_pairs={{0,128},{8,40},{16,144},{24,56},{32,160},{40,8},{48,176},{56,24},{... | collective-permute-start | bytes 4718600 | tf_op jit(solution)/shard_map/ppermute | solution.py:425
  22.8 38.0 %collective-permute-start.6 = (bf16[16,128,384]{2,1,0:T(8,128)(2,1)}, bf16[16,128,384]{2,1,0:T(8,128)(2,1)}, u32[]{:S(2)}, u32[]{:S(2)}) collective-permute-start(bf16[16,128,384]{2,1,0:T(8,128)(2,1)} %pad_maximum_fusion.refs_5_), channel_id=1, source_target_pairs={{0,64},{8,24},{16,80},{24,40},{32,96},{40,56},{48,112},{56,8},{64,... | collective-permute-start | bytes 4718600 | tf_op jit(solution)/shard_map/ppermute | solution.py:425
  28.6 54.6 %collective-permute-start.16 = (bf16[384,3200]{1,0:T(8,128)(2,1)}, bf16[384,3200]{1,0:T(8,128)(2,1)}, u32[]{:S(2)}, u32[]{:S(2)}) collective-permute-start(bf16[384,3200]{1,0:T(8,128)(2,1)} %fusion.2), channel_id=1, source_target_pairs={{0,1},{1,0},{2,3},{3,2},{4,5},{5,4},{6,7},{7,6},{8,9},{9,8},{10,11... | collective-permute-start | bytes 7372808 | tf_op jit(solution)/shard_map/ppermute | solution.py:397
  61.4 5.6 %collective-permute-start.10 = (bf16[16,128,384]{2,1,0:T(8,128)(2,1)}, bf16[16,128,384]{2,1,0:T(8,128)(2,1)S(1)}, u32[]{:S(2)}, u32[]{:S(2)}) collective-permute-start(bf16[16,128,384]{2,1,0:T(8,128)(2,1)} %collective-permute-done.6.refs_8_), channel_id=1, source_target_pairs={{0,8},{8,0},{16,24},{24,16},{32,40},{40,32},{48,56},{56,48},{64,72... | collective-permute-start | bytes 4718600 | tf_op jit(solution)/shard_map/ppermute | solution.py:413
  61.5 7.8 %collective-permute-start.8 = (bf16[16,128,384]{2,1,0:T(8,128)(2,1)}, bf16[16,128,384]{2,1,0:T(8,128)(2,1)S(1)}, u32[]{:S(2)}, u32[]{:S(2)}) collective-permute-start(bf16[16,128,384]{2,1,0:T(8,128)(2,1)} %collective-permute-done.4.refs_6_), channel_id=1, source_target_pairs={{0,8},{8,0},{16,24},{24,16},{32,40},{40,32},{48,56},{56,48},{64,72... | collective-permute-start | bytes 4718600 | tf_op jit(solution)/shard_map/ppermute | solution.py:413
  62.3 9.2 %collective-permute-start.9 = (bf16[16,128,384]{2,1,0:T(8,128)(2,1)}, bf16[16,128,384]{2,1,0:T(8,128)(2,1)S(1)}, u32[]{:S(2)}, u32[]{:S(2)}) collective-permute-start(bf16[16,128,384]{2,1,0:T(8,128)(2,1)} %collective-permute-done.5.refs_7_), channel_id=1, source_target_pairs={{0,8},{8,0},{16,24},{24,16},{32,40},{40,32},{48,56},{56,48},{64,72... | collective-permute-start | bytes 4718600 | tf_op jit(solution)/shard_map/ppermute | solution.py:413
  71.5 14.9 %collective-permute-start.13 = (bf16[96,2048]{1,0:T(8,128)(2,1)S(1)}, bf16[96,2048]{1,0:T(8,128)(2,1)S(1)}, u32[]{:S(2)}, u32[]{:S(2)}) collective-permute-start(bf16[96,2048]{1,0:T(8,128)(2,1)S(1)} %pad_maximum_fusion.3), channel_id=1, source_target_pairs={{0,48},{8,200},{16,0},{24,216},{32,16},{40,232},{48,32},{56,248},{... | collective-permute-start | bytes 1179656 | tf_op jit(solution)/shard_map/ppermute | solution.py:425
  72.2 14.3 %collective-permute-start.14 = (bf16[96,2048]{1,0:T(8,128)(2,1)S(1)}, bf16[96,2048]{1,0:T(8,128)(2,1)S(1)}, u32[]{:S(2)}, u32[]{:S(2)}) collective-permute-start(bf16[96,2048]{1,0:T(8,128)(2,1)S(1)} %pad_maximum_fusion.3), channel_id=1, source_target_pairs={{0,32},{8,136},{16,48},{24,152},{32,0},{40,168},{48,16},{56,184},{... | collective-permute-start | bytes 1179656 | tf_op jit(solution)/shard_map/ppermute | solution.py:425
  73.0 13.5 %collective-permute-start.15 = (bf16[96,2048]{1,0:T(8,128)(2,1)S(1)}, bf16[96,2048]{1,0:T(8,128)(2,1)}, u32[]{:S(2)}, u32[]{:S(2)}) collective-permute-start(bf16[96,2048]{1,0:T(8,128)(2,1)S(1)} %pad_maximum_fusion.3), channel_id=1, source_target_pairs={{0,16},{8,72},{16,32},{24,88},{32,48},{40,104},{48,0},{56,120},{64... | collective-permute-start | bytes 1179656 | tf_op jit(solution)/shard_map/ppermute | solution.py:425
  81.2 5.2 %collective-permute-start.12 = (bf16[128,384]{1,0:T(8,128)(2,1)S(1)}, bf16[128,384]{1,0:T(8,128)(2,1)S(1)}, u32[]{:S(2)}, u32[]{:S(2)}) collective-permute-start(bf16[128,384]{1,0:T(8,128)(2,1)S(1)} %dynamic-slice_bitcast_fusion), channel_id=1, source_target_pairs={{0,1},{1,0},{2,3},{3,2},{4,5},{5,4},{6,7},{7,6},{8,9},{9,8},{10,11... | collective-permute-start | bytes 294920 | tf_op jit(solution)/shard_map/ppermute | solution.py:397
  89.4 32.9 %collective-permute-start.20 = (bf16[384,2048]{1,0:T(8,128)(2,1)}, bf16[384,2048]{1,0:T(8,128)(2,1)S(1)}, u32[]{:S(2)}, u32[]{:S(2)}) collective-permute-start(bf16[384,2048]{1,0:T(8,128)(2,1)} %pad_maximum_fusion.1.refs_3_), channel_id=1, source_target_pairs={{0,192},{8,56},{16,208},{24,8},{32,224},{40,24},{48,240},{56,40},{... | collective-permute-start | bytes 4718600 | tf_op jit(solution)/shard_map/ppermute | solution.py:425
  89.4 32.9 %collective-permute-start.21 = (bf16[384,2048]{1,0:T(8,128)(2,1)}, bf16[384,2048]{1,0:T(8,128)(2,1)}, u32[]{:S(2)}, u32[]{:S(2)}) collective-permute-start(bf16[384,2048]{1,0:T(8,128)(2,1)} %pad_maximum_fusion.1.refs_3_), channel_id=1, source_target_pairs={{0,64},{8,24},{16,80},{24,40},{32,96},{40,56},{48,112},{56,8},{64,... | collective-permute-start | bytes 4718600 | tf_op jit(solution)/shard_map/ppermute | solution.py:425
  97.4 17.9 %collective-permute-start.17 = (bf16[32,3200]{1,0:T(8,128)(2,1)S(1)}, bf16[32,3200]{1,0:T(8,128)(2,1)S(1)}, u32[]{:S(2)}, u32[]{:S(2)}) collective-permute-start(bf16[32,3200]{1,0:T(8,128)(2,1)S(1)} %get-tuple-element.96), channel_id=1, source_target_pairs={{0,4},{1,5},{2,6},{3,7},{4,0},{5,1},{6,2},{7,3},{8,12},{9,13},{10,... | collective-permute-start | bytes 614408 | tf_op jit(solution)/shard_map/ppermute | solution.py:393
  104.9 12.9 %collective-permute-start.18 = (bf16[32,3200]{1,0:T(8,128)(2,1)S(1)}, bf16[32,3200]{1,0:T(8,128)(2,1)S(1)}, u32[]{:S(2)}, u32[]{:S(2)}) collective-permute-start(bf16[32,3200]{1,0:T(8,128)(2,1)S(1)} %get-tuple-element.95), channel_id=1, source_target_pairs={{0,2},{1,3},{2,4},{3,5},{4,6},{5,7},{6,0},{7,1},{8,10},{9,11},{10,... | collective-permute-start | bytes 614408 | tf_op jit(solution)/shard_map/ppermute | solution.py:393
  106.4 15.9 %collective-permute-start.19 = (bf16[32,3200]{1,0:T(8,128)(2,1)S(1)}, bf16[32,3200]{1,0:T(8,128)(2,1)S(1)}, u32[]{:S(2)}, u32[]{:S(2)}) collective-permute-start(bf16[32,3200]{1,0:T(8,128)(2,1)S(1)} %get-tuple-element.94), channel_id=1, source_target_pairs={{0,6},{1,7},{2,0},{3,1},{4,2},{5,3},{6,4},{7,5},{8,14},{9,15},{10,... | collective-permute-start | bytes 614408 | tf_op jit(solution)/shard_map/ppermute | solution.py:393
  122.3 12.2 %collective-permute-start.24 = (bf16[384,2048]{1,0:T(8,128)(2,1)}, bf16[384,2048]{1,0:T(8,128)(2,1)S(1)}, u32[]{:S(2)}, u32[]{:S(2)}) collective-permute-start(bf16[384,2048]{1,0:T(8,128)(2,1)} %pad_maximum_fusion.1.refs_3_), channel_id=1, source_target_pairs={{0,8},{8,0},{16,24},{24,16},{32,40},{40,32},{48,56},{56,48},{64,72... | collective-permute-start | bytes 4718600 | tf_op jit(solution)/shard_map/ppermute | solution.py:413
  122.4 12.1 %collective-permute-start.25 = (bf16[384,2048]{1,0:T(8,128)(2,1)S(1)}, bf16[384,2048]{1,0:T(8,128)(2,1)S(1)}, u32[]{:S(2)}, u32[]{:S(2)}) collective-permute-start(bf16[384,2048]{1,0:T(8,128)(2,1)S(1)} %collective-permute-done.20.refs_4_), channel_id=1, source_target_pairs={{0,8},{8,0},{16,24},{24,16},{32,40},{40,32},{48,56},{56,48},{64,72... | collective-permute-start | bytes 4718600 | tf_op jit(solution)/shard_map/ppermute | solution.py:413
  123.3 7.7 %collective-permute-start.22 = (bf16[32,3200]{1,0:T(8,128)(2,1)S(1)}, bf16[32,3200]{1,0:T(8,128)(2,1)S(1)}, u32[]{:S(2)}, u32[]{:S(2)}) collective-permute-start(bf16[32,3200]{1,0:T(8,128)(2,1)S(1)} %settle.1.refs_12_), channel_id=1, source_target_pairs={{0,7},{1,0},{2,1},{3,2},{4,3},{5,4},{6,5},{7,6},{8,15},{9,8},{10,9... | collective-permute-start | bytes 614408 | tf_op jit(solution)/shard_map/ppermute | solution.py:393
  126.4 8.0 %collective-permute-start.23 = (bf16[32,3200]{1,0:T(8,128)(2,1)S(1)}, bf16[32,3200]{1,0:T(8,128)(2,1)S(1)}, u32[]{:S(2)}, u32[]{:S(2)}) collective-permute-start(bf16[32,3200]{1,0:T(8,128)(2,1)S(1)} %settle.1.refs_12_), channel_id=1, source_target_pairs={{0,1},{1,2},{2,3},{3,4},{4,5},{5,6},{6,7},{7,0},{8,9},{9,10},{10,1... | collective-permute-start | bytes 614408 | tf_op jit(solution)/shard_map/ppermute | solution.py:393
  126.4 22.2 %collective-permute-start.28 = (bf16[384,2048]{1,0:T(8,128)(2,1)}, bf16[384,2048]{1,0:T(8,128)(2,1)}, u32[]{:S(2)}, u32[]{:S(2)}) collective-permute-start(bf16[384,2048]{1,0:T(8,128)(2,1)} %pad_maximum_fusion.1.refs_3_), channel_id=1, source_target_pairs={{0,128},{8,40},{16,144},{24,56},{32,160},{40,8},{48,176},{56,24},{... | collective-permute-start | bytes 4718600 | tf_op jit(solution)/shard_map/ppermute | solution.py:425
  134.5 14.2 %collective-permute-start.29 = (bf16[384,2048]{1,0:T(8,128)(2,1)}, bf16[384,2048]{1,0:T(8,128)(2,1)S(1)}, u32[]{:S(2)}, u32[]{:S(2)}) collective-permute-start(bf16[384,2048]{1,0:T(8,128)(2,1)} %collective-permute-done.21.refs_6_), channel_id=1, source_target_pairs={{0,8},{8,0},{16,24},{24,16},{32,40},{40,32},{48,56},{56,48},{64,72... | collective-permute-start | bytes 4718600 | tf_op jit(solution)/shard_map/ppermute | solution.py:413
  134.6 14.1 %collective-permute-start.26 = (bf16[32,3200]{1,0:T(8,128)(2,1)S(1)}, bf16[32,3200]{1,0:T(8,128)(2,1)S(1)}, u32[]{:S(2)}, u32[]{:S(2)}) collective-permute-start(bf16[32,3200]{1,0:T(8,128)(2,1)S(1)} %collective-permute-done.22.refs_14_), channel_id=1, source_target_pairs={{0,7},{1,0},{2,1},{3,2},{4,3},{5,4},{6,5},{7,6},{8,15},{9,8},{10,9... | collective-permute-start | bytes 614408 | tf_op jit(solution)/shard_map/ppermute | solution.py:393
  134.9 13.7 %collective-permute-start.27 = (bf16[32,3200]{1,0:T(8,128)(2,1)S(1)}, bf16[32,3200]{1,0:T(8,128)(2,1)S(1)}, u32[]{:S(2)}, u32[]{:S(2)}) collective-permute-start(bf16[32,3200]{1,0:T(8,128)(2,1)S(1)} %collective-permute-done.23.refs_16_), channel_id=1, source_target_pairs={{0,1},{1,2},{2,3},{3,4},{4,5},{5,6},{6,7},{7,0},{8,9},{9,10},{10,1... | collective-permute-start | bytes 614408 | tf_op jit(solution)/shard_map/ppermute | solution.py:393
  149.9 6.7 %collective-permute-start.34 = (bf16[384,2048]{1,0:T(8,128)(2,1)}, bf16[384,2048]{1,0:T(8,128)(2,1)}, u32[]{:S(2)}, u32[]{:S(2)}) collective-permute-start(bf16[384,2048]{1,0:T(8,128)(2,1)} %collective-permute-done.28.refs_5_), channel_id=1, source_target_pairs={{0,8},{8,0},{16,24},{24,16},{32,40},{40,32},{48,56},{56,48},{64,72... | collective-permute-start | bytes 4718600 | tf_op jit(solution)/shard_map/ppermute | solution.py:413
  150.2 15.5 %collective-permute-start.30 = (bf16[32,3200]{1,0:T(8,128)(2,1)S(1)}, bf16[32,3200]{1,0:T(8,128)(2,1)S(1)}, u32[]{:S(2)}, u32[]{:S(2)}) collective-permute-start(bf16[32,3200]{1,0:T(8,128)(2,1)S(1)} %collective-permute-done.26.refs_18_), channel_id=1, source_target_pairs={{0,7},{1,0},{2,1},{3,2},{4,3},{5,4},{6,5},{7,6},{8,15},{9,8},{10,9... | collective-permute-start | bytes 614408 | tf_op jit(solution)/shard_map/ppermute | solution.py:393
  153.5 12.3 %collective-permute-start.31 = (bf16[32,3200]{1,0:T(8,128)(2,1)S(1)}, bf16[32,3200]{1,0:T(8,128)(2,1)S(1)}, u32[]{:S(2)}, u32[]{:S(2)}) collective-permute-start(bf16[32,3200]{1,0:T(8,128)(2,1)S(1)} %collective-permute-done.27.refs_20_), channel_id=1, source_target_pairs={{0,1},{1,2},{2,3},{3,4},{4,5},{5,6},{6,7},{7,0},{8,9},{9,10},{10,1... | collective-permute-start | bytes 614408 | tf_op jit(solution)/shard_map/ppermute | solution.py:393
  153.6 12.1 %collective-permute-start.32 = (bf16[16,3200]{1,0:T(8,128)(2,1)S(1)}, bf16[16,3200]{1,0:T(8,128)(2,1)S(1)}, u32[]{:S(2)}, u32[]{:S(2)}) collective-permute-start(bf16[16,3200]{1,0:T(8,128)(2,1)S(1)} %slice.53), channel_id=1, source_target_pairs={{0,6},{1,7},{2,0},{3,1},{4,2},{5,3},{6,4},{7,5},{8,14},{9,15},{10,... | collective-permute-start | bytes 307208 | tf_op jit(solution)/shard_map/ppermute | solution.py:393
  155.3 10.4 %collective-permute-start.33 = (bf16[16,3200]{1,0:T(8,128)(2,1)S(1)}, bf16[16,3200]{1,0:T(8,128)(2,1)S(1)}, u32[]{:S(2)}, u32[]{:S(2)}) collective-permute-start(bf16[16,3200]{1,0:T(8,128)(2,1)S(1)} %slice.54), channel_id=1, source_target_pairs={{0,2},{1,3},{2,4},{3,5},{4,6},{5,7},{6,0},{7,1},{8,10},{9,11},{10,... | collective-permute-start | bytes 307208 | tf_op jit(solution)/shard_map/ppermute | solution.py:393
  (26 other events, 330.8 us)

commit v4 on v3

--- a/solution.py
+++ b/solution.py
@@ -485,11 +485,10 @@
         jnp.cos(angles),
         jnp.sin(angles),
     )
-    ahead, qkv, head_columns = lax.optimization_barrier((ahead, qkv, head.T))
+    ahead, near, qkv, head_columns = lax.optimization_barrier((ahead, near, qkv, head.T))
     pieces = [line] + ahead + [near] + [crossed(piece) for piece in ahead]
     half = head_columns.shape[0] // 2
     head_pair = start_pair(head_columns[:half], head_columns[half:])
-    pieces, head_pair = lax.optimization_barrier((pieces, head_pair))
     head_line = along_first(head_pair)
     attended = attend(
         jnp.stack([first, me // 8, me // 2 % 4, me % 2]).astype(jnp.int32),
@@ -500,17 +499,17 @@
         pieces,
     )
     theirs = partnered(lax.dynamic_index_in_dim(attended, 1 - rank % 2, 0, False), ranks)
+    attended, head_line, partner_weights = lax.optimization_barrier(
+        (attended, head_line, partner_weights)
+    )
     own = lax.dynamic_index_in_dim(attended, rank % 2, 0, False)
-    theirs, head_line, partner_weights = lax.optimization_barrier(
-        (theirs, head_line, partner_weights)
-    )
     head_line = lax.optimization_barrier(jnp.concatenate(head_line))
     head_ahead = [turned(head_line, 1, 3), turned(head_line, 1, 1)]
     branch = jnp.dot(own, weights, preferred_element_type=F32)
     branch = branch + jnp.dot(theirs, partner_weights, preferred_element_type=F32)
-    parts, head_line, head_ahead = lax.optimization_barrier(
-        (reduce_rows(branch.astype(BF16), ranks), head_line, head_ahead)
-    )
+    parts = reduce_rows(branch.astype(BF16), ranks)
+    parts, head_line, head_ahead = lax.optimization_barrier((parts, head_line, head_ahead))
+    head_opposite = turned(head_line, 1, 2)
     mine = settle(
         rank[None].astype(jnp.int32),
         hidden,
@@ -538,7 +537,6 @@
     def place(offset):
         return (rank + offset) % ranks
 
-    head_opposite = turned(head_line, 1, 2)
     after_one, before_one, line_swapped, first_swapped, third = lax.optimization_barrier(
         (
             shifted(mine, ranks, -1),

time: 190 us -> 190 us (level)
    ppermute x2, waiting for transfers between devices: 3.23 us -> 9.17 us  [partnered(): return lax.ppermute(value, 'tensor', [(i, i ^ 1) for i in range(ranks)])]
    ppermute x10, waiting for transfers between devices: 10.9 us -> 6.66 us  [crossed(): return lax.ppermute(value, 'seq', [(i, i ^ 1) for i in range(32)])]
    ppermute x11, waiting for transfers between devices: 20 us -> 17.8 us  [shifted(): lax.ppermute(value, 'tensor', [(i, (i + step) % ranks) for i in range(ran...]
    unnamed x47 -> x39, local copies, waits for them, and re-layouts: 4.99 us -> 5.9 us
  transfers between devices with their start and end apart: 35 -> 35, of which waited for: 17 -> 15; matrix products, arithmetic and copies ran while one was open for 6% -> 6% of each run, Pallas kernels for 11% -> 11%
where the time goes in v4:
time: 190 us; the launch traced here: 188 us
  waiting for transfers between devices  78.2 us (41%)
  starting transfers between devices  44 us (23%)
  Pallas kernels  28 us (15%)
  blocking collectives  14.6 us (8%)
  other arithmetic  10.2 us (5%)
  local copies, waits for them, and re-layouts  7.65 us (4%)
  matrix products  4.6 us (2%)
    ppermute x12, waiting for transfers between devices, turned(): return lax.ppermute(value, 'seq', [(i, target(i)) for i in range(32)])  44.6 us
    ppermute x11, starting transfers between devices, shifted(): lax.ppermute(value, 'tensor', [(i, (i + step) % ranks) for i in range(ran...  22.8 us
    ppermute x11, waiting for transfers between devices, shifted(): lax.ppermute(value, 'tensor', [(i, (i + step) % ranks) for i in range(ran...  17.8 us
    pallas_call x2, Pallas kernels, score(): pl.pallas_call(score_kernel, grid_spec=pltpu.PrefetchScalarGridSpec(num_s...  17.3 us
    ppermute x12, starting transfers between devices, turned(): return lax.ppermute(value, 'seq', [(i, target(i)) for i in range(32)])  15.4 us
    all_to_all x1, blocking collectives, local(): lax.all_to_all(jnp.broadcast_to(ordered[None], (ranks, 8, 2 * tok_rows)),...  14.6 us
    ppermute x2, waiting for transfers between devices, partnered(): return lax.ppermute(value, 'tensor', [(i, i ^ 1) for i in range(ranks)])  9.17 us
    ppermute x10, waiting for transfers between devices, crossed(): return lax.ppermute(value, 'seq', [(i, i ^ 1) for i in range(32)])  6.66 us
  transfers between devices with their start and end apart: 35, of which 15 were waited for; matrix products, arithmetic and copies ran while one was open for 6% of the time, Pallas kernels for 11%

profile of v4, /device:TPU:24, one launch (start us, length us, event | category | flops | bytes accessed | tf_op | source)
XLA Modules:
  0.0 188.4 jit_solution(12075560035183709294)
XLA Ops:
  3.3 2.8 %collective-permute-start.1 = (bf16[4,128,384]{2,1,0:T(8,128)(2,1)S(1)}, bf16[4,128,384]{2,1,0:T(8,128)(2,1)S(1)}, u32[]{:S(2)}, u32[]{:S(2)}) collective-permute-start(bf16[4,128,384]{2,1,0:T(8,128)(2,1)S(1)} %pad_maximum_fusion.2), channel_id=1, source_target_pairs={{0,48},{8,200},{16,0},{24,216},{32,16},{40,232},{48,32},{56,248},{... | collective-permute-start | bytes 1179656 | tf_op jit(solution)/shard_map/ppermute | solution.py:425
  7.8 7.9 %collective-permute-done.1 = bf16[4,128,384]{2,1,0:T(8,128)(2,1)S(1)} collective-permute-done((bf16[4,128,384]{2,1,0:T(8,128)(2,1)S(1)}, bf16[4,128,384]{2,1,0:T(8,128)(2,1)S(1)}, u32[]{:S(2)}, u32[]{:S(2)}) %collective-permute-start.1) | collective-permute-done | bytes 393248 | tf_op jit(solution)/shard_map/ppermute | solution.py:425
  15.7 3.9 %collective-permute-done.3 = bf16[4,128,384]{2,1,0:T(8,128)(2,1)S(1)} collective-permute-done((bf16[4,128,384]{2,1,0:T(8,128)(2,1)S(1)}, bf16[4,128,384]{2,1,0:T(8,128)(2,1)S(1)}, u32[]{:S(2)}, u32[]{:S(2)}) %collective-permute-start.3) | collective-permute-done | bytes 393248 | tf_op jit(solution)/shard_map/ppermute | solution.py:425
  22.8 2.2 %collective-permute-start.6 = (bf16[16,128,384]{2,1,0:T(8,128)(2,1)}, bf16[16,128,384]{2,1,0:T(8,128)(2,1)}, u32[]{:S(2)}, u32[]{:S(2)}) collective-permute-start(bf16[16,128,384]{2,1,0:T(8,128)(2,1)} %pad_maximum_fusion.refs_5_), channel_id=1, source_target_pairs={{0,64},{8,24},{16,80},{24,40},{32,96},{40,56},{48,112},{56,8},{64,... | collective-permute-start | bytes 4718600 | tf_op jit(solution)/shard_map/ppermute | solution.py:425
  25.1 3.5 %fusion.2 = bf16[384,3200]{1,0:T(8,128)(2,1)} fusion(bf16[384,16]{1,0:T(8,128)(2,1)S(1)} %copy.54, bf16[384,3072]{1,0:T(8,128)(2,1)} %param.17), kind=kLoop, calls=%fused_computation.4 | loop fusion | flops 7372800 | bytes 4829184 | tf_op jit(solution)/shard_map/concatenate | solution.py:464
  28.6 1.9 %collective-permute-start.15 = (bf16[384,3200]{1,0:T(8,128)(2,1)}, bf16[384,3200]{1,0:T(8,128)(2,1)}, u32[]{:S(2)}, u32[]{:S(2)}) collective-permute-start(bf16[384,3200]{1,0:T(8,128)(2,1)} %fusion.2), channel_id=1, source_target_pairs={{0,1},{1,0},{2,3},{3,2},{4,5},{5,4},{6,7},{7,6},{8,9},{9,8},{10,11... | collective-permute-start | bytes 7372808 | tf_op jit(solution)/shard_map/ppermute | solution.py:397
  32.4 3.0 %copy-done = bf16[3,3072,384]{2,1,0:T(8,128)(2,1)S(1)} copy-done((bf16[3,3072,384]{2,1,0:T(8,128)(2,1)S(1)}, bf16[3,3072,384]{2,1,0:T(8,128)(2,1)}, u32[]{:S(2)}) %copy-start) | copy-done | bytes 7077912
  35.5 4.5 %project.1.refs_4_ = bf16[3,256,384]{2,1,0:T(8,128)(2,1)S(1)} custom-call(bf16[256,3072]{1,0:T(8,128)(2,1)S(1)} %copy-done.1, bf16[1,3072]{1,0:T(2,128)(2,1)S(1)} %broadcast_in_dim.45.gain_ref, bf16[3,3072,384]{2,1,0:T(8,128)(2,1)S(1)} %copy-done, f32[256,384]{1,0:T(8,128)S(1)} %get-tuple-element.95.cos_ref, f32[256,384]{1,0:T(8,128)S(1)} %get-tuple-element.94.sin_ref), custom_call_target="tpu_custom_call" | custom-call | tf_op jit(solution)/shard_map/project/pallas_call | solution.py:58
  40.0 19.9 %collective-permute-done.4.refs_6_ = bf16[16,128,384]{2,1,0:T(8,128)(2,1)} collective-permute-done((bf16[16,128,384]{2,1,0:T(8,128)(2,1)}, bf16[16,128,384]{2,1,0:T(8,128)(2,1)}, u32[]{:S(2)}, u32[]{:S(2)}) %collective-permute-start.4) | collective-permute-done | bytes 1572896 | tf_op jit(solution)/shard_map/ppermute | solution.py:425
  62.1 2.9 %collective-permute-done.11 = bf16[48,2048]{1,0:T(8,128)(2,1)S(1)} collective-permute-done((bf16[48,2048]{1,0:T(8,128)(2,1)S(1)}, bf16[48,2048]{1,0:T(8,128)(2,1)S(1)}, u32[]{:S(2)}, u32[]{:S(2)}) %collective-permute-start.11) | collective-permute-done | bytes 196640 | tf_op jit(solution)/shard_map/ppermute | solution.py:413
  66.9 2.3 %collective-permute-done.9.refs_11_ = bf16[16,128,384]{2,1,0:T(8,128)(2,1)S(1)} collective-permute-done((bf16[16,128,384]{2,1,0:T(8,128)(2,1)}, bf16[16,128,384]{2,1,0:T(8,128)(2,1)S(1)}, u32[]{:S(2)}, u32[]{:S(2)}) %collective-permute-start.9) | collective-permute-done | bytes 1572896 | tf_op jit(solution)/shard_map/ppermute | solution.py:413
  70.4 5.8 %attend.1 = bf16[2,128,384]{2,1,0:T(8,128)(2,1)S(1)} custom-call(s32[4]{0:T(128)S(1)} %pad_add_fusion.refs_0_, s32[8]{0:T(128)S(1)} %copy-done.3, s32[64]{0:T(128)S(1)} %copy-done.4, s32[128]{0:T(128)S(1)} %copy-done.5, bf16[3,256,384]{2,1,0:T(8,128)(2,1)S(1)} %project.1.refs_4_, bf16[16,128,384]{2,1,0:T(8,128)(2,1)} %pad_maximum_fusion.refs_5_, ...), custom_call_target="tpu_custom_call" | custom-call | tf_op jit(solution)/shard_map/attend/pallas_call | solution.py:179
  76.2 8.6 %collective-permute-done.15 = bf16[384,3200]{1,0:T(8,128)(2,1)} collective-permute-done((bf16[384,3200]{1,0:T(8,128)(2,1)}, bf16[384,3200]{1,0:T(8,128)(2,1)}, u32[]{:S(2)}, u32[]{:S(2)}) %collective-permute-start.15) | collective-permute-done | bytes 2457632 | tf_op jit(solution)/shard_map/ppermute | solution.py:397
  84.9 2.3 %pad_maximum_fusion.1.refs_3_ = bf16[384,2048]{1,0:T(8,128)(2,1)} fusion(bf16[96,2048]{1,0:T(8,128)(2,1)} %collective-permute-done.14, bf16[96,2048]{1,0:T(8,128)(2,1)S(1)} %collective-permute-done.13, bf16[96,2048]{1,0:T(8,128)(2,1)S(1)} %collective-permute-done.12, bf16[96,2048]{1,0:T(8,128)(2,1)S(1)} %pad_maximum_fusion.3), kind=kLoop, calls=%fused_computation.6 | loop fusion | flops 6291456 | bytes 3145728 | tf_op jit(solution)/shard_map/concatenate | solution.py:506
  87.4 3.0 %collective-permute-start.21 = (bf16[384,2048]{1,0:T(8,128)(2,1)}, bf16[384,2048]{1,0:T(8,128)(2,1)}, u32[]{:S(2)}, u32[]{:S(2)}) collective-permute-start(bf16[384,2048]{1,0:T(8,128)(2,1)} %pad_maximum_fusion.1.refs_3_), channel_id=1, source_target_pairs={{0,64},{8,24},{16,80},{24,40},{32,96},{40,56},{48,112},{56,8},{64,... | collective-permute-start | bytes 4718600 | tf_op jit(solution)/shard_map/ppermute | solution.py:425
  90.4 1.8 collective-permute-start.16
  92.3 2.3 %fusion.3 = f32[128,3200]{1,0:T(8,128)S(1)} fusion(bf16[2,128,384]{2,1,0:T(8,128)(2,1)S(1)} %attend.1, s32[]{:T(128)S(6)} %select_n.180, bf16[384,16]{1,0:T(8,128)(2,1)S(1)} %copy-done.14, bf16[384,3072]{1,0:T(8,128)(2,1)} %param.17), kind=kOutput, calls=%fused_computation.15 | convolution fusion | flops 321945600 | bytes 4194308 | tf_op jit(solution)/shard_map/dot_general | solution.py:508
  95.1 2.3 %fusion.1 = bf16[128,3200]{1,0:T(8,128)(2,1)S(1)} fusion(f32[128,3200]{1,0:T(8,128)S(1)} %fusion.3, bf16[128,384]{1,0:T(8,128)(2,1)S(1)} %collective-permute-done.16, bf16[384,3200]{1,0:T(8,128)(2,1)} %collective-permute-done.15), kind=kOutput, calls=%fused_computation.3 | convolution fusion | flops 315392000 | bytes 5013504 | tf_op jit(solution)/shard_map/dot_general | solution.py:509
  97.6 7.1 %collective-permute-start.17 = (bf16[32,3200]{1,0:T(8,128)(2,1)S(1)}, bf16[32,3200]{1,0:T(8,128)(2,1)S(1)}, u32[]{:S(2)}, u32[]{:S(2)}) collective-permute-start(bf16[32,3200]{1,0:T(8,128)(2,1)S(1)} %get-tuple-element.80), channel_id=1, source_target_pairs={{0,4},{1,5},{2,6},{3,7},{4,0},{5,1},{6,2},{7,3},{8,12},{9,13},{10,... | collective-permute-start | bytes 614408 | tf_op jit(solution)/shard_map/ppermute | solution.py:393
  106.1 2.7 %collective-permute-start.19 = (bf16[32,3200]{1,0:T(8,128)(2,1)S(1)}, bf16[32,3200]{1,0:T(8,128)(2,1)S(1)}, u32[]{:S(2)}, u32[]{:S(2)}) collective-permute-start(bf16[32,3200]{1,0:T(8,128)(2,1)S(1)} %get-tuple-element.78), channel_id=1, source_target_pairs={{0,6},{1,7},{2,0},{3,1},{4,2},{5,3},{6,4},{7,5},{8,14},{9,15},{10,... | collective-permute-start | bytes 614408 | tf_op jit(solution)/shard_map/ppermute | solution.py:393
  108.8 4.9 %collective-permute-done.17.refs_1_ = bf16[32,3200]{1,0:T(8,128)(2,1)S(1)} collective-permute-done((bf16[32,3200]{1,0:T(8,128)(2,1)S(1)}, bf16[32,3200]{1,0:T(8,128)(2,1)S(1)}, u32[]{:S(2)}, u32[]{:S(2)}) %collective-permute-start.17) | collective-permute-done | bytes 204832 | tf_op jit(solution)/shard_map/ppermute | solution.py:393
  113.7 5.5 %collective-permute-done.18.refs_2_ = bf16[32,3200]{1,0:T(8,128)(2,1)S(1)} collective-permute-done((bf16[32,3200]{1,0:T(8,128)(2,1)S(1)}, bf16[32,3200]{1,0:T(8,128)(2,1)S(1)}, u32[]{:S(2)}, u32[]{:S(2)}) %collective-permute-start.18) | collective-permute-done | bytes 204832 | tf_op jit(solution)/shard_map/ppermute | solution.py:393
  121.9 3.1 %collective-permute-start.22 = (bf16[32,3200]{1,0:T(8,128)(2,1)S(1)}, bf16[32,3200]{1,0:T(8,128)(2,1)S(1)}, u32[]{:S(2)}, u32[]{:S(2)}) collective-permute-start(bf16[32,3200]{1,0:T(8,128)(2,1)S(1)} %settle.1.refs_12_), channel_id=1, source_target_pairs={{0,7},{1,0},{2,1},{3,2},{4,3},{5,4},{6,5},{7,6},{8,15},{9,8},{10,9... | collective-permute-start | bytes 614408 | tf_op jit(solution)/shard_map/ppermute | solution.py:393
  125.1 2.3 %collective-permute-start.28 = (bf16[384,2048]{1,0:T(8,128)(2,1)}, bf16[384,2048]{1,0:T(8,128)(2,1)}, u32[]{:S(2)}, u32[]{:S(2)}) collective-permute-start(bf16[384,2048]{1,0:T(8,128)(2,1)} %pad_maximum_fusion.1.refs_3_), channel_id=1, source_target_pairs={{0,128},{8,40},{16,144},{24,56},{32,160},{40,8},{48,176},{56,24},{... | collective-permute-start | bytes 4718600 | tf_op jit(solution)/shard_map/ppermute | solution.py:425
  127.4 2.3 %collective-permute-done.22.refs_14_ = bf16[32,3200]{1,0:T(8,128)(2,1)S(1)} collective-permute-done((bf16[32,3200]{1,0:T(8,128)(2,1)S(1)}, bf16[32,3200]{1,0:T(8,128)(2,1)S(1)}, u32[]{:S(2)}, u32[]{:S(2)}) %collective-permute-start.22) | collective-permute-done | bytes 204832 | tf_op jit(solution)/shard_map/ppermute | solution.py:393
  129.7 3.4 %collective-permute-done.23.refs_16_ = bf16[32,3200]{1,0:T(8,128)(2,1)S(1)} collective-permute-done((bf16[32,3200]{1,0:T(8,128)(2,1)S(1)}, bf16[32,3200]{1,0:T(8,128)(2,1)S(1)}, u32[]{:S(2)}, u32[]{:S(2)}) %collective-permute-start.23) | collective-permute-done | bytes 204832 | tf_op jit(solution)/shard_map/ppermute | solution.py:393
  133.6 1.7 collective-permute-start.27
  135.3 12.0 %collective-permute-done.28.refs_5_ = bf16[384,2048]{1,0:T(8,128)(2,1)} collective-permute-done((bf16[384,2048]{1,0:T(8,128)(2,1)}, bf16[384,2048]{1,0:T(8,128)(2,1)}, u32[]{:S(2)}, u32[]{:S(2)}) %collective-permute-start.28) | collective-permute-done | bytes 1572896 | tf_op jit(solution)/shard_map/ppermute | solution.py:425
  148.9 3.2 %collective-permute-start.30 = (bf16[32,3200]{1,0:T(8,128)(2,1)S(1)}, bf16[32,3200]{1,0:T(8,128)(2,1)S(1)}, u32[]{:S(2)}, u32[]{:S(2)}) collective-permute-start(bf16[32,3200]{1,0:T(8,128)(2,1)S(1)} %collective-permute-done.26.refs_18_), channel_id=1, source_target_pairs={{0,7},{1,0},{2,1},{3,2},{4,3},{5,4},{6,5},{7,6},{8,15},{9,8},{10,9... | collective-permute-start | bytes 614408 | tf_op jit(solution)/shard_map/ppermute | solution.py:393
  155.3 9.1 %score.2 = f32[8,320]{1,0:T(8,128)S(1)} custom-call(s32[9]{0:T(128)S(1)} %stack.70.refs_0_, bf16[16,3072]{1,0:T(8,128)(2,1)S(1)} %copy-done.2, bf16[1,3072]{1,0:T(2,128)(2,1)S(1)} %broadcast_in_dim.44.gain_ref.refs_2_, bf16[384,2048]{1,0:T(8,128)(2,1)} %pad_maximum_fusion.1.refs_3_, bf16[384,2048]{1,0:T(8,128)(2,1)} %copy-done.6, ...), custom_call_target="tpu_custom_call" | custom-call | flops 4026531840 | bytes 12582912 | tf_op jit(solution)/shard_map/score/pallas_call | solution.py:360
  164.5 8.2 %score.3 = f32[8,192]{1,0:T(8,128)S(1)} custom-call(s32[8]{0:T(128)S(1)} %stack.75.refs_0_, bf16[16,3072]{1,0:T(8,128)(2,1)S(1)} %copy-done.2, bf16[1,3072]{1,0:T(2,128)(2,1)S(1)} %broadcast_in_dim.44.gain_ref.refs_2_, bf16[384,2048]{1,0:T(8,128)(2,1)} %pad_maximum_fusion.1.refs_3_, bf16[384,2048]{1,0:T(8,128)(2,1)} %copy-done.6, ...), custom_call_target="tpu_custom_call" | custom-call | flops 2415919104 | bytes 12582912 | tf_op jit(solution)/shard_map/score/pallas_call | solution.py:360
  173.1 14.6 %all_to_all.5 = f32[8,8,512]{2,1,0:T(8,128)S(1)} all-to-all(f32[8,8,512]{2,1,0:T(8,128)S(1)} %broadcast_in_dim.51), channel_id=1, replica_groups=mesh['seq'=32,'tensor'=8] {'tensor'}, dimensions={0} | all-to-all | bytes 262144 | tf_op jit(solution)/shard_map/all_to_all | solution.py:575
  (122 shorter events, 26.1 us)
Async XLA Ops:
  3.3 12.4 %collective-permute-start.1 = (bf16[4,128,384]{2,1,0:T(8,128)(2,1)S(1)}, bf16[4,128,384]{2,1,0:T(8,128)(2,1)S(1)}, u32[]{:S(2)}, u32[]{:S(2)}) collective-permute-start(bf16[4,128,384]{2,1,0:T(8,128)(2,1)S(1)} %pad_maximum_fusion.2), channel_id=1, source_target_pairs={{0,48},{8,200},{16,0},{24,216},{32,16},{40,232},{48,32},{56,248},{... | collective-permute-start | bytes 1179656 | tf_op jit(solution)/shard_map/ppermute | solution.py:425
  6.1 9.5 %collective-permute-start.2 = (bf16[4,128,384]{2,1,0:T(8,128)(2,1)S(1)}, bf16[4,128,384]{2,1,0:T(8,128)(2,1)S(1)}, u32[]{:S(2)}, u32[]{:S(2)}) collective-permute-start(bf16[4,128,384]{2,1,0:T(8,128)(2,1)S(1)} %pad_maximum_fusion.2), channel_id=1, source_target_pairs={{0,32},{8,136},{16,48},{24,152},{32,0},{40,168},{48,16},{56,184},{... | collective-permute-start | bytes 1179656 | tf_op jit(solution)/shard_map/ppermute | solution.py:425
  6.9 12.7 %collective-permute-start.3 = (bf16[4,128,384]{2,1,0:T(8,128)(2,1)S(1)}, bf16[4,128,384]{2,1,0:T(8,128)(2,1)S(1)}, u32[]{:S(2)}, u32[]{:S(2)}) collective-permute-start(bf16[4,128,384]{2,1,0:T(8,128)(2,1)S(1)} %pad_maximum_fusion.2), channel_id=1, source_target_pairs={{0,16},{8,72},{16,32},{24,88},{32,48},{40,104},{48,0},{56,120},{64... | collective-permute-start | bytes 1179656 | tf_op jit(solution)/shard_map/ppermute | solution.py:425
  21.1 38.8 %collective-permute-start.4 = (bf16[16,128,384]{2,1,0:T(8,128)(2,1)}, bf16[16,128,384]{2,1,0:T(8,128)(2,1)}, u32[]{:S(2)}, u32[]{:S(2)}) collective-permute-start(bf16[16,128,384]{2,1,0:T(8,128)(2,1)} %pad_maximum_fusion.refs_5_), channel_id=1, source_target_pairs={{0,192},{8,56},{16,208},{24,8},{32,224},{40,24},{48,240},{56,40},{... | collective-permute-start | bytes 4718600 | tf_op jit(solution)/shard_map/ppermute | solution.py:425
  21.8 38.1 %collective-permute-start.5 = (bf16[16,128,384]{2,1,0:T(8,128)(2,1)}, bf16[16,128,384]{2,1,0:T(8,128)(2,1)}, u32[]{:S(2)}, u32[]{:S(2)}) collective-permute-start(bf16[16,128,384]{2,1,0:T(8,128)(2,1)} %pad_maximum_fusion.refs_5_), channel_id=1, source_target_pairs={{0,128},{8,40},{16,144},{24,56},{32,160},{40,8},{48,176},{56,24},{... | collective-permute-start | bytes 4718600 | tf_op jit(solution)/shard_map/ppermute | solution.py:425
  22.8 38.0 %collective-permute-start.6 = (bf16[16,128,384]{2,1,0:T(8,128)(2,1)}, bf16[16,128,384]{2,1,0:T(8,128)(2,1)}, u32[]{:S(2)}, u32[]{:S(2)}) collective-permute-start(bf16[16,128,384]{2,1,0:T(8,128)(2,1)} %pad_maximum_fusion.refs_5_), channel_id=1, source_target_pairs={{0,64},{8,24},{16,80},{24,40},{32,96},{40,56},{48,112},{56,8},{64,... | collective-permute-start | bytes 4718600 | tf_op jit(solution)/shard_map/ppermute | solution.py:425
  24.9 35.8 %collective-permute-start.7 = (bf16[16,128,384]{2,1,0:T(8,128)(2,1)}, bf16[16,128,384]{2,1,0:T(8,128)(2,1)}, u32[]{:S(2)}, u32[]{:S(2)}) collective-permute-start(bf16[16,128,384]{2,1,0:T(8,128)(2,1)} %pad_maximum_fusion.refs_5_), channel_id=1, source_target_pairs={{0,8},{8,0},{16,24},{24,16},{32,40},{40,32},{48,56},{56,48},{64,72... | collective-permute-start | bytes 4718600 | tf_op jit(solution)/shard_map/ppermute | solution.py:413
  28.6 56.3 %collective-permute-start.15 = (bf16[384,3200]{1,0:T(8,128)(2,1)}, bf16[384,3200]{1,0:T(8,128)(2,1)}, u32[]{:S(2)}, u32[]{:S(2)}) collective-permute-start(bf16[384,3200]{1,0:T(8,128)(2,1)} %fusion.2), channel_id=1, source_target_pairs={{0,1},{1,0},{2,3},{3,2},{4,5},{5,4},{6,7},{7,6},{8,9},{9,8},{10,11... | collective-permute-start | bytes 7372808 | tf_op jit(solution)/shard_map/ppermute | solution.py:397
  60.8 5.0 %collective-permute-start.8 = (bf16[16,128,384]{2,1,0:T(8,128)(2,1)}, bf16[16,128,384]{2,1,0:T(8,128)(2,1)S(1)}, u32[]{:S(2)}, u32[]{:S(2)}) collective-permute-start(bf16[16,128,384]{2,1,0:T(8,128)(2,1)} %collective-permute-done.4.refs_6_), channel_id=1, source_target_pairs={{0,8},{8,0},{16,24},{24,16},{32,40},{40,32},{48,56},{56,48},{64,72... | collective-permute-start | bytes 4718600 | tf_op jit(solution)/shard_map/ppermute | solution.py:413
  60.8 8.4 %collective-permute-start.9 = (bf16[16,128,384]{2,1,0:T(8,128)(2,1)}, bf16[16,128,384]{2,1,0:T(8,128)(2,1)S(1)}, u32[]{:S(2)}, u32[]{:S(2)}) collective-permute-start(bf16[16,128,384]{2,1,0:T(8,128)(2,1)} %collective-permute-done.5.refs_7_), channel_id=1, source_target_pairs={{0,8},{8,0},{16,24},{24,16},{32,40},{40,32},{48,56},{56,48},{64,72... | collective-permute-start | bytes 4718600 | tf_op jit(solution)/shard_map/ppermute | solution.py:413
  61.3 9.2 %collective-permute-start.10 = (bf16[16,128,384]{2,1,0:T(8,128)(2,1)}, bf16[16,128,384]{2,1,0:T(8,128)(2,1)}, u32[]{:S(2)}, u32[]{:S(2)}) collective-permute-start(bf16[16,128,384]{2,1,0:T(8,128)(2,1)} %collective-permute-done.6.refs_8_), channel_id=1, source_target_pairs={{0,8},{8,0},{16,24},{24,16},{32,40},{40,32},{48,56},{56,48},{64,72... | collective-permute-start | bytes 4718600 | tf_op jit(solution)/shard_map/ppermute | solution.py:413
  65.1 19.8 %collective-permute-start.12 = (bf16[96,2048]{1,0:T(8,128)(2,1)S(1)}, bf16[96,2048]{1,0:T(8,128)(2,1)S(1)}, u32[]{:S(2)}, u32[]{:S(2)}) collective-permute-start(bf16[96,2048]{1,0:T(8,128)(2,1)S(1)} %pad_maximum_fusion.3), channel_id=1, source_target_pairs={{0,48},{8,200},{16,0},{24,216},{32,16},{40,232},{48,32},{56,248},{... | collective-permute-start | bytes 1179656 | tf_op jit(solution)/shard_map/ppermute | solution.py:425
  65.7 19.1 %collective-permute-start.13 = (bf16[96,2048]{1,0:T(8,128)(2,1)S(1)}, bf16[96,2048]{1,0:T(8,128)(2,1)S(1)}, u32[]{:S(2)}, u32[]{:S(2)}) collective-permute-start(bf16[96,2048]{1,0:T(8,128)(2,1)S(1)} %pad_maximum_fusion.3), channel_id=1, source_target_pairs={{0,32},{8,136},{16,48},{24,152},{32,0},{40,168},{48,16},{56,184},{... | collective-permute-start | bytes 1179656 | tf_op jit(solution)/shard_map/ppermute | solution.py:425
  70.4 14.5 %collective-permute-start.14 = (bf16[96,2048]{1,0:T(8,128)(2,1)S(1)}, bf16[96,2048]{1,0:T(8,128)(2,1)}, u32[]{:S(2)}, u32[]{:S(2)}) collective-permute-start(bf16[96,2048]{1,0:T(8,128)(2,1)S(1)} %pad_maximum_fusion.3), channel_id=1, source_target_pairs={{0,16},{8,72},{16,32},{24,88},{32,48},{40,104},{48,0},{56,120},{64... | collective-permute-start | bytes 1179656 | tf_op jit(solution)/shard_map/ppermute | solution.py:425
  87.2 33.7 %collective-permute-start.20 = (bf16[384,2048]{1,0:T(8,128)(2,1)}, bf16[384,2048]{1,0:T(8,128)(2,1)S(1)}, u32[]{:S(2)}, u32[]{:S(2)}) collective-permute-start(bf16[384,2048]{1,0:T(8,128)(2,1)} %pad_maximum_fusion.1.refs_3_), channel_id=1, source_target_pairs={{0,192},{8,56},{16,208},{24,8},{32,224},{40,24},{48,240},{56,40},{... | collective-permute-start | bytes 4718600 | tf_op jit(solution)/shard_map/ppermute | solution.py:425
  87.4 33.5 %collective-permute-start.21 = (bf16[384,2048]{1,0:T(8,128)(2,1)}, bf16[384,2048]{1,0:T(8,128)(2,1)}, u32[]{:S(2)}, u32[]{:S(2)}) collective-permute-start(bf16[384,2048]{1,0:T(8,128)(2,1)} %pad_maximum_fusion.1.refs_3_), channel_id=1, source_target_pairs={{0,64},{8,24},{16,80},{24,40},{32,96},{40,56},{48,112},{56,8},{64,... | collective-permute-start | bytes 4718600 | tf_op jit(solution)/shard_map/ppermute | solution.py:425
  97.6 16.2 %collective-permute-start.17 = (bf16[32,3200]{1,0:T(8,128)(2,1)S(1)}, bf16[32,3200]{1,0:T(8,128)(2,1)S(1)}, u32[]{:S(2)}, u32[]{:S(2)}) collective-permute-start(bf16[32,3200]{1,0:T(8,128)(2,1)S(1)} %get-tuple-element.80), channel_id=1, source_target_pairs={{0,4},{1,5},{2,6},{3,7},{4,0},{5,1},{6,2},{7,3},{8,12},{9,13},{10,... | collective-permute-start | bytes 614408 | tf_op jit(solution)/shard_map/ppermute | solution.py:393
  104.7 14.6 %collective-permute-start.18 = (bf16[32,3200]{1,0:T(8,128)(2,1)S(1)}, bf16[32,3200]{1,0:T(8,128)(2,1)S(1)}, u32[]{:S(2)}, u32[]{:S(2)}) collective-permute-start(bf16[32,3200]{1,0:T(8,128)(2,1)S(1)} %get-tuple-element.79), channel_id=1, source_target_pairs={{0,2},{1,3},{2,4},{3,5},{4,6},{5,7},{6,0},{7,1},{8,10},{9,11},{10,... | collective-permute-start | bytes 614408 | tf_op jit(solution)/shard_map/ppermute | solution.py:393
  106.1 14.7 %collective-permute-start.19 = (bf16[32,3200]{1,0:T(8,128)(2,1)S(1)}, bf16[32,3200]{1,0:T(8,128)(2,1)S(1)}, u32[]{:S(2)}, u32[]{:S(2)}) collective-permute-start(bf16[32,3200]{1,0:T(8,128)(2,1)S(1)} %get-tuple-element.78), channel_id=1, source_target_pairs={{0,6},{1,7},{2,0},{3,1},{4,2},{5,3},{6,4},{7,5},{8,14},{9,15},{10,... | collective-permute-start | bytes 614408 | tf_op jit(solution)/shard_map/ppermute | solution.py:393
  120.9 12.2 %collective-permute-start.24 = (bf16[384,2048]{1,0:T(8,128)(2,1)}, bf16[384,2048]{1,0:T(8,128)(2,1)S(1)}, u32[]{:S(2)}, u32[]{:S(2)}) collective-permute-start(bf16[384,2048]{1,0:T(8,128)(2,1)} %pad_maximum_fusion.1.refs_3_), channel_id=1, source_target_pairs={{0,8},{8,0},{16,24},{24,16},{32,40},{40,32},{48,56},{56,48},{64,72... | collective-permute-start | bytes 4718600 | tf_op jit(solution)/shard_map/ppermute | solution.py:413
  121.0 12.1 %collective-permute-start.25 = (bf16[384,2048]{1,0:T(8,128)(2,1)S(1)}, bf16[384,2048]{1,0:T(8,128)(2,1)S(1)}, u32[]{:S(2)}, u32[]{:S(2)}) collective-permute-start(bf16[384,2048]{1,0:T(8,128)(2,1)S(1)} %collective-permute-done.20.refs_4_), channel_id=1, source_target_pairs={{0,8},{8,0},{16,24},{24,16},{32,40},{40,32},{48,56},{56,48},{64,72... | collective-permute-start | bytes 4718600 | tf_op jit(solution)/shard_map/ppermute | solution.py:413
  121.9 7.7 %collective-permute-start.22 = (bf16[32,3200]{1,0:T(8,128)(2,1)S(1)}, bf16[32,3200]{1,0:T(8,128)(2,1)S(1)}, u32[]{:S(2)}, u32[]{:S(2)}) collective-permute-start(bf16[32,3200]{1,0:T(8,128)(2,1)S(1)} %settle.1.refs_12_), channel_id=1, source_target_pairs={{0,7},{1,0},{2,1},{3,2},{4,3},{5,4},{6,5},{7,6},{8,15},{9,8},{10,9... | collective-permute-start | bytes 614408 | tf_op jit(solution)/shard_map/ppermute | solution.py:393
  125.1 8.0 %collective-permute-start.23 = (bf16[32,3200]{1,0:T(8,128)(2,1)S(1)}, bf16[32,3200]{1,0:T(8,128)(2,1)S(1)}, u32[]{:S(2)}, u32[]{:S(2)}) collective-permute-start(bf16[32,3200]{1,0:T(8,128)(2,1)S(1)} %settle.1.refs_12_), channel_id=1, source_target_pairs={{0,1},{1,2},{2,3},{3,4},{4,5},{5,6},{6,7},{7,0},{8,9},{9,10},{10,1... | collective-permute-start | bytes 614408 | tf_op jit(solution)/shard_map/ppermute | solution.py:393
  125.1 22.2 %collective-permute-start.28 = (bf16[384,2048]{1,0:T(8,128)(2,1)}, bf16[384,2048]{1,0:T(8,128)(2,1)}, u32[]{:S(2)}, u32[]{:S(2)}) collective-permute-start(bf16[384,2048]{1,0:T(8,128)(2,1)} %pad_maximum_fusion.1.refs_3_), channel_id=1, source_target_pairs={{0,128},{8,40},{16,144},{24,56},{32,160},{40,8},{48,176},{56,24},{... | collective-permute-start | bytes 4718600 | tf_op jit(solution)/shard_map/ppermute | solution.py:425
  133.1 14.2 %collective-permute-start.29 = (bf16[384,2048]{1,0:T(8,128)(2,1)}, bf16[384,2048]{1,0:T(8,128)(2,1)S(1)}, u32[]{:S(2)}, u32[]{:S(2)}) collective-permute-start(bf16[384,2048]{1,0:T(8,128)(2,1)} %collective-permute-done.21.refs_6_), channel_id=1, source_target_pairs={{0,8},{8,0},{16,24},{24,16},{32,40},{40,32},{48,56},{56,48},{64,72... | collective-permute-start | bytes 4718600 | tf_op jit(solution)/shard_map/ppermute | solution.py:413
  133.2 14.1 %collective-permute-start.26 = (bf16[32,3200]{1,0:T(8,128)(2,1)S(1)}, bf16[32,3200]{1,0:T(8,128)(2,1)S(1)}, u32[]{:S(2)}, u32[]{:S(2)}) collective-permute-start(bf16[32,3200]{1,0:T(8,128)(2,1)S(1)} %collective-permute-done.22.refs_14_), channel_id=1, source_target_pairs={{0,7},{1,0},{2,1},{3,2},{4,3},{5,4},{6,5},{7,6},{8,15},{9,8},{10,9... | collective-permute-start | bytes 614408 | tf_op jit(solution)/shard_map/ppermute | solution.py:393
  133.6 13.7 %collective-permute-start.27 = (bf16[32,3200]{1,0:T(8,128)(2,1)S(1)}, bf16[32,3200]{1,0:T(8,128)(2,1)S(1)}, u32[]{:S(2)}, u32[]{:S(2)}) collective-permute-start(bf16[32,3200]{1,0:T(8,128)(2,1)S(1)} %collective-permute-done.23.refs_16_), channel_id=1, source_target_pairs={{0,1},{1,2},{2,3},{3,4},{4,5},{5,6},{6,7},{7,0},{8,9},{9,10},{10,1... | collective-permute-start | bytes 614408 | tf_op jit(solution)/shard_map/ppermute | solution.py:393
  148.5 6.7 %collective-permute-start.34 = (bf16[384,2048]{1,0:T(8,128)(2,1)}, bf16[384,2048]{1,0:T(8,128)(2,1)}, u32[]{:S(2)}, u32[]{:S(2)}) collective-permute-start(bf16[384,2048]{1,0:T(8,128)(2,1)} %collective-permute-done.28.refs_5_), channel_id=1, source_target_pairs={{0,8},{8,0},{16,24},{24,16},{32,40},{40,32},{48,56},{56,48},{64,72... | collective-permute-start | bytes 4718600 | tf_op jit(solution)/shard_map/ppermute | solution.py:413
  148.9 15.5 %collective-permute-start.30 = (bf16[32,3200]{1,0:T(8,128)(2,1)S(1)}, bf16[32,3200]{1,0:T(8,128)(2,1)S(1)}, u32[]{:S(2)}, u32[]{:S(2)}) collective-permute-start(bf16[32,3200]{1,0:T(8,128)(2,1)S(1)} %collective-permute-done.26.refs_18_), channel_id=1, source_target_pairs={{0,7},{1,0},{2,1},{3,2},{4,3},{5,4},{6,5},{7,6},{8,15},{9,8},{10,9... | collective-permute-start | bytes 614408 | tf_op jit(solution)/shard_map/ppermute | solution.py:393
  152.1 12.3 %collective-permute-start.31 = (bf16[32,3200]{1,0:T(8,128)(2,1)S(1)}, bf16[32,3200]{1,0:T(8,128)(2,1)S(1)}, u32[]{:S(2)}, u32[]{:S(2)}) collective-permute-start(bf16[32,3200]{1,0:T(8,128)(2,1)S(1)} %collective-permute-done.27.refs_20_), channel_id=1, source_target_pairs={{0,1},{1,2},{2,3},{3,4},{4,5},{5,6},{6,7},{7,0},{8,9},{9,10},{10,1... | collective-permute-start | bytes 614408 | tf_op jit(solution)/shard_map/ppermute | solution.py:393
  152.2 12.1 %collective-permute-start.32 = (bf16[16,3200]{1,0:T(8,128)(2,1)S(1)}, bf16[16,3200]{1,0:T(8,128)(2,1)S(1)}, u32[]{:S(2)}, u32[]{:S(2)}) collective-permute-start(bf16[16,3200]{1,0:T(8,128)(2,1)S(1)} %slice.53), channel_id=1, source_target_pairs={{0,6},{1,7},{2,0},{3,1},{4,2},{5,3},{6,4},{7,5},{8,14},{9,15},{10,... | collective-permute-start | bytes 307208 | tf_op jit(solution)/shard_map/ppermute | solution.py:393
  153.9 10.4 %collective-permute-start.33 = (bf16[16,3200]{1,0:T(8,128)(2,1)S(1)}, bf16[16,3200]{1,0:T(8,128)(2,1)S(1)}, u32[]{:S(2)}, u32[]{:S(2)}) collective-permute-start(bf16[16,3200]{1,0:T(8,128)(2,1)S(1)} %slice.54), channel_id=1, source_target_pairs={{0,2},{1,3},{2,4},{3,5},{4,6},{5,7},{6,0},{7,1},{8,10},{9,11},{10,... | collective-permute-start | bytes 307208 | tf_op jit(solution)/shard_map/ppermute | solution.py:393
  (22 other events, 312.8 us)

commit v5 on v4

--- a/solution.py
+++ b/solution.py
@@ -461,7 +461,6 @@
     me = lax.axis_index("seq")
     rank = lax.axis_index("tensor")
     down = jnp.pad(adapter_down_weight, ((0, 0), (0, PAD - adapter_down_weight.shape[1])))
-    weights = jnp.concatenate([output_weight, down], axis=1)
     groups_iota = jnp.arange(counts.shape[0], dtype=jnp.int32)
     my_groups = lax.dynamic_slice_in_dim(owner, first, rollouts_here, 0)
     my_pages = jnp.sum(
@@ -473,7 +472,8 @@
     frequency = 10000.0 ** (-place_in_head.astype(F32) * 2.0 / HEAD_WIDTH)
     angles = positions.astype(F32)[:, None] * frequency[None, :]
     pair = start_pair(prompt_key_slots, prompt_value_slots)
-    partner_weights = partnered(weights, ranks)
+    partner_weights = partnered(output_weight, ranks)
+    partner_down = partnered(down, ranks)
     line = lax.optimization_barrier(along_first(pair))
     line = lax.optimization_barrier(jnp.concatenate(line))
     ahead = [turned(line, 1, step) for step in (3, 2, 1)]
@@ -485,7 +485,9 @@
         jnp.cos(angles),
         jnp.sin(angles),
     )
-    ahead, near, qkv, head_columns = lax.optimization_barrier((ahead, near, qkv, head.T))
+    ahead, near, qkv, head_columns, partner_weights = lax.optimization_barrier(
+        (ahead, near, qkv, head.T, partner_weights)
+    )
     pieces = [line] + ahead + [near] + [crossed(piece) for piece in ahead]
     half = head_columns.shape[0] // 2
     head_pair = start_pair(head_columns[:half], head_columns[half:])
@@ -499,15 +501,21 @@
         pieces,
     )
     theirs = partnered(lax.dynamic_index_in_dim(attended, 1 - rank % 2, 0, False), ranks)
-    attended, head_line, partner_weights = lax.optimization_barrier(
-        (attended, head_line, partner_weights)
+    attended, head_line, partner_down = lax.optimization_barrier(
+        (attended, head_line, partner_down)
     )
     own = lax.dynamic_index_in_dim(attended, rank % 2, 0, False)
     head_line = lax.optimization_barrier(jnp.concatenate(head_line))
     head_ahead = [turned(head_line, 1, 3), turned(head_line, 1, 1)]
-    branch = jnp.dot(own, weights, preferred_element_type=F32)
-    branch = branch + jnp.dot(theirs, partner_weights, preferred_element_type=F32)
-    parts = reduce_rows(branch.astype(BF16), ranks)
+    branch = [
+        jnp.dot(own, factor, preferred_element_type=F32)
+        + jnp.dot(theirs, partner_factor, preferred_element_type=F32)
+        for factor, partner_factor in (
+            (output_weight, partner_weights),
+            (down, partner_down),
+        )
+    ]
+    parts = reduce_rows(jnp.concatenate([part.astype(BF16) for part in branch], axis=1), ranks)
     parts, head_line, head_ahead = lax.optimization_barrier((parts, head_line, head_ahead))
     head_opposite = turned(head_line, 1, 2)
     mine = settle(
@@ -554,22 +562,23 @@
             crossed(third),
         )
     )
-    near = [after_one, before_one, after_two, before_two]
     head_pieces = [head_line, head_ahead[0], head_opposite, head_ahead[1]]
     head_pieces += [line_swapped, first_swapped, crossed(head_opposite), third_swapped]
-    far = [
+    blocks = [
+        mine,
+        after_one,
+        before_one,
+        after_two,
+        before_two,
         shifted(after_two, ranks, -1),
         shifted(before_two, ranks, 1),
         shifted(after_two[:half], ranks, -2),
         shifted(before_two[half:], ranks, 2),
     ]
-    near_offsets = (0, 1, ranks - 1, 2, ranks - 2)
-    near_part = score_blocks([place(n) for n in near_offsets], [mine] + near)
-    far, near_part = lax.optimization_barrier((far, near_part))
-    far_offsets = (3, ranks - 3, ranks // 2)
+    offsets = (0, 1, ranks - 1, 2, ranks - 2, 3, ranks - 3)
     opposite = 2 * place(ranks // 2)
-    far_part = score_blocks([place(3), place(ranks - 3), opposite, opposite + 1], far)
-    stats = by_offset(near_offsets, near_part) | by_offset(far_offsets, far_part)
+    part = score_blocks([place(n) for n in offsets] + [opposite, opposite + 1], blocks)
+    stats = by_offset(offsets + (ranks // 2,), part)
     line = jnp.stack([stats[k] for k in range(ranks)] * 2, axis=2)
     ordered = lax.dynamic_slice_in_dim(line, ranks - rank, ranks, 2).reshape(8, 2 * tok_rows)
     every = lax.all_to_all(

time: 190 us -> 182 us (0.958)
  waiting for transfers between devices: 78.2 us -> 85.4 us
  Pallas kernels: 28 us -> 21.8 us
  other arithmetic: 10.2 us -> 5.59 us
  local copies, waits for them, and re-layouts: 7.65 us -> 4.63 us
    ppermute x12, waiting for transfers between devices: 44.6 us -> 53.4 us  [turned(): return lax.ppermute(value, 'seq', [(i, target(i)) for i in range(32)])]
    ppermute x11, waiting for transfers between devices: 17.8 us -> 26.2 us  [shifted(): lax.ppermute(value, 'tensor', [(i, (i + step) % ranks) for i in range(ran...]
    ppermute x2 -> x3, waiting for transfers between devices: 9.17 us -> 2.54 us  [partnered(): return lax.ppermute(value, 'tensor', [(i, i ^ 1) for i in range(ranks)])]
    pallas_call x2 -> x1, Pallas kernels: 17.3 us -> 10.8 us  [score(): pl.pallas_call(score_kernel, grid_spec=pltpu.PrefetchScalarGridSpec(num_s...]
    concatenate x1, other arithmetic: 3.45 us -> 0.08 us  [local(): jnp.concatenate([part.astype(BF16) for part in branch], axis=1)]
    ppermute x10, waiting for transfers between devices: 6.66 us -> 3.33 us  [crossed(): return lax.ppermute(value, 'seq', [(i, i ^ 1) for i in range(32)])]
    unnamed x39 -> x36, local copies, waits for them, and re-layouts: 5.9 us -> 3.09 us
    dot_general x2 -> x4, matrix products: 4.6 us -> 3.18 us  [the longest x2 2.45 us: local(): jnp.dot(theirs, partner_factor, preferred_element_type=F32)]
  transfers between devices with their start and end apart: 35 -> 36, of which waited for: 15 -> 17; matrix products, arithmetic and copies ran while one was open for 6% -> 4% of each run, Pallas kernels for 11% -> 6%
where the time goes in v5:
time: 182 us; the launch traced here: 180 us
  waiting for transfers between devices  85.4 us (47%)
  starting transfers between devices  44.5 us (24%)
  Pallas kernels  21.8 us (12%)
  blocking collectives  14.2 us (8%)
  other arithmetic  5.59 us (3%)
  local copies, waits for them, and re-layouts  4.63 us (3%)
  matrix products  3.18 us (2%)
    ppermute x12, waiting for transfers between devices, turned(): return lax.ppermute(value, 'seq', [(i, target(i)) for i in range(32)])  53.4 us
    ppermute x11, waiting for transfers between devices, shifted(): lax.ppermute(value, 'tensor', [(i, (i + step) % ranks) for i in range(ran...  26.2 us
    ppermute x11, starting transfers between devices, shifted(): lax.ppermute(value, 'tensor', [(i, (i + step) % ranks) for i in range(ran...  22.2 us
    ppermute x12, starting transfers between devices, turned(): return lax.ppermute(value, 'seq', [(i, target(i)) for i in range(32)])  15.2 us
    all_to_all x1, blocking collectives, local(): lax.all_to_all(jnp.broadcast_to(ordered[None], (ranks, 8, 2 * tok_rows)),...  14.2 us
    pallas_call x1, Pallas kernels, score(): pl.pallas_call(score_kernel, grid_spec=pltpu.PrefetchScalarGridSpec(num_s...  10.8 us
    pallas_call x1, Pallas kernels, attend(): pl.pallas_call(attend_kernel, grid_spec=pltpu.PrefetchScalarGridSpec(num_...  6 us
    ppermute x3, starting transfers between devices, partnered(): return lax.ppermute(value, 'tensor', [(i, i ^ 1) for i in range(ranks)])  4.85 us
  transfers between devices with their start and end apart: 36, of which 17 were waited for; matrix products, arithmetic and copies ran while one was open for 4% of the time, Pallas kernels for 6%

profile of v5, /device:TPU:24, one launch (start us, length us, event | category | flops | bytes accessed | tf_op | source)
XLA Modules:
  0.0 180.4 jit_solution(4813997785567391318)
XLA Ops:
  1.8 2.0 %collective-permute-start.8 = (bf16[384,3072]{1,0:T(8,128)(2,1)}, bf16[384,3072]{1,0:T(8,128)(2,1)}, u32[]{:S(2)}, u32[]{:S(2)}) collective-permute-start(bf16[384,3072]{1,0:T(8,128)(2,1)} %param.17), channel_id=1, source_target_pairs={{0,1},{1,0},{2,3},{3,2},{4,5},{5,4},{6,7},{7,6},{8,9},{9,8},{10,11... | collective-permute-start | bytes 7077896 | tf_op jit(solution)/shard_map/ppermute | solution.py:397
  3.9 2.8 %collective-permute-start.1 = (bf16[4,128,384]{2,1,0:T(8,128)(2,1)S(1)}, bf16[4,128,384]{2,1,0:T(8,128)(2,1)S(1)}, u32[]{:S(2)}, u32[]{:S(2)}) collective-permute-start(bf16[4,128,384]{2,1,0:T(8,128)(2,1)S(1)} %pad_maximum_fusion.2), channel_id=1, source_target_pairs={{0,48},{8,200},{16,0},{24,216},{32,16},{40,232},{48,32},{56,248},{... | collective-permute-start | bytes 1179656 | tf_op jit(solution)/shard_map/ppermute | solution.py:425
  8.4 7.9 %collective-permute-done.1 = bf16[4,128,384]{2,1,0:T(8,128)(2,1)S(1)} collective-permute-done((bf16[4,128,384]{2,1,0:T(8,128)(2,1)S(1)}, bf16[4,128,384]{2,1,0:T(8,128)(2,1)S(1)}, u32[]{:S(2)}, u32[]{:S(2)}) %collective-permute-start.1) | collective-permute-done | bytes 393248 | tf_op jit(solution)/shard_map/ppermute | solution.py:425
  16.3 3.9 %collective-permute-done.3 = bf16[4,128,384]{2,1,0:T(8,128)(2,1)S(1)} collective-permute-done((bf16[4,128,384]{2,1,0:T(8,128)(2,1)S(1)}, bf16[4,128,384]{2,1,0:T(8,128)(2,1)S(1)}, u32[]{:S(2)}, u32[]{:S(2)}) %collective-permute-start.3) | collective-permute-done | bytes 393248 | tf_op jit(solution)/shard_map/ppermute | solution.py:425
  23.3 2.2 %collective-permute-start.6 = (bf16[16,128,384]{2,1,0:T(8,128)(2,1)}, bf16[16,128,384]{2,1,0:T(8,128)(2,1)}, u32[]{:S(2)}, u32[]{:S(2)}) collective-permute-start(bf16[16,128,384]{2,1,0:T(8,128)(2,1)} %pad_maximum_fusion.refs_5_), channel_id=1, source_target_pairs={{0,64},{8,24},{16,80},{24,40},{32,96},{40,56},{48,112},{56,8},{64,... | collective-permute-start | bytes 4718600 | tf_op jit(solution)/shard_map/ppermute | solution.py:425
  26.0 1.4 multiply_sine_fusion
  27.5 3.0 %copy-done = bf16[3,3072,384]{2,1,0:T(8,128)(2,1)S(1)} copy-done((bf16[3,3072,384]{2,1,0:T(8,128)(2,1)S(1)}, bf16[3,3072,384]{2,1,0:T(8,128)(2,1)}, u32[]{:S(2)}) %copy-start) | copy-done | bytes 7077912
  30.5 4.6 %project.1.refs_4_ = bf16[3,256,384]{2,1,0:T(8,128)(2,1)S(1)} custom-call(bf16[256,3072]{1,0:T(8,128)(2,1)S(1)} %copy-done.1, bf16[1,3072]{1,0:T(2,128)(2,1)S(1)} %broadcast_in_dim.40.gain_ref, bf16[3,3072,384]{2,1,0:T(8,128)(2,1)S(1)} %copy-done, f32[256,384]{1,0:T(8,128)S(1)} %get-tuple-element.87.cos_ref, f32[256,384]{1,0:T(8,128)S(1)} %get-tuple-element.86.sin_ref), custom_call_target="tpu_custom_call" | custom-call | tf_op jit(solution)/shard_map/project/pallas_call | solution.py:58
  35.1 25.4 %collective-permute-done.4.refs_6_ = bf16[16,128,384]{2,1,0:T(8,128)(2,1)} collective-permute-done((bf16[16,128,384]{2,1,0:T(8,128)(2,1)}, bf16[16,128,384]{2,1,0:T(8,128)(2,1)}, u32[]{:S(2)}, u32[]{:S(2)}) %collective-permute-start.4) | collective-permute-done | bytes 1572896 | tf_op jit(solution)/shard_map/ppermute | solution.py:425
  62.7 2.6 %collective-permute-done.12 = bf16[48,2048]{1,0:T(8,128)(2,1)S(1)} collective-permute-done((bf16[48,2048]{1,0:T(8,128)(2,1)S(1)}, bf16[48,2048]{1,0:T(8,128)(2,1)S(1)}, u32[]{:S(2)}, u32[]{:S(2)}) %collective-permute-start.12) | collective-permute-done | bytes 196640 | tf_op jit(solution)/shard_map/ppermute | solution.py:413
  67.7 1.4 collective-permute-start.16
  69.9 6.0 %attend.1 = bf16[2,128,384]{2,1,0:T(8,128)(2,1)S(1)} custom-call(s32[4]{0:T(128)S(1)} %pad_add_fusion.refs_0_, s32[8]{0:T(128)S(1)} %copy-done.3, s32[64]{0:T(128)S(1)} %copy-done.4, s32[128]{0:T(128)S(1)} %copy-done.5, bf16[3,256,384]{2,1,0:T(8,128)(2,1)S(1)} %project.1.refs_4_, bf16[16,128,384]{2,1,0:T(8,128)(2,1)} %pad_maximum_fusion.refs_5_, ...), custom_call_target="tpu_custom_call" | custom-call | tf_op jit(solution)/shard_map/attend/pallas_call | solution.py:179
  75.9 3.7 %collective-permute-done.15 = bf16[96,2048]{1,0:T(8,128)(2,1)} collective-permute-done((bf16[96,2048]{1,0:T(8,128)(2,1)S(1)}, bf16[96,2048]{1,0:T(8,128)(2,1)}, u32[]{:S(2)}, u32[]{:S(2)}) %collective-permute-start.15) | collective-permute-done | bytes 393248 | tf_op jit(solution)/shard_map/ppermute | solution.py:425
  81.5 2.6 %collective-permute-start.22 = (bf16[384,2048]{1,0:T(8,128)(2,1)S(1)}, bf16[384,2048]{1,0:T(8,128)(2,1)S(1)}, u32[]{:S(2)}, u32[]{:S(2)}) collective-permute-start(bf16[384,2048]{1,0:T(8,128)(2,1)S(1)} %pad_maximum_fusion.1.refs_3_), channel_id=1, source_target_pairs={{0,64},{8,24},{16,80},{24,40},{32,96},{40,56},{48,112},{56,8},{64,... | collective-permute-start | bytes 4718600 | tf_op jit(solution)/shard_map/ppermute | solution.py:425
  86.3 2.5 %collective-permute-done.17 = bf16[128,384]{1,0:T(8,128)(2,1)S(1)} collective-permute-done((bf16[128,384]{1,0:T(8,128)(2,1)S(1)}, bf16[128,384]{1,0:T(8,128)(2,1)S(1)}, u32[]{:S(2)}, u32[]{:S(2)}) %collective-permute-start.17) | collective-permute-done | bytes 98336 | tf_op jit(solution)/shard_map/ppermute | solution.py:397
  89.0 2.3 %fusion = bf16[128,3072]{1,0:T(8,128)(2,1)S(1)} fusion(f32[128,3072]{1,0:T(8,128)S(1)} %fusion.8, bf16[128,384]{1,0:T(8,128)(2,1)S(1)} %collective-permute-done.17, bf16[384,3072]{1,0:T(8,128)(2,1)} %collective-permute-done.8), kind=kOutput, calls=%fused_computation.1 | convolution fusion | flops 302776320 | bytes 4816896 | tf_op jit(solution)/shard_map/dot_general | solution.py:512
  91.4 6.7 %collective-permute-start.18 = (bf16[32,3200]{1,0:T(8,128)(2,1)S(1)}, bf16[32,3200]{1,0:T(8,128)(2,1)S(1)}, u32[]{:S(2)}, u32[]{:S(2)}) collective-permute-start(bf16[32,3200]{1,0:T(8,128)(2,1)S(1)} %get-tuple-element.72), channel_id=1, source_target_pairs={{0,4},{1,5},{2,6},{3,7},{4,0},{5,1},{6,2},{7,3},{8,12},{9,13},{10,... | collective-permute-start | bytes 614408 | tf_op jit(solution)/shard_map/ppermute | solution.py:393
  98.1 1.5 collective-permute-start.19
  99.6 2.7 %collective-permute-start.20 = (bf16[32,3200]{1,0:T(8,128)(2,1)S(1)}, bf16[32,3200]{1,0:T(8,128)(2,1)S(1)}, u32[]{:S(2)}, u32[]{:S(2)}) collective-permute-start(bf16[32,3200]{1,0:T(8,128)(2,1)S(1)} %get-tuple-element.70), channel_id=1, source_target_pairs={{0,6},{1,7},{2,0},{3,1},{4,2},{5,3},{6,4},{7,5},{8,14},{9,15},{10,... | collective-permute-start | bytes 614408 | tf_op jit(solution)/shard_map/ppermute | solution.py:393
  102.2 4.0 %collective-permute-done.18.refs_1_ = bf16[32,3200]{1,0:T(8,128)(2,1)S(1)} collective-permute-done((bf16[32,3200]{1,0:T(8,128)(2,1)S(1)}, bf16[32,3200]{1,0:T(8,128)(2,1)S(1)}, u32[]{:S(2)}, u32[]{:S(2)}) %collective-permute-start.18) | collective-permute-done | bytes 204832 | tf_op jit(solution)/shard_map/ppermute | solution.py:393
  106.3 4.7 %collective-permute-done.19.refs_2_ = bf16[32,3200]{1,0:T(8,128)(2,1)S(1)} collective-permute-done((bf16[32,3200]{1,0:T(8,128)(2,1)S(1)}, bf16[32,3200]{1,0:T(8,128)(2,1)S(1)}, u32[]{:S(2)}, u32[]{:S(2)}) %collective-permute-start.19) | collective-permute-done | bytes 204832 | tf_op jit(solution)/shard_map/ppermute | solution.py:393
  111.0 2.5 %collective-permute-done.20.refs_3_ = bf16[32,3200]{1,0:T(8,128)(2,1)S(1)} collective-permute-done((bf16[32,3200]{1,0:T(8,128)(2,1)S(1)}, bf16[32,3200]{1,0:T(8,128)(2,1)S(1)}, u32[]{:S(2)}, u32[]{:S(2)}) %collective-permute-start.20) | collective-permute-done | bytes 204832 | tf_op jit(solution)/shard_map/ppermute | solution.py:393
  114.6 2.9 %collective-permute-start.23 = (bf16[32,3200]{1,0:T(8,128)(2,1)S(1)}, bf16[32,3200]{1,0:T(8,128)(2,1)S(1)}, u32[]{:S(2)}, u32[]{:S(2)}) collective-permute-start(bf16[32,3200]{1,0:T(8,128)(2,1)S(1)} %settle.1.refs_12_), channel_id=1, source_target_pairs={{0,7},{1,0},{2,1},{3,2},{4,3},{5,4},{6,5},{7,6},{8,15},{9,8},{10,9... | collective-permute-start | bytes 614408 | tf_op jit(solution)/shard_map/ppermute | solution.py:393
  118.7 3.6 %collective-permute-done.23.refs_14_ = bf16[32,3200]{1,0:T(8,128)(2,1)S(1)} collective-permute-done((bf16[32,3200]{1,0:T(8,128)(2,1)S(1)}, bf16[32,3200]{1,0:T(8,128)(2,1)S(1)}, u32[]{:S(2)}, u32[]{:S(2)}) %collective-permute-start.23) | collective-permute-done | bytes 204832 | tf_op jit(solution)/shard_map/ppermute | solution.py:393
  122.3 3.4 %collective-permute-done.24.refs_16_ = bf16[32,3200]{1,0:T(8,128)(2,1)S(1)} collective-permute-done((bf16[32,3200]{1,0:T(8,128)(2,1)S(1)}, bf16[32,3200]{1,0:T(8,128)(2,1)S(1)}, u32[]{:S(2)}, u32[]{:S(2)}) %collective-permute-start.24) | collective-permute-done | bytes 204832 | tf_op jit(solution)/shard_map/ppermute | solution.py:393
  126.2 1.7 collective-permute-start.28
  127.9 11.6 %collective-permute-done.29.refs_5_ = bf16[384,2048]{1,0:T(8,128)(2,1)} collective-permute-done((bf16[384,2048]{1,0:T(8,128)(2,1)S(1)}, bf16[384,2048]{1,0:T(8,128)(2,1)}, u32[]{:S(2)}, u32[]{:S(2)}) %collective-permute-start.29) | collective-permute-done | bytes 1572896 | tf_op jit(solution)/shard_map/ppermute | solution.py:425
  139.6 3.3 %collective-permute-start.32 = (bf16[32,3200]{1,0:T(8,128)(2,1)S(1)}, bf16[32,3200]{1,0:T(8,128)(2,1)S(1)}, u32[]{:S(2)}, u32[]{:S(2)}) collective-permute-start(bf16[32,3200]{1,0:T(8,128)(2,1)S(1)} %collective-permute-done.27.refs_18_), channel_id=1, source_target_pairs={{0,7},{1,0},{2,1},{3,2},{4,3},{5,4},{6,5},{7,6},{8,15},{9,8},{10,9... | collective-permute-start | bytes 614408 | tf_op jit(solution)/shard_map/ppermute | solution.py:393
  143.0 1.7 collective-permute-start.34
  146.3 5.9 %collective-permute-done.34.refs_26_ = bf16[16,3200]{1,0:T(8,128)(2,1)S(1)} collective-permute-done((bf16[16,3200]{1,0:T(8,128)(2,1)S(1)}, bf16[16,3200]{1,0:T(8,128)(2,1)S(1)}, u32[]{:S(2)}, u32[]{:S(2)}) %collective-permute-start.34) | collective-permute-done | bytes 102432 | tf_op jit(solution)/shard_map/ppermute | solution.py:393
  154.3 10.8 %score.1 = f32[8,512]{1,0:T(8,128)S(1)} custom-call(s32[13]{0:T(128)S(1)} %stack.68.refs_0_, bf16[16,3072]{1,0:T(8,128)(2,1)S(1)} %copy-done.2, bf16[1,3072]{1,0:T(2,128)(2,1)S(1)} %broadcast_in_dim.39.gain_ref.refs_2_, bf16[384,2048]{1,0:T(8,128)(2,1)} %copy-done.7, bf16[384,2048]{1,0:T(8,128)(2,1)} %copy-done.13, ...), custom_call_target="tpu_custom_call" | custom-call | flops 6442450944 | bytes 12582912 | tf_op jit(solution)/shard_map/score/pallas_call | solution.py:360
  165.5 14.2 %all_to_all.5 = f32[8,8,512]{2,1,0:T(8,128)S(1)} all-to-all(f32[8,8,512]{2,1,0:T(8,128)S(1)} %broadcast_in_dim.46), channel_id=1, replica_groups=mesh['seq'=32,'tensor'=8] {'tensor'}, dimensions={0} | all-to-all | bytes 262144 | tf_op jit(solution)/shard_map/all_to_all | solution.py:584
  (120 shorter events, 23.7 us)
Async XLA Ops:
  1.8 59.5 %collective-permute-start.8 = (bf16[384,3072]{1,0:T(8,128)(2,1)}, bf16[384,3072]{1,0:T(8,128)(2,1)}, u32[]{:S(2)}, u32[]{:S(2)}) collective-permute-start(bf16[384,3072]{1,0:T(8,128)(2,1)} %param.17), channel_id=1, source_target_pairs={{0,1},{1,0},{2,3},{3,2},{4,5},{5,4},{6,7},{7,6},{8,9},{9,8},{10,11... | collective-permute-start | bytes 7077896 | tf_op jit(solution)/shard_map/ppermute | solution.py:397
  3.9 12.4 %collective-permute-start.1 = (bf16[4,128,384]{2,1,0:T(8,128)(2,1)S(1)}, bf16[4,128,384]{2,1,0:T(8,128)(2,1)S(1)}, u32[]{:S(2)}, u32[]{:S(2)}) collective-permute-start(bf16[4,128,384]{2,1,0:T(8,128)(2,1)S(1)} %pad_maximum_fusion.2), channel_id=1, source_target_pairs={{0,48},{8,200},{16,0},{24,216},{32,16},{40,232},{48,32},{56,248},{... | collective-permute-start | bytes 1179656 | tf_op jit(solution)/shard_map/ppermute | solution.py:425
  6.8 9.5 %collective-permute-start.2 = (bf16[4,128,384]{2,1,0:T(8,128)(2,1)S(1)}, bf16[4,128,384]{2,1,0:T(8,128)(2,1)S(1)}, u32[]{:S(2)}, u32[]{:S(2)}) collective-permute-start(bf16[4,128,384]{2,1,0:T(8,128)(2,1)S(1)} %pad_maximum_fusion.2), channel_id=1, source_target_pairs={{0,32},{8,136},{16,48},{24,152},{32,0},{40,168},{48,16},{56,184},{... | collective-permute-start | bytes 1179656 | tf_op jit(solution)/shard_map/ppermute | solution.py:425
  7.6 12.7 %collective-permute-start.3 = (bf16[4,128,384]{2,1,0:T(8,128)(2,1)S(1)}, bf16[4,128,384]{2,1,0:T(8,128)(2,1)S(1)}, u32[]{:S(2)}, u32[]{:S(2)}) collective-permute-start(bf16[4,128,384]{2,1,0:T(8,128)(2,1)S(1)} %pad_maximum_fusion.2), channel_id=1, source_target_pairs={{0,16},{8,72},{16,32},{24,88},{32,48},{40,104},{48,0},{56,120},{64... | collective-permute-start | bytes 1179656 | tf_op jit(solution)/shard_map/ppermute | solution.py:425
  21.6 38.8 %collective-permute-start.4 = (bf16[16,128,384]{2,1,0:T(8,128)(2,1)}, bf16[16,128,384]{2,1,0:T(8,128)(2,1)}, u32[]{:S(2)}, u32[]{:S(2)}) collective-permute-start(bf16[16,128,384]{2,1,0:T(8,128)(2,1)} %pad_maximum_fusion.refs_5_), channel_id=1, source_target_pairs={{0,192},{8,56},{16,208},{24,8},{32,224},{40,24},{48,240},{56,40},{... | collective-permute-start | bytes 4718600 | tf_op jit(solution)/shard_map/ppermute | solution.py:425
  22.4 38.1 %collective-permute-start.5 = (bf16[16,128,384]{2,1,0:T(8,128)(2,1)}, bf16[16,128,384]{2,1,0:T(8,128)(2,1)}, u32[]{:S(2)}, u32[]{:S(2)}) collective-permute-start(bf16[16,128,384]{2,1,0:T(8,128)(2,1)} %pad_maximum_fusion.refs_5_), channel_id=1, source_target_pairs={{0,128},{8,40},{16,144},{24,56},{32,160},{40,8},{48,176},{56,24},{... | collective-permute-start | bytes 4718600 | tf_op jit(solution)/shard_map/ppermute | solution.py:425
  23.3 38.0 %collective-permute-start.6 = (bf16[16,128,384]{2,1,0:T(8,128)(2,1)}, bf16[16,128,384]{2,1,0:T(8,128)(2,1)}, u32[]{:S(2)}, u32[]{:S(2)}) collective-permute-start(bf16[16,128,384]{2,1,0:T(8,128)(2,1)} %pad_maximum_fusion.refs_5_), channel_id=1, source_target_pairs={{0,64},{8,24},{16,80},{24,40},{32,96},{40,56},{48,112},{56,8},{64,... | collective-permute-start | bytes 4718600 | tf_op jit(solution)/shard_map/ppermute | solution.py:425
  25.5 35.8 %collective-permute-start.7 = (bf16[16,128,384]{2,1,0:T(8,128)(2,1)}, bf16[16,128,384]{2,1,0:T(8,128)(2,1)}, u32[]{:S(2)}, u32[]{:S(2)}) collective-permute-start(bf16[16,128,384]{2,1,0:T(8,128)(2,1)} %pad_maximum_fusion.refs_5_), channel_id=1, source_target_pairs={{0,8},{8,0},{16,24},{24,16},{32,40},{40,32},{48,56},{56,48},{64,72... | collective-permute-start | bytes 4718600 | tf_op jit(solution)/shard_map/ppermute | solution.py:413
  61.4 6.3 %collective-permute-start.10 = (bf16[16,128,384]{2,1,0:T(8,128)(2,1)}, bf16[16,128,384]{2,1,0:T(8,128)(2,1)}, u32[]{:S(2)}, u32[]{:S(2)}) collective-permute-start(bf16[16,128,384]{2,1,0:T(8,128)(2,1)} %collective-permute-done.5.refs_7_), channel_id=1, source_target_pairs={{0,8},{8,0},{16,24},{24,16},{32,40},{40,32},{48,56},{56,48},{64,72... | collective-permute-start | bytes 4718600 | tf_op jit(solution)/shard_map/ppermute | solution.py:413
  61.9 8.0 %collective-permute-start.11 = (bf16[16,128,384]{2,1,0:T(8,128)(2,1)}, bf16[16,128,384]{2,1,0:T(8,128)(2,1)}, u32[]{:S(2)}, u32[]{:S(2)}) collective-permute-start(bf16[16,128,384]{2,1,0:T(8,128)(2,1)} %collective-permute-done.6.refs_8_), channel_id=1, source_target_pairs={{0,8},{8,0},{16,24},{24,16},{32,40},{40,32},{48,56},{56,48},{64,72... | collective-permute-start | bytes 4718600 | tf_op jit(solution)/shard_map/ppermute | solution.py:413
  65.4 10.6 %collective-permute-start.13 = (bf16[96,2048]{1,0:T(8,128)(2,1)S(1)}, bf16[96,2048]{1,0:T(8,128)(2,1)S(1)}, u32[]{:S(2)}, u32[]{:S(2)}) collective-permute-start(bf16[96,2048]{1,0:T(8,128)(2,1)S(1)} %pad_maximum_fusion.3), channel_id=1, source_target_pairs={{0,48},{8,200},{16,0},{24,216},{32,16},{40,232},{48,32},{56,248},{... | collective-permute-start | bytes 1179656 | tf_op jit(solution)/shard_map/ppermute | solution.py:425
  66.0 9.9 %collective-permute-start.14 = (bf16[96,2048]{1,0:T(8,128)(2,1)S(1)}, bf16[96,2048]{1,0:T(8,128)(2,1)S(1)}, u32[]{:S(2)}, u32[]{:S(2)}) collective-permute-start(bf16[96,2048]{1,0:T(8,128)(2,1)S(1)} %pad_maximum_fusion.3), channel_id=1, source_target_pairs={{0,32},{8,136},{16,48},{24,152},{32,0},{40,168},{48,16},{56,184},{... | collective-permute-start | bytes 1179656 | tf_op jit(solution)/shard_map/ppermute | solution.py:425
  66.8 12.8 %collective-permute-start.15 = (bf16[96,2048]{1,0:T(8,128)(2,1)S(1)}, bf16[96,2048]{1,0:T(8,128)(2,1)}, u32[]{:S(2)}, u32[]{:S(2)}) collective-permute-start(bf16[96,2048]{1,0:T(8,128)(2,1)S(1)} %pad_maximum_fusion.3), channel_id=1, source_target_pairs={{0,16},{8,72},{16,32},{24,88},{32,48},{40,104},{48,0},{56,120},{64... | collective-permute-start | bytes 1179656 | tf_op jit(solution)/shard_map/ppermute | solution.py:425
  67.7 8.2 %collective-permute-start.16 = (bf16[384,128]{0,1:T(8,128)(2,1)S(1)}, bf16[384,128]{0,1:T(8,128)(2,1)S(1)}, u32[]{:S(2)}, u32[]{:S(2)}) collective-permute-start(bf16[384,128]{0,1:T(8,128)(2,1)S(1)} %pad.4), channel_id=1, source_target_pairs={{0,1},{1,0},{2,3},{3,2},{4,5},{5,4},{6,7},{7,6},{8,9},{9,8},{10,11... | collective-permute-start | bytes 294920 | tf_op jit(solution)/shard_map/ppermute | solution.py:397
  80.8 32.7 %collective-permute-start.21 = (bf16[384,2048]{1,0:T(8,128)(2,1)S(1)}, bf16[384,2048]{1,0:T(8,128)(2,1)S(1)}, u32[]{:S(2)}, u32[]{:S(2)}) collective-permute-start(bf16[384,2048]{1,0:T(8,128)(2,1)S(1)} %pad_maximum_fusion.1.refs_3_), channel_id=1, source_target_pairs={{0,192},{8,56},{16,208},{24,8},{32,224},{40,24},{48,240},{56,40},{... | collective-permute-start | bytes 4718600 | tf_op jit(solution)/shard_map/ppermute | solution.py:425
  81.5 32.0 %collective-permute-start.22 = (bf16[384,2048]{1,0:T(8,128)(2,1)S(1)}, bf16[384,2048]{1,0:T(8,128)(2,1)S(1)}, u32[]{:S(2)}, u32[]{:S(2)}) collective-permute-start(bf16[384,2048]{1,0:T(8,128)(2,1)S(1)} %pad_maximum_fusion.1.refs_3_), channel_id=1, source_target_pairs={{0,64},{8,24},{16,80},{24,40},{32,96},{40,56},{48,112},{56,8},{64,... | collective-permute-start | bytes 4718600 | tf_op jit(solution)/shard_map/ppermute | solution.py:425
  91.4 14.8 %collective-permute-start.18 = (bf16[32,3200]{1,0:T(8,128)(2,1)S(1)}, bf16[32,3200]{1,0:T(8,128)(2,1)S(1)}, u32[]{:S(2)}, u32[]{:S(2)}) collective-permute-start(bf16[32,3200]{1,0:T(8,128)(2,1)S(1)} %get-tuple-element.72), channel_id=1, source_target_pairs={{0,4},{1,5},{2,6},{3,7},{4,0},{5,1},{6,2},{7,3},{8,12},{9,13},{10,... | collective-permute-start | bytes 614408 | tf_op jit(solution)/shard_map/ppermute | solution.py:393
  98.1 12.8 %collective-permute-start.19 = (bf16[32,3200]{1,0:T(8,128)(2,1)S(1)}, bf16[32,3200]{1,0:T(8,128)(2,1)S(1)}, u32[]{:S(2)}, u32[]{:S(2)}) collective-permute-start(bf16[32,3200]{1,0:T(8,128)(2,1)S(1)} %get-tuple-element.73), channel_id=1, source_target_pairs={{0,2},{1,3},{2,4},{3,5},{4,6},{5,7},{6,0},{7,1},{8,10},{9,11},{10,... | collective-permute-start | bytes 614408 | tf_op jit(solution)/shard_map/ppermute | solution.py:393
  99.6 13.9 %collective-permute-start.20 = (bf16[32,3200]{1,0:T(8,128)(2,1)S(1)}, bf16[32,3200]{1,0:T(8,128)(2,1)S(1)}, u32[]{:S(2)}, u32[]{:S(2)}) collective-permute-start(bf16[32,3200]{1,0:T(8,128)(2,1)S(1)} %get-tuple-element.70), channel_id=1, source_target_pairs={{0,6},{1,7},{2,0},{3,1},{4,2},{5,3},{6,4},{7,5},{8,14},{9,15},{10,... | collective-permute-start | bytes 614408 | tf_op jit(solution)/shard_map/ppermute | solution.py:393
  113.5 12.2 %collective-permute-start.25 = (bf16[384,2048]{1,0:T(8,128)(2,1)S(1)}, bf16[384,2048]{1,0:T(8,128)(2,1)S(1)}, u32[]{:S(2)}, u32[]{:S(2)}) collective-permute-start(bf16[384,2048]{1,0:T(8,128)(2,1)S(1)} %pad_maximum_fusion.1.refs_3_), channel_id=1, source_target_pairs={{0,8},{8,0},{16,24},{24,16},{32,40},{40,32},{48,56},{56,48},{64,72... | collective-permute-start | bytes 4718600 | tf_op jit(solution)/shard_map/ppermute | solution.py:413
  113.6 12.1 %collective-permute-start.26 = (bf16[384,2048]{1,0:T(8,128)(2,1)S(1)}, bf16[384,2048]{1,0:T(8,128)(2,1)S(1)}, u32[]{:S(2)}, u32[]{:S(2)}) collective-permute-start(bf16[384,2048]{1,0:T(8,128)(2,1)S(1)} %collective-permute-done.21.refs_4_), channel_id=1, source_target_pairs={{0,8},{8,0},{16,24},{24,16},{32,40},{40,32},{48,56},{56,48},{64,72... | collective-permute-start | bytes 4718600 | tf_op jit(solution)/shard_map/ppermute | solution.py:413
  114.6 7.7 %collective-permute-start.23 = (bf16[32,3200]{1,0:T(8,128)(2,1)S(1)}, bf16[32,3200]{1,0:T(8,128)(2,1)S(1)}, u32[]{:S(2)}, u32[]{:S(2)}) collective-permute-start(bf16[32,3200]{1,0:T(8,128)(2,1)S(1)} %settle.1.refs_12_), channel_id=1, source_target_pairs={{0,7},{1,0},{2,1},{3,2},{4,3},{5,4},{6,5},{7,6},{8,15},{9,8},{10,9... | collective-permute-start | bytes 614408 | tf_op jit(solution)/shard_map/ppermute | solution.py:393
  117.5 8.2 %collective-permute-start.24 = (bf16[32,3200]{1,0:T(8,128)(2,1)S(1)}, bf16[32,3200]{1,0:T(8,128)(2,1)S(1)}, u32[]{:S(2)}, u32[]{:S(2)}) collective-permute-start(bf16[32,3200]{1,0:T(8,128)(2,1)S(1)} %settle.1.refs_12_), channel_id=1, source_target_pairs={{0,1},{1,2},{2,3},{3,4},{4,5},{5,6},{6,7},{7,0},{8,9},{9,10},{10,1... | collective-permute-start | bytes 614408 | tf_op jit(solution)/shard_map/ppermute | solution.py:393
  117.5 22.0 %collective-permute-start.29 = (bf16[384,2048]{1,0:T(8,128)(2,1)S(1)}, bf16[384,2048]{1,0:T(8,128)(2,1)}, u32[]{:S(2)}, u32[]{:S(2)}) collective-permute-start(bf16[384,2048]{1,0:T(8,128)(2,1)S(1)} %pad_maximum_fusion.1.refs_3_), channel_id=1, source_target_pairs={{0,128},{8,40},{16,144},{24,56},{32,160},{40,8},{48,176},{56,24},{... | collective-permute-start | bytes 4718600 | tf_op jit(solution)/shard_map/ppermute | solution.py:425
  125.7 13.8 %collective-permute-start.30 = (bf16[384,2048]{1,0:T(8,128)(2,1)S(1)}, bf16[384,2048]{1,0:T(8,128)(2,1)S(1)}, u32[]{:S(2)}, u32[]{:S(2)}) collective-permute-start(bf16[384,2048]{1,0:T(8,128)(2,1)S(1)} %collective-permute-done.22.refs_6_), channel_id=1, source_target_pairs={{0,8},{8,0},{16,24},{24,16},{32,40},{40,32},{48,56},{56,48},{64,72... | collective-permute-start | bytes 4718600 | tf_op jit(solution)/shard_map/ppermute | solution.py:413
  125.8 13.7 %collective-permute-start.27 = (bf16[32,3200]{1,0:T(8,128)(2,1)S(1)}, bf16[32,3200]{1,0:T(8,128)(2,1)S(1)}, u32[]{:S(2)}, u32[]{:S(2)}) collective-permute-start(bf16[32,3200]{1,0:T(8,128)(2,1)S(1)} %collective-permute-done.23.refs_14_), channel_id=1, source_target_pairs={{0,7},{1,0},{2,1},{3,2},{4,3},{5,4},{6,5},{7,6},{8,15},{9,8},{10,9... | collective-permute-start | bytes 614408 | tf_op jit(solution)/shard_map/ppermute | solution.py:393
  126.2 13.3 %collective-permute-start.28 = (bf16[32,3200]{1,0:T(8,128)(2,1)S(1)}, bf16[32,3200]{1,0:T(8,128)(2,1)S(1)}, u32[]{:S(2)}, u32[]{:S(2)}) collective-permute-start(bf16[32,3200]{1,0:T(8,128)(2,1)S(1)} %collective-permute-done.24.refs_16_), channel_id=1, source_target_pairs={{0,1},{1,2},{2,3},{3,4},{4,5},{5,6},{6,7},{7,0},{8,9},{9,10},{10,1... | collective-permute-start | bytes 614408 | tf_op jit(solution)/shard_map/ppermute | solution.py:393
  139.5 14.7 %collective-permute-start.31 = (bf16[384,2048]{1,0:T(8,128)(2,1)}, bf16[384,2048]{1,0:T(8,128)(2,1)}, u32[]{:S(2)}, u32[]{:S(2)}) collective-permute-start(bf16[384,2048]{1,0:T(8,128)(2,1)} %collective-permute-done.29.refs_5_), channel_id=1, source_target_pairs={{0,8},{8,0},{16,24},{24,16},{32,40},{40,32},{48,56},{56,48},{64,72... | collective-permute-start | bytes 4718600 | tf_op jit(solution)/shard_map/ppermute | solution.py:413
  139.6 13.7 %collective-permute-start.32 = (bf16[32,3200]{1,0:T(8,128)(2,1)S(1)}, bf16[32,3200]{1,0:T(8,128)(2,1)S(1)}, u32[]{:S(2)}, u32[]{:S(2)}) collective-permute-start(bf16[32,3200]{1,0:T(8,128)(2,1)S(1)} %collective-permute-done.27.refs_18_), channel_id=1, source_target_pairs={{0,7},{1,0},{2,1},{3,2},{4,3},{5,4},{6,5},{7,6},{8,15},{9,8},{10,9... | collective-permute-start | bytes 614408 | tf_op jit(solution)/shard_map/ppermute | solution.py:393
  142.9 11.3 %collective-permute-start.33 = (bf16[32,3200]{1,0:T(8,128)(2,1)S(1)}, bf16[32,3200]{1,0:T(8,128)(2,1)S(1)}, u32[]{:S(2)}, u32[]{:S(2)}) collective-permute-start(bf16[32,3200]{1,0:T(8,128)(2,1)S(1)} %collective-permute-done.28.refs_20_), channel_id=1, source_target_pairs={{0,1},{1,2},{2,3},{3,4},{4,5},{5,6},{6,7},{7,0},{8,9},{9,10},{10,1... | collective-permute-start | bytes 614408 | tf_op jit(solution)/shard_map/ppermute | solution.py:393
  143.0 9.3 %collective-permute-start.34 = (bf16[16,3200]{1,0:T(8,128)(2,1)S(1)}, bf16[16,3200]{1,0:T(8,128)(2,1)S(1)}, u32[]{:S(2)}, u32[]{:S(2)}) collective-permute-start(bf16[16,3200]{1,0:T(8,128)(2,1)S(1)} %slice.53), channel_id=1, source_target_pairs={{0,6},{1,7},{2,0},{3,1},{4,2},{5,3},{6,4},{7,5},{8,14},{9,15},{10,... | collective-permute-start | bytes 307208 | tf_op jit(solution)/shard_map/ppermute | solution.py:393
  144.7 8.7 %collective-permute-start.35 = (bf16[16,3200]{1,0:T(8,128)(2,1)S(1)}, bf16[16,3200]{1,0:T(8,128)(2,1)S(1)}, u32[]{:S(2)}, u32[]{:S(2)}) collective-permute-start(bf16[16,3200]{1,0:T(8,128)(2,1)S(1)} %slice.54), channel_id=1, source_target_pairs={{0,2},{1,3},{2,4},{3,5},{4,6},{5,7},{6,0},{7,1},{8,10},{9,11},{10,... | collective-permute-start | bytes 307208 | tf_op jit(solution)/shard_map/ppermute | solution.py:393
  (22 other events, 435.4 us)

commit v6 on v5

--- a/solution.py
+++ b/solution.py
@@ -485,12 +485,12 @@
         jnp.cos(angles),
         jnp.sin(angles),
     )
-    ahead, near, qkv, head_columns, partner_weights = lax.optimization_barrier(
-        (ahead, near, qkv, head.T, partner_weights)
+    half = head.shape[1] // 2
+    head_pair = start_pair(head.T[:half], head.T[half:])
+    ahead, near, qkv, head_pair, partner_weights = lax.optimization_barrier(
+        (ahead, near, qkv, head_pair, partner_weights)
     )
     pieces = [line] + ahead + [near] + [crossed(piece) for piece in ahead]
-    half = head_columns.shape[0] // 2
-    head_pair = start_pair(head_columns[:half], head_columns[half:])
     head_line = along_first(head_pair)
     attended = attend(
         jnp.stack([first, me // 8, me // 2 % 4, me % 2]).astype(jnp.int32),

time: 182 us -> 181 us (level)
  waiting for transfers between devices: 85.4 us -> 83.2 us
    ppermute x12, waiting for transfers between devices: 53.4 us -> 49.5 us  [turned(): return lax.ppermute(value, 'seq', [(i, target(i)) for i in range(32)])]
  transfers between devices with their start and end apart: 36 -> 36, of which waited for: 17 -> 17; matrix products, arithmetic and copies ran while one was open for 4% -> 4% of each run, Pallas kernels for 6% -> 7%
where the time goes in v6:
time: 181 us; the launch traced here: 178 us
  waiting for transfers between devices  83.2 us (46%)
  starting transfers between devices  42.9 us (24%)
  Pallas kernels  22.7 us (13%)
  blocking collectives  14.2 us (8%)
  other arithmetic  5.75 us (3%)
  local copies, waits for them, and re-layouts  4.62 us (3%)
  matrix products  3.18 us (2%)
    ppermute x12, waiting for transfers between devices, turned(): return lax.ppermute(value, 'seq', [(i, target(i)) for i in range(32)])  49.5 us
    ppermute x11, waiting for transfers between devices, shifted(): lax.ppermute(value, 'tensor', [(i, (i + step) % ranks) for i in range(ran...  26.5 us
    ppermute x11, starting transfers between devices, shifted(): lax.ppermute(value, 'tensor', [(i, (i + step) % ranks) for i in range(ran...  22.2 us
    ppermute x12, starting transfers between devices, turned(): return lax.ppermute(value, 'seq', [(i, target(i)) for i in range(32)])  14.4 us
    all_to_all x1, blocking collectives, local(): lax.all_to_all(jnp.broadcast_to(ordered[None], (ranks, 8, 2 * tok_rows)),...  14.2 us
    pallas_call x1, Pallas kernels, score(): pl.pallas_call(score_kernel, grid_spec=pltpu.PrefetchScalarGridSpec(num_s...  10.8 us
    pallas_call x1, Pallas kernels, attend(): pl.pallas_call(attend_kernel, grid_spec=pltpu.PrefetchScalarGridSpec(num_...  6.97 us
    ppermute x3, starting transfers between devices, partnered(): return lax.ppermute(value, 'tensor', [(i, i ^ 1) for i in range(ranks)])  4.79 us
  transfers between devices with their start and end apart: 36, of which 17 were waited for; matrix products, arithmetic and copies ran while one was open for 4% of the time, Pallas kernels for 7%

profile of v6, /device:TPU:24, one launch (start us, length us, event | category | flops | bytes accessed | tf_op | source)
XLA Modules:
  0.0 177.8 jit_solution(14991997914308946274)
XLA Ops:
  1.9 2.0 %collective-permute-start.9 = (bf16[384,3072]{1,0:T(8,128)(2,1)}, bf16[384,3072]{1,0:T(8,128)(2,1)}, u32[]{:S(2)}, u32[]{:S(2)}) collective-permute-start(bf16[384,3072]{1,0:T(8,128)(2,1)} %param.17), channel_id=1, source_target_pairs={{0,1},{1,0},{2,3},{3,2},{4,5},{5,4},{6,7},{7,6},{8,9},{9,8},{10,11... | collective-permute-start | bytes 7077896 | tf_op jit(solution)/shard_map/ppermute | solution.py:397
  3.9 2.8 %collective-permute-start.1 = (bf16[4,128,384]{2,1,0:T(8,128)(2,1)S(1)}, bf16[4,128,384]{2,1,0:T(8,128)(2,1)S(1)}, u32[]{:S(2)}, u32[]{:S(2)}) collective-permute-start(bf16[4,128,384]{2,1,0:T(8,128)(2,1)S(1)} %pad_maximum_fusion.2), channel_id=1, source_target_pairs={{0,48},{8,200},{16,0},{24,216},{32,16},{40,232},{48,32},{56,248},{... | collective-permute-start | bytes 1179656 | tf_op jit(solution)/shard_map/ppermute | solution.py:425
  8.6 7.7 %collective-permute-done.1 = bf16[4,128,384]{2,1,0:T(8,128)(2,1)S(1)} collective-permute-done((bf16[4,128,384]{2,1,0:T(8,128)(2,1)S(1)}, bf16[4,128,384]{2,1,0:T(8,128)(2,1)S(1)}, u32[]{:S(2)}, u32[]{:S(2)}) %collective-permute-start.1) | collective-permute-done | bytes 393248 | tf_op jit(solution)/shard_map/ppermute | solution.py:425
  16.3 3.9 %collective-permute-done.3 = bf16[4,128,384]{2,1,0:T(8,128)(2,1)S(1)} collective-permute-done((bf16[4,128,384]{2,1,0:T(8,128)(2,1)S(1)}, bf16[4,128,384]{2,1,0:T(8,128)(2,1)S(1)}, u32[]{:S(2)}, u32[]{:S(2)}) %collective-permute-start.3) | collective-permute-done | bytes 393248 | tf_op jit(solution)/shard_map/ppermute | solution.py:425
  23.3 2.2 %collective-permute-start.6 = (bf16[16,128,384]{2,1,0:T(8,128)(2,1)}, bf16[16,128,384]{2,1,0:T(8,128)(2,1)}, u32[]{:S(2)}, u32[]{:S(2)}) collective-permute-start(bf16[16,128,384]{2,1,0:T(8,128)(2,1)} %pad_maximum_fusion.refs_5_), channel_id=1, source_target_pairs={{0,64},{8,24},{16,80},{24,40},{32,96},{40,56},{48,112},{56,8},{64,... | collective-permute-start | bytes 4718600 | tf_op jit(solution)/shard_map/ppermute | solution.py:425
  26.0 1.4 multiply_sine_fusion
  27.5 3.0 %copy-done = bf16[3,3072,384]{2,1,0:T(8,128)(2,1)S(1)} copy-done((bf16[3,3072,384]{2,1,0:T(8,128)(2,1)S(1)}, bf16[3,3072,384]{2,1,0:T(8,128)(2,1)}, u32[]{:S(2)}) %copy-start) | copy-done | bytes 7077912
  30.5 4.6 %project.1.refs_4_ = bf16[3,256,384]{2,1,0:T(8,128)(2,1)S(1)} custom-call(bf16[256,3072]{1,0:T(8,128)(2,1)S(1)} %copy-done.1, bf16[1,3072]{1,0:T(2,128)(2,1)S(1)} %broadcast_in_dim.40.gain_ref, bf16[3,3072,384]{2,1,0:T(8,128)(2,1)S(1)} %copy-done, f32[256,384]{1,0:T(8,128)S(1)} %get-tuple-element.87.cos_ref, f32[256,384]{1,0:T(8,128)S(1)} %get-tuple-element.86.sin_ref), custom_call_target="tpu_custom_call" | custom-call | tf_op jit(solution)/shard_map/project/pallas_call | solution.py:58
  35.1 25.4 %collective-permute-done.4.refs_6_ = bf16[16,128,384]{2,1,0:T(8,128)(2,1)} collective-permute-done((bf16[16,128,384]{2,1,0:T(8,128)(2,1)}, bf16[16,128,384]{2,1,0:T(8,128)(2,1)}, u32[]{:S(2)}, u32[]{:S(2)}) %collective-permute-start.4) | collective-permute-done | bytes 1572896 | tf_op jit(solution)/shard_map/ppermute | solution.py:425
  63.4 1.7 collective-permute-done.10.refs_10_
  65.2 2.2 %collective-permute-done.11.refs_11_ = bf16[16,128,384]{2,1,0:T(8,128)(2,1)} collective-permute-done((bf16[16,128,384]{2,1,0:T(8,128)(2,1)}, bf16[16,128,384]{2,1,0:T(8,128)(2,1)}, u32[]{:S(2)}, u32[]{:S(2)}) %collective-permute-start.11) | collective-permute-done | bytes 1572896 | tf_op jit(solution)/shard_map/ppermute | solution.py:413
  69.6 7.0 %attend.1 = bf16[2,128,384]{2,1,0:T(8,128)(2,1)S(1)} custom-call(s32[4]{0:T(128)S(1)} %pad_add_fusion.refs_0_, s32[8]{0:T(128)S(1)} %copy-done.3, s32[64]{0:T(128)S(1)} %copy-done.4, s32[128]{0:T(128)S(1)} %copy-done.5, bf16[3,256,384]{2,1,0:T(8,128)(2,1)S(1)} %project.1.refs_4_, bf16[16,128,384]{2,1,0:T(8,128)(2,1)} %pad_maximum_fusion.refs_5_, ...), custom_call_target="tpu_custom_call" | custom-call | tf_op jit(solution)/shard_map/attend/pallas_call | solution.py:179
  78.2 3.1 %collective-permute-start.22 = (bf16[384,2048]{1,0:T(8,128)(2,1)S(1)}, bf16[384,2048]{1,0:T(8,128)(2,1)S(1)}, u32[]{:S(2)}, u32[]{:S(2)}) collective-permute-start(bf16[384,2048]{1,0:T(8,128)(2,1)S(1)} %pad_maximum_fusion.1.refs_3_), channel_id=1, source_target_pairs={{0,64},{8,24},{16,80},{24,40},{32,96},{40,56},{48,112},{56,8},{64,... | collective-permute-start | bytes 4718600 | tf_op jit(solution)/shard_map/ppermute | solution.py:425
  81.2 1.4 collective-permute-start.17
  83.4 2.5 %collective-permute-done.17 = bf16[128,384]{1,0:T(8,128)(2,1)S(1)} collective-permute-done((bf16[128,384]{1,0:T(8,128)(2,1)S(1)}, bf16[128,384]{1,0:T(8,128)(2,1)S(1)}, u32[]{:S(2)}, u32[]{:S(2)}) %collective-permute-start.17) | collective-permute-done | bytes 98336 | tf_op jit(solution)/shard_map/ppermute | solution.py:397
  86.1 2.3 %fusion = bf16[128,3072]{1,0:T(8,128)(2,1)S(1)} fusion(f32[128,3072]{1,0:T(8,128)S(1)} %fusion.8, bf16[128,384]{1,0:T(8,128)(2,1)S(1)} %collective-permute-done.17, bf16[384,3072]{1,0:T(8,128)(2,1)} %collective-permute-done.9), kind=kOutput, calls=%fused_computation.1 | convolution fusion | flops 302776320 | bytes 4816896 | tf_op jit(solution)/shard_map/dot_general | solution.py:512
  88.5 6.7 %collective-permute-start.18 = (bf16[32,3200]{1,0:T(8,128)(2,1)S(1)}, bf16[32,3200]{1,0:T(8,128)(2,1)S(1)}, u32[]{:S(2)}, u32[]{:S(2)}) collective-permute-start(bf16[32,3200]{1,0:T(8,128)(2,1)S(1)} %get-tuple-element.72), channel_id=1, source_target_pairs={{0,4},{1,5},{2,6},{3,7},{4,0},{5,1},{6,2},{7,3},{8,12},{9,13},{10,... | collective-permute-start | bytes 614408 | tf_op jit(solution)/shard_map/ppermute | solution.py:393
  95.2 1.5 collective-permute-start.19
  96.7 2.7 %collective-permute-start.20 = (bf16[32,3200]{1,0:T(8,128)(2,1)S(1)}, bf16[32,3200]{1,0:T(8,128)(2,1)S(1)}, u32[]{:S(2)}, u32[]{:S(2)}) collective-permute-start(bf16[32,3200]{1,0:T(8,128)(2,1)S(1)} %get-tuple-element.70), channel_id=1, source_target_pairs={{0,6},{1,7},{2,0},{3,1},{4,2},{5,3},{6,4},{7,5},{8,14},{9,15},{10,... | collective-permute-start | bytes 614408 | tf_op jit(solution)/shard_map/ppermute | solution.py:393
  99.3 4.3 %collective-permute-done.18.refs_1_ = bf16[32,3200]{1,0:T(8,128)(2,1)S(1)} collective-permute-done((bf16[32,3200]{1,0:T(8,128)(2,1)S(1)}, bf16[32,3200]{1,0:T(8,128)(2,1)S(1)}, u32[]{:S(2)}, u32[]{:S(2)}) %collective-permute-start.18) | collective-permute-done | bytes 204832 | tf_op jit(solution)/shard_map/ppermute | solution.py:393
  103.7 4.5 %collective-permute-done.19.refs_2_ = bf16[32,3200]{1,0:T(8,128)(2,1)S(1)} collective-permute-done((bf16[32,3200]{1,0:T(8,128)(2,1)S(1)}, bf16[32,3200]{1,0:T(8,128)(2,1)S(1)}, u32[]{:S(2)}, u32[]{:S(2)}) %collective-permute-start.19) | collective-permute-done | bytes 204832 | tf_op jit(solution)/shard_map/ppermute | solution.py:393
  108.1 2.8 %collective-permute-done.20.refs_3_ = bf16[32,3200]{1,0:T(8,128)(2,1)S(1)} collective-permute-done((bf16[32,3200]{1,0:T(8,128)(2,1)S(1)}, bf16[32,3200]{1,0:T(8,128)(2,1)S(1)}, u32[]{:S(2)}, u32[]{:S(2)}) %collective-permute-start.20) | collective-permute-done | bytes 204832 | tf_op jit(solution)/shard_map/ppermute | solution.py:393
  112.0 2.9 %collective-permute-start.23 = (bf16[32,3200]{1,0:T(8,128)(2,1)S(1)}, bf16[32,3200]{1,0:T(8,128)(2,1)S(1)}, u32[]{:S(2)}, u32[]{:S(2)}) collective-permute-start(bf16[32,3200]{1,0:T(8,128)(2,1)S(1)} %settle.1.refs_12_), channel_id=1, source_target_pairs={{0,7},{1,0},{2,1},{3,2},{4,3},{5,4},{6,5},{7,6},{8,15},{9,8},{10,9... | collective-permute-start | bytes 614408 | tf_op jit(solution)/shard_map/ppermute | solution.py:393
  116.1 3.6 %collective-permute-done.23.refs_14_ = bf16[32,3200]{1,0:T(8,128)(2,1)S(1)} collective-permute-done((bf16[32,3200]{1,0:T(8,128)(2,1)S(1)}, bf16[32,3200]{1,0:T(8,128)(2,1)S(1)}, u32[]{:S(2)}, u32[]{:S(2)}) %collective-permute-start.23) | collective-permute-done | bytes 204832 | tf_op jit(solution)/shard_map/ppermute | solution.py:393
  119.7 3.4 %collective-permute-done.24.refs_16_ = bf16[32,3200]{1,0:T(8,128)(2,1)S(1)} collective-permute-done((bf16[32,3200]{1,0:T(8,128)(2,1)S(1)}, bf16[32,3200]{1,0:T(8,128)(2,1)S(1)}, u32[]{:S(2)}, u32[]{:S(2)}) %collective-permute-start.24) | collective-permute-done | bytes 204832 | tf_op jit(solution)/shard_map/ppermute | solution.py:393
  123.6 1.7 collective-permute-start.28
  125.3 11.6 %collective-permute-done.29.refs_5_ = bf16[384,2048]{1,0:T(8,128)(2,1)} collective-permute-done((bf16[384,2048]{1,0:T(8,128)(2,1)S(1)}, bf16[384,2048]{1,0:T(8,128)(2,1)}, u32[]{:S(2)}, u32[]{:S(2)}) %collective-permute-start.29) | collective-permute-done | bytes 1572896 | tf_op jit(solution)/shard_map/ppermute | solution.py:425
  137.0 3.3 %collective-permute-start.32 = (bf16[32,3200]{1,0:T(8,128)(2,1)S(1)}, bf16[32,3200]{1,0:T(8,128)(2,1)S(1)}, u32[]{:S(2)}, u32[]{:S(2)}) collective-permute-start(bf16[32,3200]{1,0:T(8,128)(2,1)S(1)} %collective-permute-done.27.refs_18_), channel_id=1, source_target_pairs={{0,7},{1,0},{2,1},{3,2},{4,3},{5,4},{6,5},{7,6},{8,15},{9,8},{10,9... | collective-permute-start | bytes 614408 | tf_op jit(solution)/shard_map/ppermute | solution.py:393
  140.4 1.7 collective-permute-start.34
  143.8 5.9 %collective-permute-done.34.refs_26_ = bf16[16,3200]{1,0:T(8,128)(2,1)S(1)} collective-permute-done((bf16[16,3200]{1,0:T(8,128)(2,1)S(1)}, bf16[16,3200]{1,0:T(8,128)(2,1)S(1)}, u32[]{:S(2)}, u32[]{:S(2)}) %collective-permute-start.34) | collective-permute-done | bytes 102432 | tf_op jit(solution)/shard_map/ppermute | solution.py:393
  151.7 10.8 %score.1 = f32[8,512]{1,0:T(8,128)S(1)} custom-call(s32[13]{0:T(128)S(1)} %stack.68.refs_0_, bf16[16,3072]{1,0:T(8,128)(2,1)S(1)} %copy-done.2, bf16[1,3072]{1,0:T(2,128)(2,1)S(1)} %broadcast_in_dim.39.gain_ref.refs_2_, bf16[384,2048]{1,0:T(8,128)(2,1)} %copy-done.7, bf16[384,2048]{1,0:T(8,128)(2,1)} %copy-done.13, ...), custom_call_target="tpu_custom_call" | custom-call | flops 6442450944 | bytes 12582912 | tf_op jit(solution)/shard_map/score/pallas_call | solution.py:360
  162.9 14.2 %all_to_all.5 = f32[8,8,512]{2,1,0:T(8,128)S(1)} all-to-all(f32[8,8,512]{2,1,0:T(8,128)S(1)} %broadcast_in_dim.46), channel_id=1, replica_groups=mesh['seq'=32,'tensor'=8] {'tensor'}, dimensions={0} | all-to-all | bytes 262144 | tf_op jit(solution)/shard_map/all_to_all | solution.py:584
  (120 shorter events, 22.0 us)
Async XLA Ops:
  1.9 59.5 %collective-permute-start.9 = (bf16[384,3072]{1,0:T(8,128)(2,1)}, bf16[384,3072]{1,0:T(8,128)(2,1)}, u32[]{:S(2)}, u32[]{:S(2)}) collective-permute-start(bf16[384,3072]{1,0:T(8,128)(2,1)} %param.17), channel_id=1, source_target_pairs={{0,1},{1,0},{2,3},{3,2},{4,5},{5,4},{6,7},{7,6},{8,9},{9,8},{10,11... | collective-permute-start | bytes 7077896 | tf_op jit(solution)/shard_map/ppermute | solution.py:397
  3.9 12.4 %collective-permute-start.1 = (bf16[4,128,384]{2,1,0:T(8,128)(2,1)S(1)}, bf16[4,128,384]{2,1,0:T(8,128)(2,1)S(1)}, u32[]{:S(2)}, u32[]{:S(2)}) collective-permute-start(bf16[4,128,384]{2,1,0:T(8,128)(2,1)S(1)} %pad_maximum_fusion.2), channel_id=1, source_target_pairs={{0,48},{8,200},{16,0},{24,216},{32,16},{40,232},{48,32},{56,248},{... | collective-permute-start | bytes 1179656 | tf_op jit(solution)/shard_map/ppermute | solution.py:425
  6.8 9.5 %collective-permute-start.2 = (bf16[4,128,384]{2,1,0:T(8,128)(2,1)S(1)}, bf16[4,128,384]{2,1,0:T(8,128)(2,1)S(1)}, u32[]{:S(2)}, u32[]{:S(2)}) collective-permute-start(bf16[4,128,384]{2,1,0:T(8,128)(2,1)S(1)} %pad_maximum_fusion.2), channel_id=1, source_target_pairs={{0,32},{8,136},{16,48},{24,152},{32,0},{40,168},{48,16},{56,184},{... | collective-permute-start | bytes 1179656 | tf_op jit(solution)/shard_map/ppermute | solution.py:425
  7.6 12.7 %collective-permute-start.3 = (bf16[4,128,384]{2,1,0:T(8,128)(2,1)S(1)}, bf16[4,128,384]{2,1,0:T(8,128)(2,1)S(1)}, u32[]{:S(2)}, u32[]{:S(2)}) collective-permute-start(bf16[4,128,384]{2,1,0:T(8,128)(2,1)S(1)} %pad_maximum_fusion.2), channel_id=1, source_target_pairs={{0,16},{8,72},{16,32},{24,88},{32,48},{40,104},{48,0},{56,120},{64... | collective-permute-start | bytes 1179656 | tf_op jit(solution)/shard_map/ppermute | solution.py:425
  8.5 17.0 %collective-permute-start.8 = (bf16[48,2048]{1,0:T(8,128)(2,1)S(1)}, bf16[48,2048]{1,0:T(8,128)(2,1)S(1)}, u32[]{:S(2)}, u32[]{:S(2)}) collective-permute-start(bf16[48,2048]{1,0:T(8,128)(2,1)S(1)} %get-tuple-element.75), channel_id=1, source_target_pairs={{0,8},{8,0},{16,24},{24,16},{32,40},{40,32},{48,56},{56,48},{64,72... | collective-permute-start | bytes 589832 | tf_op jit(solution)/shard_map/ppermute | solution.py:413
  21.7 38.8 %collective-permute-start.4 = (bf16[16,128,384]{2,1,0:T(8,128)(2,1)}, bf16[16,128,384]{2,1,0:T(8,128)(2,1)}, u32[]{:S(2)}, u32[]{:S(2)}) collective-permute-start(bf16[16,128,384]{2,1,0:T(8,128)(2,1)} %pad_maximum_fusion.refs_5_), channel_id=1, source_target_pairs={{0,192},{8,56},{16,208},{24,8},{32,224},{40,24},{48,240},{56,40},{... | collective-permute-start | bytes 4718600 | tf_op jit(solution)/shard_map/ppermute | solution.py:425
  22.4 38.1 %collective-permute-start.5 = (bf16[16,128,384]{2,1,0:T(8,128)(2,1)}, bf16[16,128,384]{2,1,0:T(8,128)(2,1)}, u32[]{:S(2)}, u32[]{:S(2)}) collective-permute-start(bf16[16,128,384]{2,1,0:T(8,128)(2,1)} %pad_maximum_fusion.refs_5_), channel_id=1, source_target_pairs={{0,128},{8,40},{16,144},{24,56},{32,160},{40,8},{48,176},{56,24},{... | collective-permute-start | bytes 4718600 | tf_op jit(solution)/shard_map/ppermute | solution.py:425
  23.3 38.0 %collective-permute-start.6 = (bf16[16,128,384]{2,1,0:T(8,128)(2,1)}, bf16[16,128,384]{2,1,0:T(8,128)(2,1)}, u32[]{:S(2)}, u32[]{:S(2)}) collective-permute-start(bf16[16,128,384]{2,1,0:T(8,128)(2,1)} %pad_maximum_fusion.refs_5_), channel_id=1, source_target_pairs={{0,64},{8,24},{16,80},{24,40},{32,96},{40,56},{48,112},{56,8},{64,... | collective-permute-start | bytes 4718600 | tf_op jit(solution)/shard_map/ppermute | solution.py:425
  25.5 35.8 %collective-permute-start.7 = (bf16[16,128,384]{2,1,0:T(8,128)(2,1)}, bf16[16,128,384]{2,1,0:T(8,128)(2,1)}, u32[]{:S(2)}, u32[]{:S(2)}) collective-permute-start(bf16[16,128,384]{2,1,0:T(8,128)(2,1)} %pad_maximum_fusion.refs_5_), channel_id=1, source_target_pairs={{0,8},{8,0},{16,24},{24,16},{32,40},{40,32},{48,56},{56,48},{64,72... | collective-permute-start | bytes 4718600 | tf_op jit(solution)/shard_map/ppermute | solution.py:413
  61.9 7.7 %collective-permute-start.12 = (bf16[16,128,384]{2,1,0:T(8,128)(2,1)}, bf16[16,128,384]{2,1,0:T(8,128)(2,1)}, u32[]{:S(2)}, u32[]{:S(2)}) collective-permute-start(bf16[16,128,384]{2,1,0:T(8,128)(2,1)} %collective-permute-done.6.refs_8_), channel_id=1, source_target_pairs={{0,8},{8,0},{16,24},{24,16},{32,40},{40,32},{48,56},{56,48},{64,72... | collective-permute-start | bytes 4718600 | tf_op jit(solution)/shard_map/ppermute | solution.py:413
  62.0 14.7 %collective-permute-start.13 = (bf16[96,2048]{1,0:T(8,128)(2,1)S(1)}, bf16[96,2048]{1,0:T(8,128)(2,1)S(1)}, u32[]{:S(2)}, u32[]{:S(2)}) collective-permute-start(bf16[96,2048]{1,0:T(8,128)(2,1)S(1)} %pad_maximum_fusion.3), channel_id=1, source_target_pairs={{0,48},{8,200},{16,0},{24,216},{32,16},{40,232},{48,32},{56,248},{... | collective-permute-start | bytes 1179656 | tf_op jit(solution)/shard_map/ppermute | solution.py:425
  62.6 14.1 %collective-permute-start.14 = (bf16[96,2048]{1,0:T(8,128)(2,1)S(1)}, bf16[96,2048]{1,0:T(8,128)(2,1)S(1)}, u32[]{:S(2)}, u32[]{:S(2)}) collective-permute-start(bf16[96,2048]{1,0:T(8,128)(2,1)S(1)} %pad_maximum_fusion.3), channel_id=1, source_target_pairs={{0,32},{8,136},{16,48},{24,152},{32,0},{40,168},{48,16},{56,184},{... | collective-permute-start | bytes 1179656 | tf_op jit(solution)/shard_map/ppermute | solution.py:425
  65.1 11.5 %collective-permute-start.15 = (bf16[96,2048]{1,0:T(8,128)(2,1)S(1)}, bf16[96,2048]{1,0:T(8,128)(2,1)}, u32[]{:S(2)}, u32[]{:S(2)}) collective-permute-start(bf16[96,2048]{1,0:T(8,128)(2,1)S(1)} %pad_maximum_fusion.3), channel_id=1, source_target_pairs={{0,16},{8,72},{16,32},{24,88},{32,48},{40,104},{48,0},{56,120},{64... | collective-permute-start | bytes 1179656 | tf_op jit(solution)/shard_map/ppermute | solution.py:425
  67.4 9.2 %collective-permute-start.16 = (bf16[384,128]{0,1:T(8,128)(2,1)S(1)}, bf16[384,128]{0,1:T(8,128)(2,1)S(1)}, u32[]{:S(2)}, u32[]{:S(2)}) collective-permute-start(bf16[384,128]{0,1:T(8,128)(2,1)S(1)} %pad.4), channel_id=1, source_target_pairs={{0,1},{1,0},{2,3},{3,2},{4,5},{5,4},{6,7},{7,6},{8,9},{9,8},{10,11... | collective-permute-start | bytes 294920 | tf_op jit(solution)/shard_map/ppermute | solution.py:397
  77.9 33.0 %collective-permute-start.21 = (bf16[384,2048]{1,0:T(8,128)(2,1)S(1)}, bf16[384,2048]{1,0:T(8,128)(2,1)S(1)}, u32[]{:S(2)}, u32[]{:S(2)}) collective-permute-start(bf16[384,2048]{1,0:T(8,128)(2,1)S(1)} %pad_maximum_fusion.1.refs_3_), channel_id=1, source_target_pairs={{0,192},{8,56},{16,208},{24,8},{32,224},{40,24},{48,240},{56,40},{... | collective-permute-start | bytes 4718600 | tf_op jit(solution)/shard_map/ppermute | solution.py:425
  78.2 32.8 %collective-permute-start.22 = (bf16[384,2048]{1,0:T(8,128)(2,1)S(1)}, bf16[384,2048]{1,0:T(8,128)(2,1)S(1)}, u32[]{:S(2)}, u32[]{:S(2)}) collective-permute-start(bf16[384,2048]{1,0:T(8,128)(2,1)S(1)} %pad_maximum_fusion.1.refs_3_), channel_id=1, source_target_pairs={{0,64},{8,24},{16,80},{24,40},{32,96},{40,56},{48,112},{56,8},{64,... | collective-permute-start | bytes 4718600 | tf_op jit(solution)/shard_map/ppermute | solution.py:425
  88.5 15.2 %collective-permute-start.18 = (bf16[32,3200]{1,0:T(8,128)(2,1)S(1)}, bf16[32,3200]{1,0:T(8,128)(2,1)S(1)}, u32[]{:S(2)}, u32[]{:S(2)}) collective-permute-start(bf16[32,3200]{1,0:T(8,128)(2,1)S(1)} %get-tuple-element.72), channel_id=1, source_target_pairs={{0,4},{1,5},{2,6},{3,7},{4,0},{5,1},{6,2},{7,3},{8,12},{9,13},{10,... | collective-permute-start | bytes 614408 | tf_op jit(solution)/shard_map/ppermute | solution.py:393
  95.2 12.9 %collective-permute-start.19 = (bf16[32,3200]{1,0:T(8,128)(2,1)S(1)}, bf16[32,3200]{1,0:T(8,128)(2,1)S(1)}, u32[]{:S(2)}, u32[]{:S(2)}) collective-permute-start(bf16[32,3200]{1,0:T(8,128)(2,1)S(1)} %get-tuple-element.73), channel_id=1, source_target_pairs={{0,2},{1,3},{2,4},{3,5},{4,6},{5,7},{6,0},{7,1},{8,10},{9,11},{10,... | collective-permute-start | bytes 614408 | tf_op jit(solution)/shard_map/ppermute | solution.py:393
  96.7 14.2 %collective-permute-start.20 = (bf16[32,3200]{1,0:T(8,128)(2,1)S(1)}, bf16[32,3200]{1,0:T(8,128)(2,1)S(1)}, u32[]{:S(2)}, u32[]{:S(2)}) collective-permute-start(bf16[32,3200]{1,0:T(8,128)(2,1)S(1)} %get-tuple-element.70), channel_id=1, source_target_pairs={{0,6},{1,7},{2,0},{3,1},{4,2},{5,3},{6,4},{7,5},{8,14},{9,15},{10,... | collective-permute-start | bytes 614408 | tf_op jit(solution)/shard_map/ppermute | solution.py:393
  110.9 12.2 %collective-permute-start.25 = (bf16[384,2048]{1,0:T(8,128)(2,1)S(1)}, bf16[384,2048]{1,0:T(8,128)(2,1)S(1)}, u32[]{:S(2)}, u32[]{:S(2)}) collective-permute-start(bf16[384,2048]{1,0:T(8,128)(2,1)S(1)} %pad_maximum_fusion.1.refs_3_), channel_id=1, source_target_pairs={{0,8},{8,0},{16,24},{24,16},{32,40},{40,32},{48,56},{56,48},{64,72... | collective-permute-start | bytes 4718600 | tf_op jit(solution)/shard_map/ppermute | solution.py:413
  111.0 12.1 %collective-permute-start.26 = (bf16[384,2048]{1,0:T(8,128)(2,1)S(1)}, bf16[384,2048]{1,0:T(8,128)(2,1)S(1)}, u32[]{:S(2)}, u32[]{:S(2)}) collective-permute-start(bf16[384,2048]{1,0:T(8,128)(2,1)S(1)} %collective-permute-done.21.refs_4_), channel_id=1, source_target_pairs={{0,8},{8,0},{16,24},{24,16},{32,40},{40,32},{48,56},{56,48},{64,72... | collective-permute-start | bytes 4718600 | tf_op jit(solution)/shard_map/ppermute | solution.py:413
  112.0 7.7 %collective-permute-start.23 = (bf16[32,3200]{1,0:T(8,128)(2,1)S(1)}, bf16[32,3200]{1,0:T(8,128)(2,1)S(1)}, u32[]{:S(2)}, u32[]{:S(2)}) collective-permute-start(bf16[32,3200]{1,0:T(8,128)(2,1)S(1)} %settle.1.refs_12_), channel_id=1, source_target_pairs={{0,7},{1,0},{2,1},{3,2},{4,3},{5,4},{6,5},{7,6},{8,15},{9,8},{10,9... | collective-permute-start | bytes 614408 | tf_op jit(solution)/shard_map/ppermute | solution.py:393
  114.9 8.2 %collective-permute-start.24 = (bf16[32,3200]{1,0:T(8,128)(2,1)S(1)}, bf16[32,3200]{1,0:T(8,128)(2,1)S(1)}, u32[]{:S(2)}, u32[]{:S(2)}) collective-permute-start(bf16[32,3200]{1,0:T(8,128)(2,1)S(1)} %settle.1.refs_12_), channel_id=1, source_target_pairs={{0,1},{1,2},{2,3},{3,4},{4,5},{5,6},{6,7},{7,0},{8,9},{9,10},{10,1... | collective-permute-start | bytes 614408 | tf_op jit(solution)/shard_map/ppermute | solution.py:393
  114.9 22.0 %collective-permute-start.29 = (bf16[384,2048]{1,0:T(8,128)(2,1)S(1)}, bf16[384,2048]{1,0:T(8,128)(2,1)}, u32[]{:S(2)}, u32[]{:S(2)}) collective-permute-start(bf16[384,2048]{1,0:T(8,128)(2,1)S(1)} %pad_maximum_fusion.1.refs_3_), channel_id=1, source_target_pairs={{0,128},{8,40},{16,144},{24,56},{32,160},{40,8},{48,176},{56,24},{... | collective-permute-start | bytes 4718600 | tf_op jit(solution)/shard_map/ppermute | solution.py:425
  123.1 13.8 %collective-permute-start.30 = (bf16[384,2048]{1,0:T(8,128)(2,1)S(1)}, bf16[384,2048]{1,0:T(8,128)(2,1)S(1)}, u32[]{:S(2)}, u32[]{:S(2)}) collective-permute-start(bf16[384,2048]{1,0:T(8,128)(2,1)S(1)} %collective-permute-done.22.refs_6_), channel_id=1, source_target_pairs={{0,8},{8,0},{16,24},{24,16},{32,40},{40,32},{48,56},{56,48},{64,72... | collective-permute-start | bytes 4718600 | tf_op jit(solution)/shard_map/ppermute | solution.py:413
  123.2 13.7 %collective-permute-start.27 = (bf16[32,3200]{1,0:T(8,128)(2,1)S(1)}, bf16[32,3200]{1,0:T(8,128)(2,1)S(1)}, u32[]{:S(2)}, u32[]{:S(2)}) collective-permute-start(bf16[32,3200]{1,0:T(8,128)(2,1)S(1)} %collective-permute-done.23.refs_14_), channel_id=1, source_target_pairs={{0,7},{1,0},{2,1},{3,2},{4,3},{5,4},{6,5},{7,6},{8,15},{9,8},{10,9... | collective-permute-start | bytes 614408 | tf_op jit(solution)/shard_map/ppermute | solution.py:393
  123.6 13.3 %collective-permute-start.28 = (bf16[32,3200]{1,0:T(8,128)(2,1)S(1)}, bf16[32,3200]{1,0:T(8,128)(2,1)S(1)}, u32[]{:S(2)}, u32[]{:S(2)}) collective-permute-start(bf16[32,3200]{1,0:T(8,128)(2,1)S(1)} %collective-permute-done.24.refs_16_), channel_id=1, source_target_pairs={{0,1},{1,2},{2,3},{3,4},{4,5},{5,6},{6,7},{7,0},{8,9},{9,10},{10,1... | collective-permute-start | bytes 614408 | tf_op jit(solution)/shard_map/ppermute | solution.py:393
  136.9 14.7 %collective-permute-start.31 = (bf16[384,2048]{1,0:T(8,128)(2,1)}, bf16[384,2048]{1,0:T(8,128)(2,1)}, u32[]{:S(2)}, u32[]{:S(2)}) collective-permute-start(bf16[384,2048]{1,0:T(8,128)(2,1)} %collective-permute-done.29.refs_5_), channel_id=1, source_target_pairs={{0,8},{8,0},{16,24},{24,16},{32,40},{40,32},{48,56},{56,48},{64,72... | collective-permute-start | bytes 4718600 | tf_op jit(solution)/shard_map/ppermute | solution.py:413
  137.0 13.7 %collective-permute-start.32 = (bf16[32,3200]{1,0:T(8,128)(2,1)S(1)}, bf16[32,3200]{1,0:T(8,128)(2,1)S(1)}, u32[]{:S(2)}, u32[]{:S(2)}) collective-permute-start(bf16[32,3200]{1,0:T(8,128)(2,1)S(1)} %collective-permute-done.27.refs_18_), channel_id=1, source_target_pairs={{0,7},{1,0},{2,1},{3,2},{4,3},{5,4},{6,5},{7,6},{8,15},{9,8},{10,9... | collective-permute-start | bytes 614408 | tf_op jit(solution)/shard_map/ppermute | solution.py:393
  140.3 11.3 %collective-permute-start.33 = (bf16[32,3200]{1,0:T(8,128)(2,1)S(1)}, bf16[32,3200]{1,0:T(8,128)(2,1)S(1)}, u32[]{:S(2)}, u32[]{:S(2)}) collective-permute-start(bf16[32,3200]{1,0:T(8,128)(2,1)S(1)} %collective-permute-done.28.refs_20_), channel_id=1, source_target_pairs={{0,1},{1,2},{2,3},{3,4},{4,5},{5,6},{6,7},{7,0},{8,9},{9,10},{10,1... | collective-permute-start | bytes 614408 | tf_op jit(solution)/shard_map/ppermute | solution.py:393
  140.4 9.3 %collective-permute-start.34 = (bf16[16,3200]{1,0:T(8,128)(2,1)S(1)}, bf16[16,3200]{1,0:T(8,128)(2,1)S(1)}, u32[]{:S(2)}, u32[]{:S(2)}) collective-permute-start(bf16[16,3200]{1,0:T(8,128)(2,1)S(1)} %slice.53), channel_id=1, source_target_pairs={{0,6},{1,7},{2,0},{3,1},{4,2},{5,3},{6,4},{7,5},{8,14},{9,15},{10,... | collective-permute-start | bytes 307208 | tf_op jit(solution)/shard_map/ppermute | solution.py:393
  142.1 8.7 %collective-permute-start.35 = (bf16[16,3200]{1,0:T(8,128)(2,1)S(1)}, bf16[16,3200]{1,0:T(8,128)(2,1)S(1)}, u32[]{:S(2)}, u32[]{:S(2)}) collective-permute-start(bf16[16,3200]{1,0:T(8,128)(2,1)S(1)} %slice.54), channel_id=1, source_target_pairs={{0,2},{1,3},{2,4},{3,5},{4,6},{5,7},{6,0},{7,1},{8,10},{9,11},{10,... | collective-permute-start | bytes 307208 | tf_op jit(solution)/shard_map/ppermute | solution.py:393
  (22 other events, 398.2 us)
